TPU v7x, 512 devices: a whole 4x4x16 slice. The times are simulated.
512 devices in a mesh: seq: 32 (over z, core), head: 16 (over x, y).
Axes of the slice: x: 4, y: 4, z: 16, core: 2. Of those that a mesh axis runs over, the one named last changes fastest.
Arguments:
- queries: bfloat16 [65536, 2048], P(('seq', 'head')), may hold values from -6 to 6
- keys: bfloat16 [65536, 2048], P(('seq', 'head')), may hold values from -6 to 6
- values: bfloat16 [65536, 4096], P(('seq', 'head')), may hold values from -6 to 6
- input_pre: float32 [65536, 8], P(('seq', 'head')), may hold values from -4 to 97
- forget_pre: float32 [65536, 8], P(('seq', 'head')), may hold values from 0 to 16
Outputs:
- cell_output: bfloat16 [65536, 4096], P('seq', 'head')
All inputs are finite; a program needn't handle non-finite values.
Results may differ from a plain program's by a relative error of at most 0.0028.
Values may be sent and summed in bfloat16 or wider, within the bound.
No kernel may reach another device: no remote copies, remote signals or barrier semaphores. Data moves between devices by JAX's collectives and lax.ppermute only.
A program may use at most 64 MiB of HBM per device.

v0:
```python
import jax
import jax.numpy as jnp
from jax import lax
from jax.sharding import PartitionSpec as P

GROUP = 64


VERY_NEGATIVE = -1e30
HIGHEST = lax.Precision.HIGHEST


def from_behind(block, axis, distance):
    devices = range(lax.axis_size(axis))
    route = [(i - distance, i) for i in devices if i - distance in devices]
    return lax.ppermute(block, axis, route)


def combine(earlier, latter):
    carry_c, carry_n, carry_m, carry_f = earlier
    fresh_c, fresh_n, fresh_m, fresh_f = latter
    joined_m = jnp.maximum(carry_m + fresh_f, fresh_m)
    keep_old = jnp.exp(carry_m + fresh_f - joined_m)
    keep_new = jnp.exp(fresh_m - joined_m)
    return (
        keep_old[..., None, None] * carry_c + keep_new[..., None, None] * fresh_c,
        keep_old[..., None] * carry_n + keep_new[..., None] * fresh_n,
        joined_m,
        carry_f + fresh_f,
    )


def group_parts(piece_block):
    query_rows, key_rows, value_rows, gate_in, log_forget = piece_block
    group_width = query_rows.shape[0]
    cumulated = jnp.cumsum(log_forget, axis=0)
    overall = cumulated[-1]
    places = jnp.arange(group_width)
    causal = (places[:, None] >= places[None, :])[:, :, None]
    gap_table = jnp.where(
        causal, cumulated[:, None, :] - cumulated[None, :, :] + gate_in[None, :, :], VERY_NEGATIVE
    )
    tail_gap = overall[None, :] - cumulated + gate_in
    return (cumulated, overall, gap_table, tail_gap)


def group_summary(piece_block):
    query_rows, key_rows, value_rows, gate_in, log_forget = piece_block
    cumulated, overall, gap_table, tail_gap = group_parts(piece_block)
    tail_top = jnp.max(tail_gap, axis=0)
    scaled_keys = key_rows.astype(jnp.float32) * jnp.exp(tail_gap - tail_top[None, :])[:, :, None]
    matrix = jnp.einsum(
        "spd,spe->pde", scaled_keys, value_rows.astype(jnp.float32), precision=HIGHEST
    )
    return (matrix, jnp.sum(scaled_keys, axis=0), tail_top, overall)


def group_output(running_state, piece_block):
    query_rows, key_rows, value_rows, gate_in, log_forget = piece_block
    matrix, normal, stabilizer, unused_decay = running_state
    cumulated, overall, gap_table, tail_gap = group_parts(piece_block)
    factor = query_rows.shape[-1] ** (-0.5)
    carried = cumulated + stabilizer[None, :]
    running = jnp.maximum(carried, jnp.max(gap_table, axis=1))
    inside = jnp.exp(gap_table - running[:, None, :])
    outside = jnp.exp(carried - running)
    scores = (
        jnp.einsum("tpd,spd->tsp", query_rows, key_rows, preferred_element_type=jnp.float32)
        * factor
    )
    weighted = inside * scores
    query_wide = query_rows.astype(jnp.float32)
    numerator = jnp.einsum(
        "tsp,spe->tpe", weighted, value_rows.astype(jnp.float32), precision=HIGHEST
    )
    numerator = (
        numerator
        + outside[:, :, None]
        * jnp.einsum("tpd,pde->tpe", query_wide, matrix, precision=HIGHEST)
        * factor
    )
    denominator = (
        jnp.sum(weighted, axis=1)
        + outside * jnp.einsum("tpd,pd->tp", query_wide, normal, precision=HIGHEST) * factor
    )
    return (numerator / jnp.maximum(jnp.abs(denominator), 1.0)[:, :, None]).astype(jnp.bfloat16)


def on_device(queries, keys, values, input_pre, forget_pre):
    tok_rows = queries.shape[0]
    head_count = input_pre.shape[1]
    query_dup = jnp.repeat(queries.reshape(tok_rows, head_count, -1), 2, axis=1)
    key_dup = jnp.repeat(keys.reshape(tok_rows, head_count, -1), 2, axis=1)
    value_split = values.reshape(tok_rows, 2 * head_count, -1)
    gate_dup = jnp.repeat(input_pre, 2, axis=1)
    forget_dup = jnp.repeat(forget_pre, 2, axis=1)
    query_all, key_all, value_all = (
        lax.all_to_all(query_dup, "head", split_axis=1, concat_axis=0, tiled=True),
        lax.all_to_all(key_dup, "head", split_axis=1, concat_axis=0, tiled=True),
        lax.all_to_all(value_split, "head", split_axis=1, concat_axis=0, tiled=True),
    )
    gate_all, forget_all = (
        lax.all_to_all(gate_dup, "head", split_axis=1, concat_axis=0, tiled=True),
        lax.all_to_all(forget_dup, "head", split_axis=1, concat_axis=0, tiled=True),
    )
    seq_rows, piece_count = gate_all.shape
    key_width = query_all.shape[2]
    value_width = value_all.shape[2]
    group_count = seq_rows // GROUP
    blocks = (
        query_all.reshape(group_count, GROUP, piece_count, key_width),
        key_all.reshape(group_count, GROUP, piece_count, key_width),
        value_all.reshape(group_count, GROUP, piece_count, value_width),
        gate_all.reshape(group_count, GROUP, piece_count),
        jax.nn.log_sigmoid(forget_all).reshape(group_count, GROUP, piece_count),
    )
    identity = (
        jnp.zeros((piece_count, key_width, value_width), jnp.float32),
        jnp.zeros((piece_count, key_width), jnp.float32),
        jnp.full((piece_count,), VERY_NEGATIVE, jnp.float32),
        jnp.zeros((piece_count,), jnp.float32),
    )

    def absorb(running_state, piece_block):
        return (combine(running_state, group_summary(piece_block)), None)

    own_state, unused_rest = lax.scan(absorb, identity, blocks)
    at_start = lax.axis_index("seq") == 0

    def relay(counter, incoming_state):
        outgoing = combine(incoming_state, own_state)
        received = from_behind((outgoing[0], outgoing[1], outgoing[2], outgoing[3]), "seq", 1)
        return tuple(
            (
                jnp.where(at_start, start_value, got_value)
                for start_value, got_value in zip(identity, received)
            )
        )

    incoming = lax.fori_loop(0, lax.axis_size("seq") - 1, relay, identity)

    def emit(running_state, piece_block):
        return (
            combine(running_state, group_summary(piece_block)),
            group_output(running_state, piece_block),
        )

    unused_final, outputs = lax.scan(emit, incoming, blocks)
    return outputs.reshape(seq_rows, piece_count * value_width)


def solution(mesh):
    in_specs = (
        P(("seq", "head"), None),
        P(("seq", "head"), None),
        P(("seq", "head"), None),
        P(("seq", "head"), None),
        P(("seq", "head"), None),
    )
    out_specs = P("seq", "head")
    return jax.shard_map(
        on_device, mesh=mesh, in_specs=in_specs, out_specs=out_specs, check_vma=False
    )
```

profile of v0, /device:TPU:1, one launch (start us, length us, event | category | flops | bytes accessed | tf_op | source)
XLA Modules:
  0.0 981.3 jit_solution(14466574366888900995)
XLA Ops:
  0.7 13.9 %all_to_all.74 = f32[128,16,1]{0,2,1:T(1,128)S(1)} all-to-all(f32[128,16,1]{0,2,1:T(1,128)S(1)} %bitcast.278), channel_id=1, replica_groups=mesh['seq'=32,'head'=16] {'head'}, dimensions={1} | all-to-all | bytes 16384 | tf_op jit(solution)/shard_map/all_to_all | solution.py:104
  29.0 12.1 %all-to-all-done.3 = bf16[128,16,256]{0,2,1:T(8,128)(2,1)S(1)} async-done(((bf16[128,16,256]{0,2,1:T(8,128)(2,1)}), bf16[128,16,256]{0,2,1:T(8,128)(2,1)S(1)}, u32[]{:S(2)}, u32[]{:S(2)}) %all-to-all-start.3) | async-done | bytes 1048608 | tf_op jit(solution)/shard_map/all_to_all | solution.py:100
  49.0 9.2 all-to-all-done.2
  59.2 4.3 all-to-all-start.4
  63.6 205.1 %while.49 = (s32[]{:T(128)}, f32[1,256,256]{2,1,0:T(8,128)S(1)}, f32[1,256]{1,0:T(1,128)S(1)}, f32[1]{0:T(128)}, f32[1]{0:T(128)}, /*index=5*/f32[32,64,1]{1,2,0...) while((s32[]{:T(128)}, f32[1,256,256]{2,1,0:T(8,128)S(1)}, ...), condition=%wide.region_4.5_spmd.clone, body=%wide.region_0.4_spmd.clone.sunk | while | flops 50664452 | bytes 929540 | solution.py:127
  268.7 355.0 %while.50 = (s32[]{:T(128)}, f32[1,256,256]{2,1,0:T(8,128)S(1)}, f32[1,256]{1,0:T(1,128)S(1)}, f32[1]{0:T(128)}, pred[]{:T(512)}, /*index=5*/f32[1]{0:T(128)}, f...) while((s32[]{:T(128)}, f32[1,256,256]{2,1,0:T(8,128)S(1)}, ...), condition=%wide.region_6.7_spmd.clone, body=%wide.region_5.6_spmd.clone.sunk | while | flops 328968 | bytes 2368871 | solution.py:140
  268.9 12.6 %collective-permute-start = (f32[1,256,256]{2,1,0:T(8,128)S(1)}, f32[1,256,256]{2,1,0:T(8,128)S(1)}, u32[]{:S(2)}, u32[]{:S(2)}) collective-permute-start(f32[1,256,256]{2,1,0:T(8,128)S(1)} %fusion.118), channel_id=1, source_target_pairs={{0,16},{16,32},{32,48},{48,64},{64,80},{80,96},{96,112},{112,128},... | collective-permute-start | bytes 786440 | tf_op jit(solution)/shard_map/while/body/eval_jaxpr/ppermute | solution.py:16
  283.4 4.6 collective-permute-start.2
  289.0 4.1 collective-permute-start
  295.0 4.6 collective-permute-start.2
  300.6 4.1 collective-permute-start
  307.7 4.8 collective-permute-start.2
  320.5 4.8 collective-permute-start.2
  326.2 4.1 collective-permute-start
  332.3 4.6 collective-permute-start.2
  337.9 4.1 collective-permute-start
  343.9 4.6 collective-permute-start.2
  349.5 4.1 collective-permute-start
  356.6 4.8 collective-permute-start.2
  368.5 4.8 collective-permute-start.2
  374.2 4.1 collective-permute-start
  385.0 4.1 collective-permute-start
  395.9 4.1 collective-permute-start
  406.7 4.1 collective-permute-start
  412.8 4.6 collective-permute-start.2
  450.8 4.1 collective-permute-start
  461.6 4.1 collective-permute-start
  472.4 4.1 collective-permute-start
  483.2 4.1 collective-permute-start
  494.0 4.1 collective-permute-start
  504.8 4.1 collective-permute-start
  623.7 357.6 %while.48 = (s32[]{:T(128)}, f32[1,256,256]{2,1,0:T(8,128)S(1)}, f32[1,256]{1,0:T(1,128)S(1)}, f32[1]{0:T(128)}, bf16[32,64,1,256]{3,1,2,0:T(8,128)(2,1)}, /*ind...) while((s32[]{:T(128)}, f32[1,256,256]{2,1,0:T(8,128)S(1)}, ...), condition=%wide.region_13.14_spmd, body=%wide.region_7.13_spmd.sunk | while | flops 115958976 | bytes 1267201 | solution.py:148
  (1271 shorter events, 658.7 us)
Async XLA Ops:
  25.1 15.9 %all-to-all-start.3 = ((bf16[128,16,256]{0,2,1:T(8,128)(2,1)}), bf16[128,16,256]{0,2,1:T(8,128)(2,1)S(1)}, u32[]{:S(2)}, u32[]{:S(2)}) async-start(bf16[128,16,256]{0,2,1:T(8,128)(2,1)} %bitcast.39), calls=%async_computation.3 | async-start | bytes 2097152 | tf_op jit(solution)/shard_map/all_to_all | solution.py:100
  42.2 15.9 %all-to-all-start.2 = ((bf16[128,16,256]{2,0,1:T(8,128)(2,1)}), bf16[128,16,256]{2,0,1:T(8,128)(2,1)S(1)}, u32[]{:S(2)}, u32[]{:S(2)}) async-start(bf16[128,16,256]{2,0,1:T(8,128)(2,1)} %bitcast.35), calls=%async_computation.2 | async-start | bytes 2097152 | tf_op jit(solution)/shard_map/all_to_all | solution.py:99
  59.2 209.5 %all-to-all-start.4 = ((bf16[128,16,256]{2,0,1:T(8,128)(2,1)}), bf16[128,16,256]{2,0,1:T(8,128)(2,1)}, u32[]{:S(2)}, u32[]{:S(2)}) async-start(bf16[128,16,256]{2,0,1:T(8,128)(2,1)} %bitcast.50), calls=%async_computation.4 | async-start | bytes 2097152 | tf_op jit(solution)/shard_map/all_to_all | solution.py:98
  268.9 19.9 %collective-permute-start = (f32[1,256,256]{2,1,0:T(8,128)S(1)}, f32[1,256,256]{2,1,0:T(8,128)S(1)}, u32[]{:S(2)}, u32[]{:S(2)}) collective-permute-start(f32[1,256,256]{2,1,0:T(8,128)S(1)} %fusion.118), channel_id=1, source_target_pairs={{0,16},{16,32},{32,48},{48,64},{64,80},{80,96},{96,112},{112,128},... | collective-permute-start | bytes 786440 | tf_op jit(solution)/shard_map/while/body/eval_jaxpr/ppermute | solution.py:16
  289.0 11.4 %collective-permute-start = (f32[1,256,256]{2,1,0:T(8,128)S(1)}, f32[1,256,256]{2,1,0:T(8,128)S(1)}, u32[]{:S(2)}, u32[]{:S(2)}) collective-permute-start(f32[1,256,256]{2,1,0:T(8,128)S(1)} %fusion.118), channel_id=1, source_target_pairs={{0,16},{16,32},{32,48},{48,64},{64,80},{80,96},{96,112},{112,128},... | collective-permute-start | bytes 786440 | tf_op jit(solution)/shard_map/while/body/eval_jaxpr/ppermute | solution.py:16
  300.6 12.6 %collective-permute-start = (f32[1,256,256]{2,1,0:T(8,128)S(1)}, f32[1,256,256]{2,1,0:T(8,128)S(1)}, u32[]{:S(2)}, u32[]{:S(2)}) collective-permute-start(f32[1,256,256]{2,1,0:T(8,128)S(1)} %fusion.118), channel_id=1, source_target_pairs={{0,16},{16,32},{32,48},{48,64},{64,80},{80,96},{96,112},{112,128},... | collective-permute-start | bytes 786440 | tf_op jit(solution)/shard_map/while/body/eval_jaxpr/ppermute | solution.py:16
  313.4 12.6 %collective-permute-start = (f32[1,256,256]{2,1,0:T(8,128)S(1)}, f32[1,256,256]{2,1,0:T(8,128)S(1)}, u32[]{:S(2)}, u32[]{:S(2)}) collective-permute-start(f32[1,256,256]{2,1,0:T(8,128)S(1)} %fusion.118), channel_id=1, source_target_pairs={{0,16},{16,32},{32,48},{48,64},{64,80},{80,96},{96,112},{112,128},... | collective-permute-start | bytes 786440 | tf_op jit(solution)/shard_map/while/body/eval_jaxpr/ppermute | solution.py:16
  326.2 11.4 %collective-permute-start = (f32[1,256,256]{2,1,0:T(8,128)S(1)}, f32[1,256,256]{2,1,0:T(8,128)S(1)}, u32[]{:S(2)}, u32[]{:S(2)}) collective-permute-start(f32[1,256,256]{2,1,0:T(8,128)S(1)} %fusion.118), channel_id=1, source_target_pairs={{0,16},{16,32},{32,48},{48,64},{64,80},{80,96},{96,112},{112,128},... | collective-permute-start | bytes 786440 | tf_op jit(solution)/shard_map/while/body/eval_jaxpr/ppermute | solution.py:16
  337.9 11.4 %collective-permute-start = (f32[1,256,256]{2,1,0:T(8,128)S(1)}, f32[1,256,256]{2,1,0:T(8,128)S(1)}, u32[]{:S(2)}, u32[]{:S(2)}) collective-permute-start(f32[1,256,256]{2,1,0:T(8,128)S(1)} %fusion.118), channel_id=1, source_target_pairs={{0,16},{16,32},{32,48},{48,64},{64,80},{80,96},{96,112},{112,128},... | collective-permute-start | bytes 786440 | tf_op jit(solution)/shard_map/while/body/eval_jaxpr/ppermute | solution.py:16
  349.5 12.6 %collective-permute-start = (f32[1,256,256]{2,1,0:T(8,128)S(1)}, f32[1,256,256]{2,1,0:T(8,128)S(1)}, u32[]{:S(2)}, u32[]{:S(2)}) collective-permute-start(f32[1,256,256]{2,1,0:T(8,128)S(1)} %fusion.118), channel_id=1, source_target_pairs={{0,16},{16,32},{32,48},{48,64},{64,80},{80,96},{96,112},{112,128},... | collective-permute-start | bytes 786440 | tf_op jit(solution)/shard_map/while/body/eval_jaxpr/ppermute | solution.py:16
  362.3 11.7 %collective-permute-start = (f32[1,256,256]{2,1,0:T(8,128)S(1)}, f32[1,256,256]{2,1,0:T(8,128)S(1)}, u32[]{:S(2)}, u32[]{:S(2)}) collective-permute-start(f32[1,256,256]{2,1,0:T(8,128)S(1)} %fusion.118), channel_id=1, source_target_pairs={{0,16},{16,32},{32,48},{48,64},{64,80},{80,96},{96,112},{112,128},... | collective-permute-start | bytes 786440 | tf_op jit(solution)/shard_map/while/body/eval_jaxpr/ppermute | solution.py:16
  374.2 10.6 %collective-permute-start = (f32[1,256,256]{2,1,0:T(8,128)S(1)}, f32[1,256,256]{2,1,0:T(8,128)S(1)}, u32[]{:S(2)}, u32[]{:S(2)}) collective-permute-start(f32[1,256,256]{2,1,0:T(8,128)S(1)} %fusion.118), channel_id=1, source_target_pairs={{0,16},{16,32},{32,48},{48,64},{64,80},{80,96},{96,112},{112,128},... | collective-permute-start | bytes 786440 | tf_op jit(solution)/shard_map/while/body/eval_jaxpr/ppermute | solution.py:16
  385.0 10.6 %collective-permute-start = (f32[1,256,256]{2,1,0:T(8,128)S(1)}, f32[1,256,256]{2,1,0:T(8,128)S(1)}, u32[]{:S(2)}, u32[]{:S(2)}) collective-permute-start(f32[1,256,256]{2,1,0:T(8,128)S(1)} %fusion.118), channel_id=1, source_target_pairs={{0,16},{16,32},{32,48},{48,64},{64,80},{80,96},{96,112},{112,128},... | collective-permute-start | bytes 786440 | tf_op jit(solution)/shard_map/while/body/eval_jaxpr/ppermute | solution.py:16
  395.9 10.6 %collective-permute-start = (f32[1,256,256]{2,1,0:T(8,128)S(1)}, f32[1,256,256]{2,1,0:T(8,128)S(1)}, u32[]{:S(2)}, u32[]{:S(2)}) collective-permute-start(f32[1,256,256]{2,1,0:T(8,128)S(1)} %fusion.118), channel_id=1, source_target_pairs={{0,16},{16,32},{32,48},{48,64},{64,80},{80,96},{96,112},{112,128},... | collective-permute-start | bytes 786440 | tf_op jit(solution)/shard_map/while/body/eval_jaxpr/ppermute | solution.py:16
  406.7 11.4 %collective-permute-start = (f32[1,256,256]{2,1,0:T(8,128)S(1)}, f32[1,256,256]{2,1,0:T(8,128)S(1)}, u32[]{:S(2)}, u32[]{:S(2)}) collective-permute-start(f32[1,256,256]{2,1,0:T(8,128)S(1)} %fusion.118), channel_id=1, source_target_pairs={{0,16},{16,32},{32,48},{48,64},{64,80},{80,96},{96,112},{112,128},... | collective-permute-start | bytes 786440 | tf_op jit(solution)/shard_map/while/body/eval_jaxpr/ppermute | solution.py:16
  418.3 10.6 %collective-permute-start = (f32[1,256,256]{2,1,0:T(8,128)S(1)}, f32[1,256,256]{2,1,0:T(8,128)S(1)}, u32[]{:S(2)}, u32[]{:S(2)}) collective-permute-start(f32[1,256,256]{2,1,0:T(8,128)S(1)} %fusion.118), channel_id=1, source_target_pairs={{0,16},{16,32},{32,48},{48,64},{64,80},{80,96},{96,112},{112,128},... | collective-permute-start | bytes 786440 | tf_op jit(solution)/shard_map/while/body/eval_jaxpr/ppermute | solution.py:16
  429.1 10.6 %collective-permute-start = (f32[1,256,256]{2,1,0:T(8,128)S(1)}, f32[1,256,256]{2,1,0:T(8,128)S(1)}, u32[]{:S(2)}, u32[]{:S(2)}) collective-permute-start(f32[1,256,256]{2,1,0:T(8,128)S(1)} %fusion.118), channel_id=1, source_target_pairs={{0,16},{16,32},{32,48},{48,64},{64,80},{80,96},{96,112},{112,128},... | collective-permute-start | bytes 786440 | tf_op jit(solution)/shard_map/while/body/eval_jaxpr/ppermute | solution.py:16
  439.9 10.6 %collective-permute-start = (f32[1,256,256]{2,1,0:T(8,128)S(1)}, f32[1,256,256]{2,1,0:T(8,128)S(1)}, u32[]{:S(2)}, u32[]{:S(2)}) collective-permute-start(f32[1,256,256]{2,1,0:T(8,128)S(1)} %fusion.118), channel_id=1, source_target_pairs={{0,16},{16,32},{32,48},{48,64},{64,80},{80,96},{96,112},{112,128},... | collective-permute-start | bytes 786440 | tf_op jit(solution)/shard_map/while/body/eval_jaxpr/ppermute | solution.py:16
  450.8 10.6 %collective-permute-start = (f32[1,256,256]{2,1,0:T(8,128)S(1)}, f32[1,256,256]{2,1,0:T(8,128)S(1)}, u32[]{:S(2)}, u32[]{:S(2)}) collective-permute-start(f32[1,256,256]{2,1,0:T(8,128)S(1)} %fusion.118), channel_id=1, source_target_pairs={{0,16},{16,32},{32,48},{48,64},{64,80},{80,96},{96,112},{112,128},... | collective-permute-start | bytes 786440 | tf_op jit(solution)/shard_map/while/body/eval_jaxpr/ppermute | solution.py:16
  461.6 10.6 %collective-permute-start = (f32[1,256,256]{2,1,0:T(8,128)S(1)}, f32[1,256,256]{2,1,0:T(8,128)S(1)}, u32[]{:S(2)}, u32[]{:S(2)}) collective-permute-start(f32[1,256,256]{2,1,0:T(8,128)S(1)} %fusion.118), channel_id=1, source_target_pairs={{0,16},{16,32},{32,48},{48,64},{64,80},{80,96},{96,112},{112,128},... | collective-permute-start | bytes 786440 | tf_op jit(solution)/shard_map/while/body/eval_jaxpr/ppermute | solution.py:16
  472.4 10.6 %collective-permute-start = (f32[1,256,256]{2,1,0:T(8,128)S(1)}, f32[1,256,256]{2,1,0:T(8,128)S(1)}, u32[]{:S(2)}, u32[]{:S(2)}) collective-permute-start(f32[1,256,256]{2,1,0:T(8,128)S(1)} %fusion.118), channel_id=1, source_target_pairs={{0,16},{16,32},{32,48},{48,64},{64,80},{80,96},{96,112},{112,128},... | collective-permute-start | bytes 786440 | tf_op jit(solution)/shard_map/while/body/eval_jaxpr/ppermute | solution.py:16
  483.2 10.6 %collective-permute-start = (f32[1,256,256]{2,1,0:T(8,128)S(1)}, f32[1,256,256]{2,1,0:T(8,128)S(1)}, u32[]{:S(2)}, u32[]{:S(2)}) collective-permute-start(f32[1,256,256]{2,1,0:T(8,128)S(1)} %fusion.118), channel_id=1, source_target_pairs={{0,16},{16,32},{32,48},{48,64},{64,80},{80,96},{96,112},{112,128},... | collective-permute-start | bytes 786440 | tf_op jit(solution)/shard_map/while/body/eval_jaxpr/ppermute | solution.py:16
  494.0 10.6 %collective-permute-start = (f32[1,256,256]{2,1,0:T(8,128)S(1)}, f32[1,256,256]{2,1,0:T(8,128)S(1)}, u32[]{:S(2)}, u32[]{:S(2)}) collective-permute-start(f32[1,256,256]{2,1,0:T(8,128)S(1)} %fusion.118), channel_id=1, source_target_pairs={{0,16},{16,32},{32,48},{48,64},{64,80},{80,96},{96,112},{112,128},... | collective-permute-start | bytes 786440 | tf_op jit(solution)/shard_map/while/body/eval_jaxpr/ppermute | solution.py:16
  504.8 10.6 %collective-permute-start = (f32[1,256,256]{2,1,0:T(8,128)S(1)}, f32[1,256,256]{2,1,0:T(8,128)S(1)}, u32[]{:S(2)}, u32[]{:S(2)}) collective-permute-start(f32[1,256,256]{2,1,0:T(8,128)S(1)} %fusion.118), channel_id=1, source_target_pairs={{0,16},{16,32},{32,48},{48,64},{64,80},{80,96},{96,112},{112,128},... | collective-permute-start | bytes 786440 | tf_op jit(solution)/shard_map/while/body/eval_jaxpr/ppermute | solution.py:16
  515.7 10.6 %collective-permute-start = (f32[1,256,256]{2,1,0:T(8,128)S(1)}, f32[1,256,256]{2,1,0:T(8,128)S(1)}, u32[]{:S(2)}, u32[]{:S(2)}) collective-permute-start(f32[1,256,256]{2,1,0:T(8,128)S(1)} %fusion.118), channel_id=1, source_target_pairs={{0,16},{16,32},{32,48},{48,64},{64,80},{80,96},{96,112},{112,128},... | collective-permute-start | bytes 786440 | tf_op jit(solution)/shard_map/while/body/eval_jaxpr/ppermute | solution.py:16
  526.5 10.6 %collective-permute-start = (f32[1,256,256]{2,1,0:T(8,128)S(1)}, f32[1,256,256]{2,1,0:T(8,128)S(1)}, u32[]{:S(2)}, u32[]{:S(2)}) collective-permute-start(f32[1,256,256]{2,1,0:T(8,128)S(1)} %fusion.118), channel_id=1, source_target_pairs={{0,16},{16,32},{32,48},{48,64},{64,80},{80,96},{96,112},{112,128},... | collective-permute-start | bytes 786440 | tf_op jit(solution)/shard_map/while/body/eval_jaxpr/ppermute | solution.py:16
  537.3 10.6 %collective-permute-start = (f32[1,256,256]{2,1,0:T(8,128)S(1)}, f32[1,256,256]{2,1,0:T(8,128)S(1)}, u32[]{:S(2)}, u32[]{:S(2)}) collective-permute-start(f32[1,256,256]{2,1,0:T(8,128)S(1)} %fusion.118), channel_id=1, source_target_pairs={{0,16},{16,32},{32,48},{48,64},{64,80},{80,96},{96,112},{112,128},... | collective-permute-start | bytes 786440 | tf_op jit(solution)/shard_map/while/body/eval_jaxpr/ppermute | solution.py:16
  548.1 10.6 %collective-permute-start = (f32[1,256,256]{2,1,0:T(8,128)S(1)}, f32[1,256,256]{2,1,0:T(8,128)S(1)}, u32[]{:S(2)}, u32[]{:S(2)}) collective-permute-start(f32[1,256,256]{2,1,0:T(8,128)S(1)} %fusion.118), channel_id=1, source_target_pairs={{0,16},{16,32},{32,48},{48,64},{64,80},{80,96},{96,112},{112,128},... | collective-permute-start | bytes 786440 | tf_op jit(solution)/shard_map/while/body/eval_jaxpr/ppermute | solution.py:16
  558.9 10.6 %collective-permute-start = (f32[1,256,256]{2,1,0:T(8,128)S(1)}, f32[1,256,256]{2,1,0:T(8,128)S(1)}, u32[]{:S(2)}, u32[]{:S(2)}) collective-permute-start(f32[1,256,256]{2,1,0:T(8,128)S(1)} %fusion.118), channel_id=1, source_target_pairs={{0,16},{16,32},{32,48},{48,64},{64,80},{80,96},{96,112},{112,128},... | collective-permute-start | bytes 786440 | tf_op jit(solution)/shard_map/while/body/eval_jaxpr/ppermute | solution.py:16
  569.8 10.6 %collective-permute-start = (f32[1,256,256]{2,1,0:T(8,128)S(1)}, f32[1,256,256]{2,1,0:T(8,128)S(1)}, u32[]{:S(2)}, u32[]{:S(2)}) collective-permute-start(f32[1,256,256]{2,1,0:T(8,128)S(1)} %fusion.118), channel_id=1, source_target_pairs={{0,16},{16,32},{32,48},{48,64},{64,80},{80,96},{96,112},{112,128},... | collective-permute-start | bytes 786440 | tf_op jit(solution)/shard_map/while/body/eval_jaxpr/ppermute | solution.py:16
  580.6 10.6 %collective-permute-start = (f32[1,256,256]{2,1,0:T(8,128)S(1)}, f32[1,256,256]{2,1,0:T(8,128)S(1)}, u32[]{:S(2)}, u32[]{:S(2)}) collective-permute-start(f32[1,256,256]{2,1,0:T(8,128)S(1)} %fusion.118), channel_id=1, source_target_pairs={{0,16},{16,32},{32,48},{48,64},{64,80},{80,96},{96,112},{112,128},... | collective-permute-start | bytes 786440 | tf_op jit(solution)/shard_map/while/body/eval_jaxpr/ppermute | solution.py:16
  591.4 10.6 %collective-permute-start = (f32[1,256,256]{2,1,0:T(8,128)S(1)}, f32[1,256,256]{2,1,0:T(8,128)S(1)}, u32[]{:S(2)}, u32[]{:S(2)}) collective-permute-start(f32[1,256,256]{2,1,0:T(8,128)S(1)} %fusion.118), channel_id=1, source_target_pairs={{0,16},{16,32},{32,48},{48,64},{64,80},{80,96},{96,112},{112,128},... | collective-permute-start | bytes 786440 | tf_op jit(solution)/shard_map/while/body/eval_jaxpr/ppermute | solution.py:16
  (67 other events, 387.0 us)
where the time goes:
time: 1000 us; the launch traced here: 981 us
  starting transfers between devices  342 us (34%)
  matrix products  218 us (22%)
  loops' own time  166 us (17%)
  other arithmetic  162 us (16%)
  local copies, waits for them, and re-layouts  54.4 us (5%)
  waiting for transfers between devices  25.6 us (3%)
  blocking collectives  13.9 us (1%)
    ppermute x93, starting transfers between devices, from_behind(): return lax.ppermute(block, axis, route)  326 us
    dot_general x64, matrix products, group_summary(): jnp.einsum('spd,spe->pde', scaled_keys, value_rows.astype(jnp.float32), p...  76.9 us
    another operation x1, loops' own time, on_device(): own_state, unused_rest = lax.scan(absorb, identity, blocks)  76.7 us
    another operation x1, loops' own time, on_device(): unused_final, outputs = lax.scan(emit, incoming, blocks)  62.9 us
    exp x64, other arithmetic, group_summary(): jnp.exp(tail_gap - tail_top[None, :])[:, :, None]  57.7 us
    dot_general x32, matrix products, group_output(): jnp.einsum('tsp,spe->tpe', weighted, value_rows.astype(jnp.float32), prec...  51.7 us
    another operation x96, other arithmetic, group_parts(): cumulated = jnp.cumsum(log_forget, axis=0)  46.2 us
    sub x32, other arithmetic, group_parts(): tail_gap = overall[None, :] - cumulated + gate_in  37.3 us
  transfers between devices with their start and end apart: 97, of which 3 were waited for; matrix products, arithmetic and copies ran while one was open for 14% of the time, Pallas kernels for 0%

commit v1 on v0

v1 whole, which is shorter than its diff:
```python
import jax
import jax.numpy as jnp
from jax import lax
from jax.experimental import pallas as pl
from jax.experimental.pallas import tpu as pltpu
from jax.sharding import PartitionSpec as P

VERY_NEGATIVE = -1e30
CHUNK = 256
EXTRA = 128
GATE_ROWS = 8
F32 = jnp.float32
BF16 = jnp.bfloat16
F16 = jnp.float16


def dot(a, b, contract):
    return lax.dot_general(a, b, ((contract[:1], contract[1:]), ((), ())), preferred_element_type=F32)


def halves(x):
    top = x.astype(BF16)
    return top, (x - top.astype(F32)).astype(BF16)


def thirds(x, scale):
    first = x.astype(BF16).astype(F32)
    rest = (x - first) * scale
    second = rest.astype(BF16).astype(F32)
    third = ((rest - second) * scale).astype(BF16).astype(F32)
    return first, second, third


def iota(shape, dim):
    return lax.broadcasted_iota(jnp.int32, shape, dim)


def pack_kernel(k_ref, v_ref, gate_ref, forget_ref, out_ref, parts_ref):
    head = pl.program_id(0)
    rows, width = k_ref.shape

    @pl.when(head == 0)
    def _():
        decay = -jnp.log1p(jnp.exp(-forget_ref[...]))
        for n, x in enumerate((decay.T, gate_ref[...].T)):
            for p, part in enumerate(thirds(x, 1.0)):
                parts_ref[3 * n + p] = part

    row = iota((GATE_ROWS, rows), 0)
    block = []
    for n in range(2):
        area = jnp.zeros((GATE_ROWS, rows), F32)
        for p in range(3):
            area = jnp.where(row == p, parts_ref[3 * n + p, pl.ds(head, 1), :], area)
        block.append(area)
    gates = jnp.concatenate(block, axis=1).astype(BF16)
    for u in range(2):
        out_ref[u, 0:rows, 0:width] = k_ref[...]
        out_ref[u, 0:rows, width : 2 * width] = v_ref[:, u * width : (u + 1) * width]
        out_ref[u, rows : rows + GATE_ROWS, :] = jnp.zeros((GATE_ROWS, 2 * width), BF16)
        out_ref[u, rows : rows + GATE_ROWS, 0 : 2 * rows] = gates


def twice_kernel(q_ref, out_ref):
    for u in range(2):
        out_ref[u] = q_ref[...]


def state_kernel(r_ref, entry_top_ref, entry_low_ref, aux_ref, z_ref, c_ref, n_ref, m_ref, f_ref):
    step = pl.program_id(0)
    sources, rows = r_ref.shape[0], r_ref.shape[1] - GATE_ROWS
    width = c_ref.shape[0]

    @pl.when(step == 0)
    def _():
        c_ref[...] = jnp.zeros_like(c_ref)
        n_ref[...] = jnp.zeros_like(n_ref)
        m_ref[...] = jnp.full_like(m_ref, VERY_NEGATIVE)
        f_ref[...] = jnp.zeros_like(f_ref)

    entry_top, entry_low = halves(c_ref[...])
    entry_top_ref[0] = entry_top
    entry_low_ref[0] = entry_low

    gates = [r_ref[b, rows : rows + GATE_ROWS, 0 : 2 * rows] for b in range(sources)]
    decay = jnp.concatenate([g[:, 0:rows] for g in gates], axis=1)
    gate = jnp.concatenate([g[:, rows:] for g in gates], axis=1).astype(F32)
    gate = gate[0:1] + gate[1:2] + gate[2:3]
    upper = (iota((CHUNK, CHUNK), 0) <= iota((CHUNK, CHUNK), 1)).astype(BF16)
    cum = dot(decay, upper, (1, 0))
    cum = cum[0:1] + cum[1:2] + cum[2:3]
    total = cum[:, CHUNK - 1 : CHUNK]
    tail = total - cum + gate
    old_m = m_ref[0:1, 0:1]
    new_m = jnp.maximum(old_m + total, jnp.max(tail, axis=1, keepdims=True))
    keep = jnp.exp(old_m + total - new_m)
    weight = jnp.exp(tail - new_m)

    row = iota((8, CHUNK), 0)
    aux = jnp.where(row == 0, n_ref[0:1, :], 0.0)
    for p, x in ((1, old_m), (2, f_ref[0:1, 0:1]), (3, cum), (4, gate)):
        aux = jnp.where(row == p, x, aux)
    aux_ref[0] = aux

    column = jnp.where(row == 0, weight, 0.0).T[:, 0:1]
    keys = r_ref[:, 0:rows, 0:width].reshape(CHUNK, width).astype(F32) * column
    values = r_ref[:, 0:rows, width:].reshape(CHUNK, width)
    keys_top, keys_low = halves(keys)
    c_new = keep * c_ref[...] + dot(keys_top, values, (0, 0)) + dot(keys_low, values, (0, 0))
    n_new = keep * n_ref[0:1, :] + jnp.sum(keys, axis=0, keepdims=True)
    f_new = f_ref[0:1, 0:1] + total
    c_ref[...] = c_new
    n_ref[0:1, :] = n_new
    m_ref[...] = jnp.broadcast_to(new_m, m_ref.shape)
    f_ref[...] = jnp.broadcast_to(f_new, f_ref.shape)

    @pl.when(step == pl.num_programs(0) - 1)
    def _():
        count, slab = z_ref.shape[0], z_ref.shape[1]
        most = jnp.max(jnp.max(jnp.abs(c_new), axis=1, keepdims=True), axis=0, keepdims=True)
        scaled = c_new * jnp.where(most > 0.0, 1.0 / most, 0.0)
        z_ref[:, :, 0:width] = scaled.reshape(count, slab, width)
        place = iota((slab, EXTRA), 0)
        lane = iota((slab, EXTRA), 1)
        extra = jnp.zeros((slab, EXTRA), F32)
        for p, part in enumerate(thirds(n_new, 256.0)):
            for h in range(width // EXTRA):
                extra = jnp.where(place == 2 * p + h, part[:, h * EXTRA : (h + 1) * EXTRA], extra)
        for n, x in enumerate((new_m, f_new, most * 0.25)):
            for p, part in enumerate(thirds(x, 256.0)):
                extra = jnp.where((place == 6) & (lane == 3 * n + p), part, extra)
        z_ref[:, :, width:] = jnp.broadcast_to(extra[None], (count, slab, EXTRA))


def prefix_kernel(own_ref, z_ref, y_ref, nin_ref):
    slab, count, wide = z_ref.shape
    width = wide - EXTRA
    own = own_ref[0]

    def joined(a, b, c):
        return a + (b + c * (1.0 / 256.0)) * (1.0 / 256.0)

    scalars = z_ref[6, :, width:]
    m, f, most = (joined(*(scalars[:, 3 * n + p : 3 * n + p + 1] for p in range(3))) for n in range(3))
    most = most * 4.0
    shard = iota((count, EXTRA), 0)
    later = iota((count, EXTRA), 1)
    gap = jnp.zeros((count, EXTRA), F32)
    for j in range(count):
        gap = jnp.where((shard < j) & (later > j), gap + f[j : j + 1, :], gap)
    before = shard < later
    reach = jnp.where(before, m + gap, VERY_NEGATIVE)
    top = jnp.max(reach, axis=0, keepdims=True)
    weight = jnp.where(before, jnp.exp(reach - top), 0.0)
    heavy = weight * most
    bound = jnp.sum(heavy, axis=0, keepdims=True)
    heavy = heavy * jnp.where(bound > 0.0, 1.0 / bound, 0.0)
    heavy_top, heavy_low = halves(heavy)
    both = jnp.concatenate([heavy_top, heavy_low], axis=1)
    for r in range(slab):
        x_top, x_low = halves(z_ref[r, :, 0:width])
        y = dot(both, x_top, (0, 0))
        y = y[0:count] + y[EXTRA : EXTRA + count] + dot(heavy_top, x_low, (0, 0))[0:count]
        y_ref[r] = y

    mine = iota((1, EXTRA), 1) == own
    column = jnp.sum(jnp.where(mine, weight, 0.0), axis=1, keepdims=True)
    row = iota((8, EXTRA), 0)
    own_top = jnp.sum(jnp.where(mine, top, 0.0), axis=1, keepdims=True)
    own_bound = jnp.sum(jnp.where(mine, bound, 0.0), axis=1, keepdims=True)
    for h in range(width // EXTRA):
        n = joined(*(z_ref[2 * p + h, :, width:] for p in range(3)))
        n = jnp.sum(column * n, axis=0, keepdims=True)
        area = jnp.where(row == 0, n, jnp.where(row == 1, own_top, own_bound))
        nin_ref[:, h * EXTRA : (h + 1) * EXTRA] = area


def inside_kernel(q_ref, r_ref, entry_top_ref, entry_low_ref, aux_ref, num_ref, col_ref):
    rows = q_ref.shape[1]
    width = q_ref.shape[2]
    factor = width**-0.5
    queries = q_ref[...].reshape(CHUNK, width)
    keys = r_ref[:, 0:rows, 0:width].reshape(CHUNK, width)
    values = r_ref[:, 0:rows, width:].reshape(CHUNK, width)
    aux = aux_ref[0]
    turned = aux.T
    cum_column = turned[:, 3:4]
    old_m = aux[1:2, 0:1]
    start = aux[2:3, 0:1]
    score = dot(queries, keys, (1, 1))
    causal = iota((CHUNK, CHUNK), 0) >= iota((CHUNK, CHUNK), 1)
    gap = jnp.where(causal, cum_column + (aux[4:5] - aux[3:4]), VERY_NEGATIVE)
    carried = cum_column + old_m
    top = jnp.maximum(carried, jnp.max(gap, axis=1, keepdims=True))
    weighted = jnp.exp(gap - top) * (score * factor)
    outside = jnp.exp(carried - top) * factor
    weighted_top, weighted_low = halves(weighted)
    num = dot(weighted_top, values, (1, 0)) + dot(weighted_low, values, (1, 0))
    num = num + outside * (
        dot(queries, entry_top_ref[0], (1, 0)) + dot(queries, entry_low_ref[0], (1, 0))
    )
    reached = jnp.sum(queries.astype(F32) * aux[0:1], axis=1, keepdims=True)
    den = jnp.sum(weighted, axis=1, keepdims=True) + outside * reached
    num_ref[...] = num
    lane = iota((CHUNK, EXTRA), 1)
    col_ref[...] = jnp.where(lane == 0, top, jnp.where(lane == 1, den, cum_column + start))


def finish_kernel(q_ref, num_ref, col_ref, c_ref, nin_ref, out_ref, top_ref, low_ref):
    width = q_ref.shape[2]
    count = q_ref.shape[0] * q_ref.shape[1]
    factor = width**-0.5

    @pl.when(pl.program_id(0) == 0)
    def _():
        top, low = halves(c_ref[...])
        top_ref[...] = top
        low_ref[...] = low

    queries = q_ref[...].reshape(count, width)
    cols = col_ref[...]
    m, den, cum = cols[:, 0:1], cols[:, 1:2], cols[:, 2:3]
    before_m = nin_ref[1:2, 0:1]
    bound = nin_ref[2:3, 0:1]
    carried = cum + before_m
    new_m = jnp.maximum(m, carried)
    inside = jnp.exp(m - new_m)
    outside = jnp.exp(carried - new_m) * factor
    reached = jnp.sum(queries.astype(F32) * nin_ref[0:1, :], axis=1, keepdims=True)
    den = den * inside + outside * reached
    over = 1.0 / jnp.maximum(jnp.abs(den), 1.0)
    read = dot(queries, top_ref[...], (1, 0)) + dot(queries, low_ref[...], (1, 0))
    out_ref[...] = (num_ref[...] * (inside * over) + read * (outside * bound * over)).astype(BF16)


def whole(shape):
    return pl.BlockSpec(shape, lambda i: (0,) * len(shape))


def stepped(shape, at=0):
    return pl.BlockSpec(shape, lambda i: tuple(i if d == at else 0 for d in range(len(shape))))


def on_device(queries, keys, values, input_pre, forget_pre):
    rows = queries.shape[0]
    heads = input_pre.shape[1]
    pieces = lax.axis_size("head")
    shards = lax.axis_size("seq")
    width = queries.shape[1] // heads
    tokens = pieces * rows
    steps = tokens // CHUNK
    group = CHUNK // rows
    tall = rows + GATE_ROWS
    slab = width // shards

    packed = pl.pallas_call(
        pack_kernel,
        grid=(heads,),
        in_specs=[
            stepped((rows, width), 1),
            stepped((rows, 2 * width), 1),
            whole((rows, heads)),
            whole((rows, heads)),
        ],
        out_specs=stepped((2, tall, 2 * width)),
        out_shape=jax.ShapeDtypeStruct((pieces, tall, 2 * width), BF16),
        scratch_shapes=[pltpu.VMEM((6, heads, rows), F32)],
        name="pack",
    )(keys, values, input_pre, forget_pre)
    doubled = pl.pallas_call(
        twice_kernel,
        grid=(heads,),
        in_specs=[stepped((rows, width), 1)],
        out_specs=stepped((2, rows, width)),
        out_shape=jax.ShapeDtypeStruct((pieces, rows, width), BF16),
        name="twice",
    )(queries)

    with jax.named_scope("kv"):
        received = lax.all_to_all(packed, "head", split_axis=0, concat_axis=0, tiled=True)
    with jax.named_scope("q"):
        asked = lax.all_to_all(doubled, "head", split_axis=0, concat_axis=0, tiled=True)

    entry_top, entry_low, aux, summary = pl.pallas_call(
        state_kernel,
        grid=(steps,),
        in_specs=[stepped((group, tall, 2 * width))],
        out_specs=[
            stepped((1, width, width)),
            stepped((1, width, width)),
            stepped((1, 8, CHUNK)),
            whole((shards, slab, width + EXTRA)),
        ],
        out_shape=[
            jax.ShapeDtypeStruct((steps, width, width), BF16),
            jax.ShapeDtypeStruct((steps, width, width), BF16),
            jax.ShapeDtypeStruct((steps, 8, CHUNK), F32),
            jax.ShapeDtypeStruct((shards, slab, width + EXTRA), F32),
        ],
        scratch_shapes=[
            pltpu.VMEM((width, width), F32),
            pltpu.VMEM((8, width), F32),
            pltpu.VMEM((8, EXTRA), F32),
            pltpu.VMEM((8, EXTRA), F32),
        ],
        name="state",
    )(received)

    with jax.named_scope("spread"):
        spread = lax.all_to_all(summary.astype(F16), "seq", split_axis=0, concat_axis=0, tiled=True)

    own = lax.axis_index("seq").astype(jnp.int32).reshape(1)
    before, normal = pl.pallas_call(
        prefix_kernel,
        in_specs=[
            pl.BlockSpec(memory_space=pltpu.SMEM),
            pl.BlockSpec(memory_space=pltpu.VMEM),
        ],
        out_specs=[pl.BlockSpec(memory_space=pltpu.VMEM), pl.BlockSpec(memory_space=pltpu.VMEM)],
        out_shape=[
            jax.ShapeDtypeStruct((slab, shards, width), F32),
            jax.ShapeDtypeStruct((8, width), F32),
        ],
        name="prefix",
    )(own, jnp.swapaxes(spread, 0, 1).astype(F32))

    with jax.named_scope("back"):
        back = lax.all_to_all(
            jnp.swapaxes(before, 0, 1).astype(F16), "seq", split_axis=0, concat_axis=0, tiled=True
        )

    num, cols = pl.pallas_call(
        inside_kernel,
        grid=(steps,),
        in_specs=[
            stepped((group, rows, width)),
            stepped((group, tall, 2 * width)),
            stepped((1, width, width)),
            stepped((1, width, width)),
            stepped((1, 8, CHUNK)),
        ],
        out_specs=[stepped((CHUNK, width)), stepped((CHUNK, EXTRA))],
        out_shape=[
            jax.ShapeDtypeStruct((tokens, width), F32),
            jax.ShapeDtypeStruct((tokens, EXTRA), F32),
        ],
        name="inside",
    )(asked, received, entry_top, entry_low, aux)

    return pl.pallas_call(
        finish_kernel,
        grid=(steps // 2,),
        in_specs=[
            stepped((2 * group, rows, width)),
            stepped((2 * CHUNK, width)),
            stepped((2 * CHUNK, EXTRA)),
            whole((width, width)),
            whole((8, width)),
        ],
        out_specs=stepped((2 * CHUNK, width)),
        out_shape=jax.ShapeDtypeStruct((tokens, width), BF16),
        scratch_shapes=[pltpu.VMEM((width, width), BF16), pltpu.VMEM((width, width), BF16)],
        name="finish",
    )(asked, num, cols, back.reshape(width, width).astype(F32), normal)


def solution(mesh):
    spec = P(("seq", "head"), None)
    return jax.shard_map(
        on_device, mesh=mesh, in_specs=(spec,) * 5, out_specs=P("seq", "head"), check_vma=False
    )
```

time: 1000 us -> 142 us (0.14); the launches traced: 981 us -> 141 us
  starting transfers between devices: 342 us -> 30.3 us
  matrix products: 218 us -> 0 us
  loops' own time: 166 us -> 0 us
  other arithmetic: 162 us -> 4.17 us
  local copies, waits for them, and re-layouts: 54.4 us -> 3.56 us
  Pallas kernels: 0 us -> 38.1 us
  blocking collectives: 13.9 us -> 33.6 us
    ppermute x93 -> x0, starting transfers between devices: 326 us -> none  [from_behind(): return lax.ppermute(block, axis, route)]
    dot_general x192 -> x0, matrix products: 218 us -> none  [the longest x64 76.9 us: group_summary(): jnp.einsum('spd,spe->pde', scaled_keys, value_rows.astype(jnp.float32), p...]
    another operation x3 -> x0, loops' own time: 166 us -> none  [the longest x1 76.7 us: on_device(): own_state, unused_rest = lax.scan(absorb, identity, blocks)]
    exp x64 -> x0, other arithmetic: 57.7 us -> none  [group_summary(): jnp.exp(tail_gap - tail_top[None, :])[:, :, None]]
    another operation x96 -> x0, other arithmetic: 46.2 us -> none  [group_parts(): cumulated = jnp.cumsum(log_forget, axis=0)]
    pallas_call x0 -> x6, Pallas kernels: none -> 38.1 us  [the longest x1 9.4 us: on_device(): pl.pallas_call(inside_kernel, grid=(steps,), in_specs=[stepped((group, ro...]
    sub x32 -> x0, other arithmetic: 37.3 us -> none  [group_parts(): tail_gap = overall[None, :] - cumulated + gate_in]
    slice x64 -> x0, local copies, waits for them, and re-layouts: 33.3 us -> none  [group_parts(): overall = cumulated[-1]]
  transfers between devices with their start and end apart: 97 -> 3, of which waited for: 3 -> 3; matrix products, arithmetic and copies ran while one was open for 14% -> 2% of each run, Pallas kernels for 0% -> 12%
where the time goes in v1:
time: 142 us; the launch traced here: 141 us
  Pallas kernels  38.1 us (27%)
  blocking collectives  33.6 us (24%)
  waiting for transfers between devices  30.9 us (22%)
  starting transfers between devices  30.3 us (21%)
  other arithmetic  4.17 us (3%)
  local copies, waits for them, and re-layouts  3.56 us (3%)
    all_to_all x1, blocking collectives, on_device(): lax.all_to_all(packed, 'head', split_axis=0, concat_axis=0, tiled=True)  33.6 us
    all_to_all x1, starting transfers between devices, on_device(): lax.all_to_all(summary.astype(F16), 'seq', split_axis=0, concat_axis=0, t...  20.1 us
    all_to_all x1, waiting for transfers between devices, on_device(): lax.all_to_all(summary.astype(F16), 'seq', split_axis=0, concat_axis=0, t...  13.9 us
    all_to_all x1, waiting for transfers between devices, on_device(): lax.all_to_all(doubled, 'head', split_axis=0, concat_axis=0, tiled=True)  10.2 us
    pallas_call x1, Pallas kernels, on_device(): pl.pallas_call(inside_kernel, grid=(steps,), in_specs=[stepped((group, ro...  9.4 us
    pallas_call x1, Pallas kernels, on_device(): pl.pallas_call(state_kernel, grid=(steps,), in_specs=[stepped((group, tal...  9.35 us
    all_to_all x1, waiting for transfers between devices, on_device(): lax.all_to_all(jnp.swapaxes(before, 0, 1).astype(F16), 'seq', split_axis=...  6.78 us
    all_to_all x1, starting transfers between devices, on_device(): lax.all_to_all(jnp.swapaxes(before, 0, 1).astype(F16), 'seq', split_axis=...  6.52 us
  transfers between devices with their start and end apart: 3, of which 3 were waited for; matrix products, arithmetic and copies ran while one was open for 2% of the time, Pallas kernels for 12%

profile of v1, /device:TPU:1, one launch (start us, length us, event | category | flops | bytes accessed | tf_op | source)
XLA Modules:
  0.0 140.7 jit_solution(10518668492138535997)
XLA Ops:
  0.0 1.4 %copy.10.gate_ref = f32[128,8]{1,0:T(8,128)} copy(f32[128,8]{0,1:T(8,128)} %param.8) | data formatting | bytes 8192 | tf_op args[3]
  1.4 1.4 copy.11.forget_ref
  2.8 5.8 %pack.1 = bf16[16,136,512]{2,1,0:T(8,128)(2,1)} custom-call(bf16[128,2048]{1,0:T(8,128)(2,1)} %k_ref.1, bf16[128,4096]{1,0:T(8,128)(2,1)} %v_ref.1, f32[128,8]{1,0:T(8,128)} %copy.10.gate_ref, f32[128,8]{1,0:T(8,128)} %copy.11.forget_ref), custom_call_target="tpu_custom_call" | custom-call | tf_op jit(solution)/shard_map/pack/pallas_call | solution.py:256
  8.6 33.6 %all_to_all.20.r_ref = bf16[16,136,512]{2,1,0:T(8,128)(2,1)} all-to-all(bf16[16,136,512]{2,1,0:T(8,128)(2,1)} %pack.1), channel_id=1, replica_groups=mesh['seq'=32,'head'=16] {'head'}, dimensions={0} | all-to-all | bytes 4456448 | tf_op jit(solution)/shard_map/kv/all_to_all | solution.py:280
  42.2 9.3 %state.1 = (bf16[8,256,256]{2,1,0:T(8,128)(2,1)}, bf16[8,256,256]{2,1,0:T(8,128)(2,1)}, f32[8,8,256]{2,1,0:T(8,128)}, f32[32,8,384]{2,1,0:T(8,128)}) custom-call(bf16[16,136,512]{2,1,0:T(8,128)(2,1)} %all_to_all.20.r_ref), custom_call_target="tpu_custom_call" | custom-call | tf_op jit(solution)/shard_map/state/pallas_call | solution.py:284
  51.5 1.7 %convert_element_type.19 = f16[32,8,384]{2,1,0:T(8,128)(2,1)} convert(f32[32,8,384]{2,1,0:T(8,128)} %get-tuple-element.18) | non-fusion elementwise | flops 98304 | bytes 589824 | tf_op jit(solution)/shard_map/spread/convert_element_type | solution.py:310
  53.2 20.1 %all-to-all-start.2 = ((f16[32,8,384]{2,1,0:T(8,128)(2,1)}), f16[32,8,384]{2,1,0:T(8,128)(2,1)S(1)}, u32[]{:S(2)}, u32[]{:S(2)}) async-start(f16[32,8,384]{2,1,0:T(8,128)(2,1)} %convert_element_type.19), calls=%async_computation.2 | async-start | bytes 393216 | tf_op jit(solution)/shard_map/spread/all_to_all | solution.py:310
  73.4 4.9 %twice.1 = bf16[16,128,256]{2,1,0:T(8,128)(2,1)} custom-call(bf16[128,2048]{1,0:T(8,128)(2,1)} %q_ref.1), custom_call_target="tpu_custom_call" | custom-call | tf_op jit(solution)/shard_map/twice/pallas_call | solution.py:270
  78.3 13.9 %all-to-all-done.2 = f16[32,8,384]{2,1,0:T(8,128)(2,1)S(1)} async-done(((f16[32,8,384]{2,1,0:T(8,128)(2,1)}), f16[32,8,384]{2,1,0:T(8,128)(2,1)S(1)}, u32[]{:S(2)}, u32[]{:S(2)}) %all-to-all-start.2) | async-done | bytes 196640 | tf_op jit(solution)/shard_map/spread/all_to_all | solution.py:310
  92.2 3.7 %all-to-all-start = ((bf16[16,128,256]{2,1,0:T(8,128)(2,1)}), bf16[16,128,256]{2,1,0:T(8,128)(2,1)S(1)}, u32[]{:S(2)}, u32[]{:S(2)}) async-start(bf16[16,128,256]{2,1,0:T(8,128)(2,1)} %twice.1), calls=%async_computation | async-start | bytes 2097152 | tf_op jit(solution)/shard_map/q/all_to_all | solution.py:282
  95.8 0.8 convert_bitcast_fusion.z_ref
  96.6 2.6 %prefix.1 = (f32[8,32,256]{2,1,0:T(8,128)}, f32[8,256]{1,0:T(8,128)}) custom-call(s32[1]{0:T(128)} %bitcast.own_ref, f32[8,32,384]{2,1,0:T(8,128)} %convert_bitcast_fusion.z_ref), custom_call_target="tpu_custom_call" | custom-call | tf_op jit(solution)/shard_map/prefix/pallas_call | solution.py:313
  99.2 1.0 convert_bitcast_fusion.1
  100.2 0.7 copy.13
  101.0 10.2 %all-to-all-done.q_ref = bf16[16,128,256]{2,1,0:T(8,128)(2,1)S(1)} async-done(((bf16[16,128,256]{2,1,0:T(8,128)(2,1)}), bf16[16,128,256]{2,1,0:T(8,128)(2,1)S(1)}, u32[]{:S(2)}, u32[]{:S(2)}) %all-to-all-start) | async-done | bytes 1048608 | tf_op jit(solution)/shard_map/q/all_to_all | solution.py:282
  111.2 0.0 copy-start
  111.2 6.5 %all-to-all-start.3 = ((f16[32,8,256]{2,1,0:T(8,128)(2,1)}), f16[32,8,256]{2,1,0:T(8,128)(2,1)S(1)}, u32[]{:S(2)}, u32[]{:S(2)}) async-start(f16[32,8,256]{2,1,0:T(8,128)(2,1)} %copy.13), calls=%async_computation.3 | async-start | bytes 262144 | tf_op jit(solution)/shard_map/back/all_to_all | solution.py:328
  117.7 0.0 copy-done
  117.7 9.4 %inside.1 = (f32[2048,256]{1,0:T(8,128)}, f32[2048,128]{1,0:T(8,128)}) custom-call(bf16[16,128,256]{2,1,0:T(8,128)(2,1)} %copy-done, bf16[16,136,512]{2,1,0:T(8,128)(2,1)} %all_to_all.20.r_ref, bf16[8,256,256]{2,1,0:T(8,128)(2,1)} %get-tuple-element.13.entry_top_ref, bf16[8,256,256]{2,1,0:T(8,128)(2,1)} %get-tuple-element.14.entry_low_ref, ...), custom_call_target="tpu_custom_call" | custom-call | tf_op jit(solution)/shard_map/inside/pallas_call | solution.py:332
  127.1 6.8 %all-to-all-done.3 = f16[32,8,256]{2,1,0:T(8,128)(2,1)S(1)} async-done(((f16[32,8,256]{2,1,0:T(8,128)(2,1)}), f16[32,8,256]{2,1,0:T(8,128)(2,1)S(1)}, u32[]{:S(2)}, u32[]{:S(2)}) %all-to-all-start.3) | async-done | bytes 131104 | tf_op jit(solution)/shard_map/back/all_to_all | solution.py:328
  133.9 0.7 bitcast_convert_fusion.c_ref
  134.6 6.1 %finish.1 = bf16[2048,256]{1,0:T(8,128)(2,1)} custom-call(bf16[16,128,256]{2,1,0:T(8,128)(2,1)} %copy-done, f32[2048,256]{1,0:T(8,128)} %get-tuple-element.16.num_ref, f32[2048,128]{1,0:T(8,128)} %get-tuple-element.17.col_ref, f32[256,256]{1,0:T(8,128)} %bitcast_convert_fusion.c_ref, f32[8,256]{1,0:T(8,128)} %get-tuple-element.20.nin_ref), custom_call_target="tpu_custom_call" | custom-call | tf_op jit(solution)/shard_map/finish/pallas_call | solution.py:350
Async XLA Ops:
  53.2 38.9 %all-to-all-start.2 = ((f16[32,8,384]{2,1,0:T(8,128)(2,1)}), f16[32,8,384]{2,1,0:T(8,128)(2,1)S(1)}, u32[]{:S(2)}, u32[]{:S(2)}) async-start(f16[32,8,384]{2,1,0:T(8,128)(2,1)} %convert_element_type.19), calls=%async_computation.2 | async-start | bytes 393216 | tf_op jit(solution)/shard_map/spread/all_to_all | solution.py:310
  92.2 19.0 %all-to-all-start = ((bf16[16,128,256]{2,1,0:T(8,128)(2,1)}), bf16[16,128,256]{2,1,0:T(8,128)(2,1)S(1)}, u32[]{:S(2)}, u32[]{:S(2)}) async-start(bf16[16,128,256]{2,1,0:T(8,128)(2,1)} %twice.1), calls=%async_computation | async-start | bytes 2097152 | tf_op jit(solution)/shard_map/q/all_to_all | solution.py:282
  111.2 6.5 %copy-start = (bf16[16,128,256]{2,1,0:T(8,128)(2,1)}, bf16[16,128,256]{2,1,0:T(8,128)(2,1)S(1)}, u32[]{:S(2)}) copy-start(bf16[16,128,256]{2,1,0:T(8,128)(2,1)S(1)} %all-to-all-done.q_ref) | copy-start | bytes 3145732
  111.2 22.7 %all-to-all-start.3 = ((f16[32,8,256]{2,1,0:T(8,128)(2,1)}), f16[32,8,256]{2,1,0:T(8,128)(2,1)S(1)}, u32[]{:S(2)}, u32[]{:S(2)}) async-start(f16[32,8,256]{2,1,0:T(8,128)(2,1)} %copy.13), calls=%async_computation.3 | async-start | bytes 262144 | tf_op jit(solution)/shard_map/back/all_to_all | solution.py:328

commit v2 on v1

v2 whole, which is shorter than its diff:
```python
import jax
import jax.numpy as jnp
from jax import lax
from jax.experimental import pallas as pl
from jax.experimental.pallas import tpu as pltpu
from jax.sharding import PartitionSpec as P

VERY_NEGATIVE = -1e30
CHUNK = 256
PIECE = 256
PACK_STEPS = 4
EXTRA = 128
GATE_ROWS = 8
F32 = jnp.float32
BF16 = jnp.bfloat16
F16 = jnp.float16


def dot(a, b, contract):
    return lax.dot_general(a, b, ((contract[:1], contract[1:]), ((), ())), preferred_element_type=F32)


def halves(x):
    top = x.astype(BF16)
    return top, (x - top.astype(F32)).astype(BF16)


def thirds(x, scale):
    first = x.astype(BF16).astype(F32)
    rest = (x - first) * scale
    second = rest.astype(BF16).astype(F32)
    third = ((rest - second) * scale).astype(BF16).astype(F32)
    return first, second, third


def iota(shape, dim):
    return lax.broadcasted_iota(jnp.int32, shape, dim)


def pack_kernel(q_ref, k_ref, v_ref, gate_ref, forget_ref, out_ref, parts_ref):
    at = pl.program_id(0)
    rows = k_ref.shape[0]
    heads = k_ref.shape[1] // PIECE

    @pl.when(at == 0)
    def _():
        decay = -jnp.log1p(jnp.exp(-forget_ref[...]))
        for n, x in enumerate((decay, gate_ref[...])):
            for p, part in enumerate(thirds(x, 1.0)):
                parts_ref[3 * n + p] = part

    row = iota((GATE_ROWS, rows), 0)
    for h in range(heads):
        area = jnp.zeros((GATE_ROWS, rows), F32)
        for p in range(6):
            area = jnp.where(row == p, parts_ref[p, pl.ds(at * heads + h, 1), :], area)
        area = area.astype(BF16)
        turned = q_ref[:, h * PIECE : (h + 1) * PIECE].T
        for u in range(2):
            n = 2 * h + u
            out_ref[n, 0:PIECE, :] = turned
            out_ref[n, PIECE : 2 * PIECE, :] = v_ref[:, n * PIECE : (n + 1) * PIECE].T
            for c in range(PIECE // rows):
                out_ref[n, 2 * PIECE + c * rows : 2 * PIECE + (c + 1) * rows, :] = k_ref[
                    :, h * PIECE + c * rows : h * PIECE + (c + 1) * rows
                ]
            out_ref[n, 3 * PIECE : 3 * PIECE + GATE_ROWS, :] = area


def beside(ref, blocks=None):
    return jnp.concatenate([ref[b] for b in blocks or range(ref.shape[0])], axis=1)


def key_rows(ref, blocks=None):
    rows = ref.shape[2]
    return jnp.concatenate(
        [
            jnp.concatenate([ref[b, c : c + rows, :] for c in range(0, PIECE, rows)], axis=1)
            for b in blocks or range(ref.shape[0])
        ],
        axis=0,
    )


def weighted_values(turned, weight):
    top, low = halves(turned.astype(F32) * weight)
    first, second, third = thirds(weight, 1.0)
    row = iota((8, weight.shape[1]), 0)
    left = jnp.where(row == 0, first, jnp.where(row == 1, third, 0.0)).astype(BF16)
    right = jnp.where(row == 0, second, 0.0).astype(BF16)
    return jnp.concatenate(
        [jnp.concatenate([top, left], axis=0), jnp.concatenate([low, right], axis=0)], axis=1
    )


def summary_kernel(v_ref, k_ref, g_ref, z_ref):
    sources, rows = v_ref.shape[0], v_ref.shape[2]
    decay = [g_ref[:, p, :] for p in range(3)]
    gate = [g_ref[:, 3 + p, :].astype(F32) for p in range(3)]
    gate = gate[0] + gate[1] + gate[2]
    after = (iota((rows, rows), 0) > iota((rows, rows), 1)).astype(BF16)
    later = (iota((sources, sources), 1) > iota((sources, sources), 0)).astype(BF16)
    suffix = sum(dot(d, after, (1, 0)) for d in decay)
    rest = sum(dot(later, d, (1, 0)) for d in decay)
    total = sum(jnp.sum(d.astype(F32), axis=0, keepdims=True) for d in decay)
    total = jnp.sum(total, axis=1, keepdims=True)
    tail = suffix + jnp.sum(rest, axis=1, keepdims=True) + gate
    new_m = jnp.max(jnp.max(tail, axis=1, keepdims=True), axis=0, keepdims=True)
    weight = jnp.exp(tail - new_m)
    state = jnp.zeros((PIECE + 8, PIECE), F32)
    group = CHUNK // rows
    for g in range(sources // group):
        mine = range(g * group, (g + 1) * group)
        turned = beside(v_ref, mine)
        share = jnp.concatenate([weight[b : b + 1, :] for b in mine], axis=1)
        keys = key_rows(k_ref, mine)
        state = state + dot(
            weighted_values(turned, share), jnp.concatenate([keys, keys], axis=0), (1, 0)
        )
    c_new = state[0:PIECE]
    n_new = state[PIECE : PIECE + 1] + state[PIECE + 1 : PIECE + 2]

    count, slab = z_ref.shape[0], z_ref.shape[1]
    most = jnp.max(jnp.max(jnp.abs(c_new), axis=1, keepdims=True), axis=0, keepdims=True)
    scaled = c_new * jnp.where(most > 0.0, 1.0 / most, 0.0)
    z_ref[:, :, 0:PIECE] = scaled.reshape(count, slab, PIECE)
    place = iota((slab, EXTRA), 0)
    lane = iota((slab, EXTRA), 1)
    extra = jnp.zeros((slab, EXTRA), F32)
    for p, part in enumerate(thirds(n_new, 256.0)):
        for h in range(PIECE // EXTRA):
            extra = jnp.where(place == 2 * p + h, part[:, h * EXTRA : (h + 1) * EXTRA], extra)
    for n, x in enumerate((new_m, total, most * 0.25)):
        for p, part in enumerate(thirds(x, 256.0)):
            extra = jnp.where((place == 6) & (lane == 3 * n + p), part, extra)
    z_ref[:, :, PIECE:] = jnp.broadcast_to(extra[None], (count, slab, EXTRA))


def entries_kernel(v_ref, k_ref, g_ref, top_ref, low_ref, aux_ref, c_ref, n_ref, m_ref, f_ref):
    step = pl.program_id(0)

    @pl.when(step == 0)
    def _():
        c_ref[...] = jnp.zeros_like(c_ref)
        n_ref[...] = jnp.zeros_like(n_ref)
        m_ref[...] = jnp.full_like(m_ref, VERY_NEGATIVE)
        f_ref[...] = jnp.zeros_like(f_ref)

    old = c_ref[...]
    entry_top, entry_low = halves(old)
    top_ref[0] = entry_top
    low_ref[0] = entry_low

    gates = beside(g_ref)
    upper = (iota((CHUNK, CHUNK), 0) <= iota((CHUNK, CHUNK), 1)).astype(BF16)
    cum = dot(gates, upper, (1, 0))
    cum = cum[0:1] + cum[1:2] + cum[2:3]
    gate = gates.astype(F32)
    gate = gate[3:4] + gate[4:5] + gate[5:6]
    total = cum[:, CHUNK - 1 : CHUNK]
    tail = total - cum + gate
    old_m = m_ref[0:1, 0:1]
    new_m = jnp.maximum(old_m + total, jnp.max(tail, axis=1, keepdims=True))
    keep = jnp.exp(old_m + total - new_m)

    row = iota((8, CHUNK), 0)
    aux = jnp.where(row == 0, n_ref[0:1, :], 0.0)
    for p, x in ((1, old_m), (2, f_ref[0:1, 0:1]), (3, cum), (4, gate - cum)):
        aux = jnp.where(row == p, x, aux)
    aux_ref[0] = aux

    keys = key_rows(k_ref)
    fresh = dot(
        weighted_values(beside(v_ref), jnp.exp(tail - new_m)),
        jnp.concatenate([keys, keys], axis=0),
        (1, 0),
    )
    c_ref[...] = keep * old + fresh[0:PIECE]
    n_ref[0:1, :] = keep * n_ref[0:1, :] + fresh[PIECE : PIECE + 1] + fresh[PIECE + 1 : PIECE + 2]
    m_ref[...] = jnp.broadcast_to(new_m, m_ref.shape)
    f_ref[...] = jnp.broadcast_to(f_ref[0:1, 0:1] + total, f_ref.shape)


def prefix_kernel(own_ref, z_ref, y_ref, nin_ref):
    count, slab, _ = z_ref.shape
    own = own_ref[0]
    small = 1.0 / 256.0

    def joined(a, b, c):
        return a + (b + c * small) * small

    scalars = z_ref[:, 6, PIECE:]
    columns = [scalars[:, p : p + 1] for p in range(9)]
    m = joined(*columns[0:3])
    most = joined(*columns[6:9]) * 4.0
    shard = iota((count, EXTRA), 0)
    later = iota((count, EXTRA), 1)
    before = shard < later
    after = (iota((count, count), 1) > iota((count, count), 0)).astype(BF16)
    gap = joined(
        *(dot(after, jnp.where(before, c, 0.0).astype(BF16), (1, 0)) for c in columns[3:6])
    )
    reach = jnp.where(before, m + gap, VERY_NEGATIVE)
    top = jnp.max(reach, axis=0, keepdims=True)
    weight = jnp.where(before, jnp.exp(reach - top), 0.0)
    heavy = weight * most
    bound = jnp.sum(heavy, axis=0, keepdims=True)
    heavy = heavy * jnp.where(bound > 0.0, 1.0 / bound, 0.0)
    heavy_top, heavy_low = halves(heavy.T)
    heavy_top, heavy_low = heavy_top[0:count], heavy_low[0:count]
    spread = jnp.concatenate([heavy_top, heavy_low, heavy_top], axis=1)
    for r in range(slab):
        x_top, x_low = halves(z_ref[:, r, 0:PIECE])
        y_ref[:, r, :] = dot(spread, jnp.concatenate([x_top, x_top, x_low], axis=0), (1, 0))

    mine = iota((1, EXTRA), 1) == own
    column = jnp.sum(jnp.where(mine, weight, 0.0), axis=1, keepdims=True)
    row = iota((8, EXTRA), 0)
    own_top = jnp.sum(jnp.where(mine, top, 0.0), axis=1, keepdims=True)
    own_bound = jnp.sum(jnp.where(mine, bound, 0.0), axis=1, keepdims=True)
    for h in range(PIECE // EXTRA):
        n = joined(*(z_ref[:, 2 * p + h, PIECE:] for p in range(3)))
        n = jnp.sum(column * n, axis=0, keepdims=True)
        area = jnp.where(row == 3, own_top, jnp.where(row == 4, own_bound, 0.0))
        for p, part in enumerate(thirds(n, 1.0)):
            area = jnp.where(row == p, part, area)
        nin_ref[:, h * EXTRA : (h + 1) * EXTRA] = area


def inside_kernel(q_ref, v_ref, k_ref, top_ref, low_ref, aux_ref, num_ref, row_ref):
    factor = PIECE**-0.5
    asked = beside(q_ref)
    turned = beside(v_ref)
    keys = key_rows(k_ref)
    aux = aux_ref[0]
    cum = aux[3:4]
    carried = cum + aux[1:2]
    score = dot(keys, asked, (1, 0))
    causal = iota((CHUNK, CHUNK), 0) <= iota((CHUNK, CHUNK), 1)
    gap = jnp.where(causal, aux.T[:, 4:5] + cum, VERY_NEGATIVE)
    top = jnp.maximum(carried, jnp.max(gap, axis=0, keepdims=True))
    weighted = jnp.exp(gap - top) * score
    outside = jnp.exp(carried - top)
    row = iota((8, CHUNK), 0)
    normal = jnp.zeros((8, CHUNK), F32)
    for p, part in enumerate(thirds(aux[0:1], 1.0)):
        normal = jnp.where(row == p, part, normal)
    reached = jnp.sum(dot(normal.astype(BF16), asked, (1, 0)), axis=0, keepdims=True)
    den = jnp.sum(weighted, axis=0, keepdims=True) + outside * reached
    num = dot(
        jnp.concatenate([turned, turned], axis=1), jnp.concatenate(halves(weighted), axis=0), (1, 0)
    )
    read = dot(
        jnp.concatenate([top_ref[0], low_ref[0]], axis=1),
        jnp.concatenate([asked, asked], axis=0),
        (1, 0),
    )
    num_ref[0] = num + outside * read
    row_ref[0] = jnp.where(row == 0, top, jnp.where(row == 1, den * factor, cum + aux[2:3]))


def finish_kernel(q_ref, num_ref, row_ref, c_ref, nin_ref, out_ref, both_ref):
    factor = PIECE**-0.5

    @pl.when(pl.program_id(0) == 0)
    def _():
        both_ref[...] = jnp.concatenate(halves(c_ref[...]), axis=1)

    asked = beside(q_ref)
    chunks = num_ref.shape[0]
    rows = jnp.concatenate([row_ref[c] for c in range(chunks)], axis=1)
    num = jnp.concatenate([num_ref[c] for c in range(chunks)], axis=1)
    m, den, cum = rows[0:1], rows[1:2], rows[2:3]
    place = iota((8, PIECE), 0)
    normal = jnp.where(place < 3, nin_ref[...], 0.0).astype(BF16)
    reached = jnp.sum(dot(normal, asked, (1, 0)), axis=0, keepdims=True)
    carried = cum + nin_ref[3:4, 0:1]
    new_m = jnp.maximum(m, carried)
    inside = jnp.exp(m - new_m)
    outside = jnp.exp(carried - new_m) * factor
    den = den * inside + outside * reached
    over = 1.0 / jnp.maximum(jnp.abs(den), 1.0)
    read = dot(both_ref[...], jnp.concatenate([asked, asked], axis=0), (1, 0))
    out = num * (inside * over * factor) + read * (outside * nin_ref[4:5, 0:1] * over)
    out_ref[...] = out.astype(BF16).T


def whole(shape):
    return pl.BlockSpec(shape, lambda i: (0,) * len(shape))


def stepped(shape, at=0):
    return pl.BlockSpec(shape, lambda i: tuple(i if d == at else 0 for d in range(len(shape))))


def part(shape, n):
    return pl.BlockSpec(shape, lambda i: (i, n, 0))


def gates(blocks):
    return pl.BlockSpec((blocks, GATE_ROWS, 128), lambda i: (i, 3 * PIECE // GATE_ROWS, 0))


def on_device(queries, keys, values, input_pre, forget_pre):
    rows = queries.shape[0]
    heads = input_pre.shape[1]
    pieces = lax.axis_size("head")
    shards = lax.axis_size("seq")
    tokens = pieces * rows
    steps = tokens // CHUNK
    group = CHUNK // rows
    tall = 3 * PIECE + GATE_ROWS
    slab = PIECE // shards
    cut = heads // PACK_STEPS
    wide = PIECE + EXTRA

    packed = pl.pallas_call(
        pack_kernel,
        grid=(PACK_STEPS,),
        in_specs=[
            stepped((rows, cut * PIECE), 1),
            stepped((rows, cut * PIECE), 1),
            stepped((rows, cut * 2 * PIECE), 1),
            whole((heads, rows)),
            whole((heads, rows)),
        ],
        out_specs=stepped((2 * cut, tall, rows)),
        out_shape=jax.ShapeDtypeStruct((pieces, tall, rows), BF16),
        scratch_shapes=[pltpu.VMEM((6, heads, rows), F32)],
        name="pack",
    )(queries, keys, values, input_pre.T, forget_pre.T)
    received = lax.all_to_all(packed, "head", split_axis=0, concat_axis=0, tiled=True)

    summary = pl.pallas_call(
        summary_kernel,
        grid=(1,),
        in_specs=[part((pieces, PIECE, rows), 1), part((pieces, PIECE, rows), 2), gates(pieces)],
        out_specs=whole((shards, slab, wide)),
        out_shape=jax.ShapeDtypeStruct((shards, slab, wide), F32),
        name="summary",
    )(received, received, received)

    spread = lax.all_to_all(summary.astype(F16), "seq", split_axis=0, concat_axis=0, tiled=True)

    entry_top, entry_low, aux = pl.pallas_call(
        entries_kernel,
        grid=(steps,),
        in_specs=[part((group, PIECE, rows), 1), part((group, PIECE, rows), 2), gates(group)],
        out_specs=[
            stepped((1, PIECE, PIECE)),
            stepped((1, PIECE, PIECE)),
            stepped((1, 8, CHUNK)),
        ],
        out_shape=[
            jax.ShapeDtypeStruct((steps, PIECE, PIECE), BF16),
            jax.ShapeDtypeStruct((steps, PIECE, PIECE), BF16),
            jax.ShapeDtypeStruct((steps, 8, CHUNK), F32),
        ],
        scratch_shapes=[
            pltpu.VMEM((PIECE, PIECE), F32),
            pltpu.VMEM((8, PIECE), F32),
            pltpu.VMEM((8, EXTRA), F32),
            pltpu.VMEM((8, EXTRA), F32),
        ],
        name="entries",
    )(received, received, received)

    own = lax.axis_index("seq").astype(jnp.int32).reshape(1)
    before, normal = pl.pallas_call(
        prefix_kernel,
        in_specs=[
            pl.BlockSpec(memory_space=pltpu.SMEM),
            pl.BlockSpec(memory_space=pltpu.VMEM),
        ],
        out_specs=[pl.BlockSpec(memory_space=pltpu.VMEM), pl.BlockSpec(memory_space=pltpu.VMEM)],
        out_shape=[
            jax.ShapeDtypeStruct((shards, slab, PIECE), F32),
            jax.ShapeDtypeStruct((8, PIECE), F32),
        ],
        name="prefix",
    )(own, spread.astype(F32))

    back = lax.all_to_all(before.astype(F16), "seq", split_axis=0, concat_axis=0, tiled=True)

    num, line = pl.pallas_call(
        inside_kernel,
        grid=(steps,),
        in_specs=[
            part((group, PIECE, rows), 0),
            part((group, PIECE, rows), 1),
            part((group, PIECE, rows), 2),
            stepped((1, PIECE, PIECE)),
            stepped((1, PIECE, PIECE)),
            stepped((1, 8, CHUNK)),
        ],
        out_specs=[stepped((1, PIECE, CHUNK)), stepped((1, 8, CHUNK))],
        out_shape=[
            jax.ShapeDtypeStruct((steps, PIECE, CHUNK), F32),
            jax.ShapeDtypeStruct((steps, 8, CHUNK), F32),
        ],
        name="inside",
    )(received, received, received, entry_top, entry_low, aux)

    return pl.pallas_call(
        finish_kernel,
        grid=(steps // 2,),
        in_specs=[
            part((2 * group, PIECE, rows), 0),
            stepped((2, PIECE, CHUNK)),
            stepped((2, 8, CHUNK)),
            whole((PIECE, PIECE)),
            whole((8, PIECE)),
        ],
        out_specs=stepped((2 * CHUNK, PIECE)),
        out_shape=jax.ShapeDtypeStruct((tokens, PIECE), BF16),
        scratch_shapes=[pltpu.VMEM((PIECE, 2 * PIECE), BF16)],
        name="finish",
    )(received, num, line, back.reshape(PIECE, PIECE).astype(F32), normal)


def solution(mesh):
    spec = P(("seq", "head"), None)

    return jax.shard_map(
        on_device, mesh=mesh, in_specs=(spec,) * 5, out_specs=P("seq", "head"), check_vma=False
    )
```

time: 142 us -> 126 us (0.89)
  waiting for transfers between devices: 30.9 us -> 18.8 us
  blocking collectives: 33.6 us -> 44.5 us
  Pallas kernels: 38.1 us -> 32.2 us
  starting transfers between devices: 30.3 us -> 24.9 us
  local copies, waits for them, and re-layouts: 3.56 us -> 0 us
    all_to_all x2 -> x1, waiting for transfers between devices: 17 us -> 0.01 us  [on_device(): lax.all_to_all(before.astype(F16), 'seq', split_axis=0, concat_axis=0, ti...]
    all_to_all x1, blocking collectives: 33.6 us -> 44.5 us  [on_device(): lax.all_to_all(packed, 'head', split_axis=0, concat_axis=0, tiled=True)]
    pallas_call x5, Pallas kernels: 35.4 us -> 29.1 us  [the longest x1 8.82 us: on_device(): pl.pallas_call(inside_kernel, grid=(steps,), in_specs=[part((group, PIECE...]
    all_to_all x2 -> x1, starting transfers between devices: 10.2 us -> 4.95 us  [on_device(): lax.all_to_all(before.astype(F16), 'seq', split_axis=0, concat_axis=0, ti...]
    all_to_all x1, waiting for transfers between devices: 13.9 us -> 18.8 us  [on_device(): lax.all_to_all(summary.astype(F16), 'seq', split_axis=0, concat_axis=0, t...]
    unnamed x4 -> x0, local copies, waits for them, and re-layouts: 2.82 us -> none
  transfers between devices with their start and end apart: 3 -> 2, of which waited for: 3 -> 1; matrix products, arithmetic and copies ran while one was open for 2% -> 0% of each run, Pallas kernels for 12% -> 13%
where the time goes in v2:
time: 126 us; the launch traced here: 125 us
  blocking collectives  44.5 us (35%)
  Pallas kernels  32.2 us (26%)
  starting transfers between devices  24.9 us (20%)
  waiting for transfers between devices  18.8 us (15%)
  other arithmetic  4.85 us (4%)
    all_to_all x1, blocking collectives, on_device(): lax.all_to_all(packed, 'head', split_axis=0, concat_axis=0, tiled=True)  44.5 us
    all_to_all x1, starting transfers between devices, on_device(): lax.all_to_all(summary.astype(F16), 'seq', split_axis=0, concat_axis=0, t...  19.9 us
    all_to_all x1, waiting for transfers between devices, on_device(): lax.all_to_all(summary.astype(F16), 'seq', split_axis=0, concat_axis=0, t...  18.8 us
    pallas_call x1, Pallas kernels, on_device(): pl.pallas_call(inside_kernel, grid=(steps,), in_specs=[part((group, PIECE...  8.82 us
    pallas_call x1, Pallas kernels, on_device(): pl.pallas_call(entries_kernel, grid=(steps,), in_specs=[part((group, PIEC...  7.83 us
    all_to_all x1, starting transfers between devices, on_device(): lax.all_to_all(before.astype(F16), 'seq', split_axis=0, concat_axis=0, ti...  4.95 us
    pallas_call x1, Pallas kernels, on_device(): pl.pallas_call(finish_kernel, grid=(steps // 2,), in_specs=[part((2 * gro...  4.68 us
    pallas_call x1, Pallas kernels, on_device(): pl.pallas_call(pack_kernel, grid=(PACK_STEPS,), in_specs=[stepped((rows,...  4.29 us
  transfers between devices with their start and end apart: 2, of which 1 were waited for; matrix products, arithmetic and copies ran while one was open for 0% of the time, Pallas kernels for 13%

profile of v2, /device:TPU:1, one launch (start us, length us, event | category | flops | bytes accessed | tf_op | source)
XLA Modules:
  0.0 125.2 jit_solution(5976790403023751718)
XLA Ops:
  0.0 4.3 %pack.1 = bf16[16,776,128]{2,1,0:T(8,128)(2,1)} custom-call(bf16[128,2048]{1,0:T(8,128)(2,1)} %q_ref.1, bf16[128,2048]{1,0:T(8,128)(2,1)} %k_ref.1, bf16[128,4096]{1,0:T(8,128)(2,1)} %v_ref.1, f32[8,128]{1,0:T(8,128)} %bitcast.6, f32[8,128]{1,0:T(8,128)} %bitcast.7), custom_call_target="tpu_custom_call" | custom-call | tf_op jit(solution)/shard_map/pack/pallas_call | solution.py:317
  4.3 44.5 %all_to_all.15.v_ref.k_ref.g_ref.q_ref = bf16[16,776,128]{2,1,0:T(8,128)(2,1)} all-to-all(bf16[16,776,128]{2,1,0:T(8,128)(2,1)} %pack.1), channel_id=1, replica_groups=mesh['seq'=32,'head'=16] {'head'}, dimensions={0} | all-to-all | bytes 6356992 | tf_op jit(solution)/shard_map/all_to_all | solution.py:332
  48.8 3.5 %summary.1 = f32[32,8,384]{2,1,0:T(8,128)} custom-call(bf16[16,776,128]{2,1,0:T(8,128)(2,1)} %all_to_all.15.v_ref.k_ref.g_ref.q_ref, bf16[16,776,128]{2,1,0:T(8,128)(2,1)} %all_to_all.15.v_ref.k_ref.g_ref.q_ref, bf16[16,776,128]{2,1,0:T(8,128)(2,1)} %all_to_all.15.v_ref.k_ref.g_ref.q_ref), custom_call_target="tpu_custom_call" | custom-call | tf_op jit(solution)/shard_map/summary/pallas_call | solution.py:334
  52.3 1.7 %convert_element_type.14 = f16[32,8,384]{2,1,0:T(8,128)(2,1)} convert(f32[32,8,384]{2,1,0:T(8,128)} %summary.1) | non-fusion elementwise | flops 98304 | bytes 589824 | tf_op jit(solution)/shard_map/convert_element_type | solution.py:343
  54.0 19.9 %all-to-all-start.1 = ((f16[32,8,384]{2,1,0:T(8,128)(2,1)}), f16[32,8,384]{2,1,0:T(8,128)(2,1)S(1)}, u32[]{:S(2)}, u32[]{:S(2)}) async-start(f16[32,8,384]{2,1,0:T(8,128)(2,1)} %convert_element_type.14), calls=%async_computation.1 | async-start | bytes 393216 | tf_op jit(solution)/shard_map/all_to_all | solution.py:343
  73.9 18.8 %all-to-all-done.1 = f16[32,8,384]{2,1,0:T(8,128)(2,1)S(1)} async-done(((f16[32,8,384]{2,1,0:T(8,128)(2,1)}), f16[32,8,384]{2,1,0:T(8,128)(2,1)S(1)}, u32[]{:S(2)}, u32[]{:S(2)}) %all-to-all-start.1) | async-done | bytes 196640 | tf_op jit(solution)/shard_map/all_to_all | solution.py:343
  92.7 0.8 convert_element_type.15.z_ref
  93.4 3.1 %prefix.1 = (f32[32,8,256]{2,1,0:T(8,128)}, f32[8,256]{1,0:T(8,128)}) custom-call(s32[1]{0:T(128)} %bitcast.2.own_ref, f32[32,8,384]{2,1,0:T(8,128)} %convert_element_type.15.z_ref), custom_call_target="tpu_custom_call" | custom-call | tf_op jit(solution)/shard_map/prefix/pallas_call | solution.py:369
  96.5 1.6 %convert_element_type.16 = f16[32,8,256]{2,1,0:T(8,128)(2,1)} convert(f32[32,8,256]{2,1,0:T(8,128)} %get-tuple-element.17) | non-fusion elementwise | flops 65536 | bytes 393216 | tf_op jit(solution)/shard_map/convert_element_type | solution.py:383
  98.2 4.9 %all-to-all-start.2 = ((f16[32,8,256]{2,1,0:T(8,128)(2,1)}), f16[32,8,256]{2,1,0:T(8,128)(2,1)S(1)}, u32[]{:S(2)}, u32[]{:S(2)}) async-start(f16[32,8,256]{2,1,0:T(8,128)(2,1)} %convert_element_type.16), calls=%async_computation.2 | async-start | bytes 262144 | tf_op jit(solution)/shard_map/all_to_all | solution.py:383
  103.1 7.8 %entries.1 = (bf16[8,256,256]{2,1,0:T(8,128)(2,1)}, bf16[8,256,256]{2,1,0:T(8,128)(2,1)}, f32[8,8,256]{2,1,0:T(8,128)}) custom-call(bf16[16,776,128]{2,1,0:T(8,128)(2,1)} %all_to_all.15.v_ref.k_ref.g_ref.q_ref, bf16[16,776,128]{2,1,0:T(8,128)(2,1)} %all_to_all.15.v_ref.k_ref.g_ref.q_ref, bf16[16,776,128]{2,1,0:T(8,128)(2,1)} %all_to_all.15.v_ref.k_ref.g_ref.q_ref), custom_call_target="tpu_custom_call" | custom-call | tf_op jit(solution)/shard_map/entries/pallas_call | solution.py:345
  110.9 8.8 %inside.1 = (f32[8,256,256]{2,1,0:T(8,128)}, f32[8,8,256]{2,1,0:T(8,128)}) custom-call(bf16[16,776,128]{2,1,0:T(8,128)(2,1)} %all_to_all.15.v_ref.k_ref.g_ref.q_ref, bf16[16,776,128]{2,1,0:T(8,128)(2,1)} %all_to_all.15.v_ref.k_ref.g_ref.q_ref, bf16[16,776,128]{2,1,0:T(8,128)(2,1)} %all_to_all.15.v_ref.k_ref.g_ref.q_ref, ...), custom_call_target="tpu_custom_call" | custom-call | tf_op jit(solution)/shard_map/inside/pallas_call | solution.py:385
  119.8 0.0 all-to-all-done.2
  119.8 0.7 bitcast_convert_fusion.c_ref
  120.5 4.7 %finish.1 = bf16[2048,256]{1,0:T(8,128)(2,1)} custom-call(bf16[16,776,128]{2,1,0:T(8,128)(2,1)} %all_to_all.15.v_ref.k_ref.g_ref.q_ref, f32[8,256,256]{2,1,0:T(8,128)} %get-tuple-element.15.num_ref, f32[8,8,256]{2,1,0:T(8,128)} %get-tuple-element.16.row_ref, f32[256,256]{1,0:T(8,128)} %bitcast_convert_fusion.c_ref, f32[8,256]{1,0:T(8,128)} %get-tuple-element.18.nin_ref), custom_call_target="tpu_custom_call" | custom-call | tf_op jit(solution)/shard_map/finish/pallas_call | solution.py:404
Async XLA Ops:
  54.0 38.7 %all-to-all-start.1 = ((f16[32,8,384]{2,1,0:T(8,128)(2,1)}), f16[32,8,384]{2,1,0:T(8,128)(2,1)S(1)}, u32[]{:S(2)}, u32[]{:S(2)}) async-start(f16[32,8,384]{2,1,0:T(8,128)(2,1)} %convert_element_type.14), calls=%async_computation.1 | async-start | bytes 393216 | tf_op jit(solution)/shard_map/all_to_all | solution.py:343
  98.2 21.6 %all-to-all-start.2 = ((f16[32,8,256]{2,1,0:T(8,128)(2,1)}), f16[32,8,256]{2,1,0:T(8,128)(2,1)S(1)}, u32[]{:S(2)}, u32[]{:S(2)}) async-start(f16[32,8,256]{2,1,0:T(8,128)(2,1)} %convert_element_type.16), calls=%async_computation.2 | async-start | bytes 262144 | tf_op jit(solution)/shard_map/all_to_all | solution.py:383

commit v3 on v2

v3 whole, which is shorter than its diff:
```python
import jax
import jax.numpy as jnp
from jax import lax
from jax.experimental import pallas as pl
from jax.experimental.pallas import tpu as pltpu
from jax.sharding import PartitionSpec as P

VERY_NEGATIVE = -1e30
CHUNK = 256
PIECE = 256
FINISH_STEPS = 4
HALF = PIECE // 2
KEYS = PIECE
ASKED = 2 * PIECE
GATES = ASKED + HALF
VMEM_LIMIT = 24 << 20
EXTRA = 128
GATE_ROWS = 8
F32 = jnp.float32
BF16 = jnp.bfloat16
F16 = jnp.float16


def dot(a, b, contract):
    return lax.dot_general(a, b, ((contract[:1], contract[1:]), ((), ())), preferred_element_type=F32)


def halves(x):
    top = x.astype(BF16)
    return top, (x - top.astype(F32)).astype(BF16)


def thirds(x, scale):
    first = x.astype(BF16).astype(F32)
    rest = (x - first) * scale
    second = rest.astype(BF16).astype(F32)
    third = ((rest - second) * scale).astype(BF16).astype(F32)
    return first, second, third


def iota(shape, dim):
    return lax.broadcasted_iota(jnp.int32, shape, dim)


def pack_kernel(q_ref, k_ref, v_ref, gate_ref, forget_ref, out_ref):
    rows = k_ref.shape[0]
    parts = []
    for x in (-jnp.log1p(jnp.exp(-forget_ref[...])), gate_ref[...]):
        parts += thirds(x, 1.0)
    row = iota((GATE_ROWS, rows), 0)
    for h in range(k_ref.shape[1] // PIECE):
        area = jnp.zeros((GATE_ROWS, rows), F32)
        for p in range(6):
            area = jnp.where(row == p, parts[p][h : h + 1], area)
        area = area.astype(BF16)
        for u in range(2):
            n = 2 * h + u
            out_ref[n, 0:PIECE, :] = v_ref[:, n * PIECE : (n + 1) * PIECE].T
            for c in range(2):
                left = h * PIECE + (c ^ u) * HALF
                out_ref[n, KEYS + c * HALF : KEYS + (c + 1) * HALF, :] = k_ref[:, left : left + HALF]
            left = h * PIECE + u * HALF
            out_ref[n, ASKED:GATES, :] = q_ref[:, left : left + HALF].T
            out_ref[n, GATES : GATES + GATE_ROWS, :] = area


def beside(ref, blocks, low, high):
    return jnp.concatenate([ref[b, low:high, :] for b in blocks], axis=1)


def key_rows(ref, blocks):
    return jnp.concatenate(
        [
            jnp.concatenate([ref[b, KEYS + c * HALF : KEYS + (c + 1) * HALF, :] for c in range(2)], axis=1)
            for b in blocks
        ],
        axis=0,
    )


def asked_rows(ref, other_ref, blocks):
    return jnp.concatenate([beside(ref, blocks, ASKED, GATES), beside(other_ref, blocks, 0, HALF)], axis=0)


def chunk_blocks(ref, chunk):
    group = CHUNK // ref.shape[2]
    return range(chunk * group, (chunk + 1) * group)


def weighted_values(turned, weight):
    top, low = halves(turned.astype(F32) * weight)
    first, second, third = thirds(weight, 1.0)
    row = iota((8, weight.shape[1]), 0)
    left = jnp.where(row == 0, first, jnp.where(row == 1, third, 0.0)).astype(BF16)
    right = jnp.where(row == 0, second, 0.0).astype(BF16)
    return jnp.concatenate(
        [jnp.concatenate([top, left], axis=0), jnp.concatenate([low, right], axis=0)], axis=1
    )


def summary_kernel(r_ref, z_ref):
    sources, rows = r_ref.shape[0], r_ref.shape[2]
    decay = [r_ref[:, GATES + p, :] for p in range(3)]
    gate = [r_ref[:, GATES + 3 + p, :].astype(F32) for p in range(3)]
    gate = gate[0] + gate[1] + gate[2]
    after = (iota((rows, rows), 0) > iota((rows, rows), 1)).astype(BF16)
    later = (iota((sources, sources), 1) > iota((sources, sources), 0)).astype(BF16)
    suffix = sum(dot(d, after, (1, 0)) for d in decay)
    rest = sum(dot(later, d, (1, 0)) for d in decay)
    total = sum(jnp.sum(d.astype(F32), axis=0, keepdims=True) for d in decay)
    total = jnp.sum(total, axis=1, keepdims=True)
    tail = suffix + jnp.sum(rest, axis=1, keepdims=True) + gate
    new_m = jnp.max(jnp.max(tail, axis=1, keepdims=True), axis=0, keepdims=True)
    weight = jnp.exp(tail - new_m)
    state = jnp.zeros((PIECE + 8, PIECE), F32)
    for g in range(sources * rows // CHUNK):
        mine = chunk_blocks(r_ref, g)
        turned = beside(r_ref, mine, 0, PIECE)
        share = jnp.concatenate([weight[b : b + 1, :] for b in mine], axis=1)
        keys = key_rows(r_ref, mine)
        state = state + dot(
            weighted_values(turned, share), jnp.concatenate([keys, keys], axis=0), (1, 0)
        )
    c_new = state[0:PIECE]
    n_new = state[PIECE : PIECE + 1] + state[PIECE + 1 : PIECE + 2]

    count, slab = z_ref.shape[0], z_ref.shape[1]
    most = jnp.max(jnp.max(jnp.abs(c_new), axis=1, keepdims=True), axis=0, keepdims=True)
    scaled = c_new * jnp.where(most > 0.0, 1.0 / most, 0.0)
    z_ref[:, :, 0:PIECE] = scaled.reshape(count, slab, PIECE)
    place = iota((slab, EXTRA), 0)
    lane = iota((slab, EXTRA), 1)
    extra = jnp.zeros((slab, EXTRA), F32)
    for p, part in enumerate(thirds(n_new, 256.0)):
        for h in range(PIECE // EXTRA):
            extra = jnp.where(place == 2 * p + h, part[:, h * EXTRA : (h + 1) * EXTRA], extra)
    for n, x in enumerate((new_m, total, most * 0.25)):
        for p, part in enumerate(thirds(x, 256.0)):
            extra = jnp.where((place == 6) & (lane == 3 * n + p), part, extra)
    z_ref[:, :, PIECE:] = jnp.broadcast_to(extra[None], (count, slab, EXTRA))


def entries_kernel(r_ref, top_ref, low_ref, aux_ref):
    upper = (iota((CHUNK, CHUNK), 0) <= iota((CHUNK, CHUNK), 1)).astype(BF16)
    row = iota((8, CHUNK), 0)
    state = jnp.zeros((PIECE, PIECE), F32)
    normal = jnp.zeros((1, PIECE), F32)
    old_m = jnp.full((1, 1), VERY_NEGATIVE, F32)
    start = jnp.zeros((1, 1), F32)
    steps = top_ref.shape[0]
    for step in range(steps):
        mine = chunk_blocks(r_ref, step)
        top_ref[step], low_ref[step] = halves(state)
        gates = beside(r_ref, mine, GATES, GATES + GATE_ROWS)
        cum = dot(gates, upper, (1, 0))
        cum = cum[0:1] + cum[1:2] + cum[2:3]
        gate = gates.astype(F32)
        gate = gate[3:4] + gate[4:5] + gate[5:6]
        total = cum[:, CHUNK - 1 : CHUNK]
        tail = total - cum + gate
        new_m = jnp.maximum(old_m + total, jnp.max(tail, axis=1, keepdims=True))
        keep = jnp.exp(old_m + total - new_m)
        aux = jnp.where(row == 0, normal, 0.0)
        for p, x in ((1, old_m), (2, start), (3, cum), (4, gate - cum)):
            aux = jnp.where(row == p, x, aux)
        aux_ref[step] = aux
        if step < steps - 1:
            keys = key_rows(r_ref, mine)
            fresh = dot(
                weighted_values(beside(r_ref, mine, 0, PIECE), jnp.exp(tail - new_m)),
                jnp.concatenate([keys, keys], axis=0),
                (1, 0),
            )
            state = keep * state + fresh[0:PIECE]
            normal = keep * normal + fresh[PIECE : PIECE + 1] + fresh[PIECE + 1 : PIECE + 2]
            old_m = new_m
            start = start + total


def prefix_kernel(own_ref, z_ref, y_ref, nin_ref):
    count, slab, _ = z_ref.shape
    own = own_ref[0]
    small = 1.0 / 256.0

    def joined(a, b, c):
        return a + (b + c * small) * small

    scalars = z_ref[:, 6, PIECE:]
    columns = [scalars[:, p : p + 1] for p in range(9)]
    m = joined(*columns[0:3])
    most = joined(*columns[6:9]) * 4.0
    shard = iota((count, EXTRA), 0)
    later = iota((count, EXTRA), 1)
    before = shard < later
    after = (iota((count, count), 1) > iota((count, count), 0)).astype(BF16)
    gap = joined(
        *(dot(after, jnp.where(before, c, 0.0).astype(BF16), (1, 0)) for c in columns[3:6])
    )
    reach = jnp.where(before, m + gap, VERY_NEGATIVE)
    top = jnp.max(reach, axis=0, keepdims=True)
    weight = jnp.where(before, jnp.exp(reach - top), 0.0)
    heavy = weight * most
    bound = jnp.sum(heavy, axis=0, keepdims=True)
    heavy = heavy * jnp.where(bound > 0.0, 1.0 / bound, 0.0)
    size = count * slab
    shift = slab.bit_length() - 1
    down = (iota((size, count), 0) >> shift == iota((size, count), 1)).astype(BF16)
    right = (iota((count, size), 0) == iota((count, size), 1) >> shift).astype(BF16)
    same = (iota((size, size), 0) & (slab - 1)) == (iota((size, size), 1) & (slab - 1))
    turned = heavy.T[0:count, :]
    wide = []
    for x in halves(turned):
        x = dot(dot(down, x, (1, 0)).astype(BF16), right, (1, 0))
        wide.append(jnp.where(same, x, 0.0).astype(BF16))
    x_top, x_low = halves(z_ref[:, :, 0:PIECE].reshape(size, PIECE))
    y = dot(
        jnp.concatenate([wide[0], wide[1], wide[0]], axis=1),
        jnp.concatenate([x_top, x_top, x_low], axis=0),
        (1, 0),
    )
    y_ref[...] = y.reshape(count, slab, PIECE)

    mine = iota((1, EXTRA), 1) == own
    column = jnp.sum(jnp.where(mine, weight, 0.0), axis=1, keepdims=True)
    row = iota((8, EXTRA), 0)
    own_top = jnp.sum(jnp.where(mine, top, 0.0), axis=1, keepdims=True)
    own_bound = jnp.sum(jnp.where(mine, bound, 0.0), axis=1, keepdims=True)
    for h in range(PIECE // EXTRA):
        n = joined(*(z_ref[:, 2 * p + h, PIECE:] for p in range(3)))
        n = jnp.sum(column * n, axis=0, keepdims=True)
        area = jnp.where(row == 3, own_top, jnp.where(row == 4, own_bound, 0.0))
        for p, part in enumerate(thirds(n, 1.0)):
            area = jnp.where(row == p, part, area)
        nin_ref[:, h * EXTRA : (h + 1) * EXTRA] = area


def inside_kernel(r_ref, other_ref, top_ref, low_ref, aux_ref, num_ref, row_ref):
    factor = PIECE**-0.5
    causal = iota((CHUNK, CHUNK), 0) <= iota((CHUNK, CHUNK), 1)
    row = iota((8, CHUNK), 0)
    for step in range(num_ref.shape[0]):
        mine = chunk_blocks(r_ref, step)
        asked = asked_rows(r_ref, other_ref, mine)
        turned = beside(r_ref, mine, 0, PIECE)
        aux = aux_ref[step]
        cum = aux[3:4]
        carried = cum + aux[1:2]
        score = dot(key_rows(r_ref, mine), asked, (1, 0))
        gap = jnp.where(causal, aux.T[:, 4:5] + cum, VERY_NEGATIVE)
        top = jnp.maximum(carried, jnp.max(gap, axis=0, keepdims=True))
        weighted = jnp.exp(gap - top) * score
        outside = jnp.exp(carried - top)
        normal = jnp.zeros((8, CHUNK), F32)
        for p, part in enumerate(thirds(aux[0:1], 1.0)):
            normal = jnp.where(row == p, part, normal)
        reached = jnp.sum(dot(normal.astype(BF16), asked, (1, 0)), axis=0, keepdims=True)
        den = jnp.sum(weighted, axis=0, keepdims=True) + outside * reached
        num = dot(
            jnp.concatenate([turned, turned], axis=1),
            jnp.concatenate(halves(weighted), axis=0),
            (1, 0),
        )
        read = dot(
            jnp.concatenate([top_ref[step], low_ref[step]], axis=1),
            jnp.concatenate([asked, asked], axis=0),
            (1, 0),
        )
        num_ref[step] = num + outside * read
        row_ref[step] = jnp.where(row == 0, top, jnp.where(row == 1, den * factor, cum + aux[2:3]))


def finish_kernel(own_ref, other_ref, num_ref, row_ref, c_ref, nin_ref, out_ref, both_ref):
    factor = PIECE**-0.5
    at = pl.program_id(0)

    @pl.when(at == 0)
    def _():
        both_ref[...] = jnp.concatenate(halves(c_ref[...]), axis=1)

    place = iota((8, PIECE), 0)
    normal = jnp.where(place < 3, nin_ref[...], 0.0).astype(BF16)
    before_m = nin_ref[3:4, 0:1]
    bound = nin_ref[4:5, 0:1]
    for step in range(num_ref.shape[0]):
        blocks = chunk_blocks(own_ref, step)
        asked = jnp.concatenate(
            [beside(own_ref, blocks, 0, HALF), beside(other_ref, blocks, 0, HALF)], axis=0
        )
        rows = row_ref[step]
        m, den, cum = rows[0:1], rows[1:2], rows[2:3]
        reached = jnp.sum(dot(normal, asked, (1, 0)), axis=0, keepdims=True)
        carried = cum + before_m
        new_m = jnp.maximum(m, carried)
        inside = jnp.exp(m - new_m)
        outside = jnp.exp(carried - new_m) * factor
        den = den * inside + outside * reached
        over = 1.0 / jnp.maximum(jnp.abs(den), 1.0)
        read = dot(both_ref[...], jnp.concatenate([asked, asked], axis=0), (1, 0))
        out = num_ref[step] * (inside * over * factor) + read * (outside * bound * over)
        out_ref[step * CHUNK : (step + 1) * CHUNK, :] = out.astype(BF16).T


def whole(shape):
    return pl.BlockSpec(shape, lambda i: (0,) * len(shape))


def stepped(shape, at=0):
    return pl.BlockSpec(shape, lambda i: tuple(i if d == at else 0 for d in range(len(shape))))


def near(x):
    return pltpu.with_memory_space_constraint(x, pltpu.VMEM)


NEAR = pl.BlockSpec(memory_space=pltpu.VMEM)
FAR = pl.BlockSpec()
PARAMS = pltpu.CompilerParams(vmem_limit_bytes=VMEM_LIMIT)


def on_device(queries, keys, values, input_pre, forget_pre):
    rows = queries.shape[0]
    pieces = lax.axis_size("head")
    shards = lax.axis_size("seq")
    tokens = pieces * rows
    steps = tokens // CHUNK
    tall = GATES + GATE_ROWS
    slab = PIECE // shards
    wide = PIECE + EXTRA

    packed = pl.pallas_call(
        pack_kernel,
        in_specs=[FAR] * 5,
        out_specs=NEAR,
        out_shape=pltpu.VMEM((pieces, tall, rows), BF16),
        compiler_params=PARAMS,
        name="pack",
    )(queries, keys, values, input_pre.T, forget_pre.T)

    received = lax.all_to_all(packed, "head", split_axis=0, concat_axis=0, tiled=True)

    summary = pl.pallas_call(
        summary_kernel,
        in_specs=[NEAR],
        out_specs=NEAR,
        out_shape=pltpu.VMEM((shards, slab, wide), F32),
        compiler_params=PARAMS,
        name="summary",
    )(near(received))

    spread = lax.all_to_all(summary.astype(F16), "seq", split_axis=0, concat_axis=0, tiled=True)

    other = lax.ppermute(received[:, ASKED:GATES, :], "head", [(i, i ^ 1) for i in range(pieces)])

    entry_top, entry_low, aux = pl.pallas_call(
        entries_kernel,
        in_specs=[NEAR],
        out_specs=[FAR] * 3,
        out_shape=[
            jax.ShapeDtypeStruct((steps, PIECE, PIECE), BF16),
            jax.ShapeDtypeStruct((steps, PIECE, PIECE), BF16),
            jax.ShapeDtypeStruct((steps, 8, CHUNK), F32),
        ],
        name="entries",
    )(near(received))

    own = lax.axis_index("seq").astype(jnp.int32).reshape(1)
    before, normal = pl.pallas_call(
        prefix_kernel,
        in_specs=[pl.BlockSpec(memory_space=pltpu.SMEM), NEAR],
        out_specs=[NEAR, FAR],
        out_shape=[
            pltpu.VMEM((shards, slab, PIECE), F32),
            jax.ShapeDtypeStruct((8, PIECE), F32),
        ],
        compiler_params=pltpu.CompilerParams(vmem_limit_bytes=60 << 20),
        name="prefix",
    )(own, near(spread.astype(F32)))

    back = lax.all_to_all(before.astype(F16), "seq", split_axis=0, concat_axis=0, tiled=True)

    num, line = pl.pallas_call(
        inside_kernel,
        in_specs=[NEAR, NEAR, FAR, FAR, FAR],
        out_specs=[FAR] * 2,
        out_shape=[
            jax.ShapeDtypeStruct((steps, PIECE, CHUNK), F32),
            jax.ShapeDtypeStruct((steps, 8, CHUNK), F32),
        ],
        name="inside",
    )(near(received), near(other), entry_top, entry_low, aux)

    return pl.pallas_call(
        finish_kernel,
        grid=(FINISH_STEPS,),
        in_specs=[
            pl.BlockSpec((pieces // FINISH_STEPS, HALF, rows), lambda i: (i, ASKED // HALF, 0)),
            stepped((pieces // FINISH_STEPS, HALF, rows)),
            stepped((steps // FINISH_STEPS, PIECE, CHUNK)),
            stepped((steps // FINISH_STEPS, 8, CHUNK)),
            NEAR,
            whole((8, PIECE)),
        ],
        out_specs=stepped((tokens // FINISH_STEPS, PIECE)),
        out_shape=jax.ShapeDtypeStruct((tokens, PIECE), BF16),
        scratch_shapes=[pltpu.VMEM((PIECE, 2 * PIECE), BF16)],
        compiler_params=pltpu.CompilerParams(vmem_limit_bytes=60 << 20),
        name="finish",
    )(received, other, num, line, near(back.reshape(PIECE, PIECE).astype(F32)), normal)


def solution(mesh):
    spec = P(("seq", "head"), None)

    return jax.shard_map(
        on_device, mesh=mesh, in_specs=(spec,) * 5, out_specs=P("seq", "head"), check_vma=False
    )
```

time: 126 us -> 113 us (0.90)
  Pallas kernels: 32.2 us -> 17 us
  local copies, waits for them, and re-layouts: 0 us -> 7.29 us
  blocking collectives: 44.5 us -> 39.5 us
  other arithmetic: 4.85 us -> 1.41 us
  waiting for transfers between devices: 18.8 us -> 21 us
    pallas_call x5, Pallas kernels: 29.1 us -> 15.6 us  [the longest x1 5.35 us: on_device(): pl.pallas_call(inside_kernel, in_specs=[NEAR, NEAR, FAR, FAR, FAR], out_s...]
    unnamed x0 -> x16, local copies, waits for them, and re-layouts: none -> 6.43 us
    all_to_all x1, waiting for transfers between devices: 0.01 us -> 5.25 us  [on_device(): lax.all_to_all(before.astype(F16), 'seq', split_axis=0, concat_axis=0, ti...]
    all_to_all x1, blocking collectives: 44.5 us -> 39.5 us  [on_device(): lax.all_to_all(packed, 'head', split_axis=0, concat_axis=0, tiled=True)]
    all_to_all x1, waiting for transfers between devices: 18.8 us -> 15.7 us  [on_device(): lax.all_to_all(summary.astype(F16), 'seq', split_axis=0, concat_axis=0, t...]
    ppermute x0 -> x1, starting transfers between devices: none -> 2.18 us  [on_device(): lax.ppermute(received[:, ASKED:GATES, :], 'head', [(i, i ^ 1) for i in ra...]
    pallas_call x1, Pallas kernels: 3.11 us -> 1.35 us  [on_device(): pl.pallas_call(prefix_kernel, in_specs=[pl.BlockSpec(memory_space=pltpu.S...]
  transfers between devices with their start and end apart: 2 -> 3, of which waited for: 1 -> 2; matrix products, arithmetic and copies ran while one was open for 0% -> 1% of each run, Pallas kernels for 13% -> 9%
where the time goes in v3:
time: 113 us; the launch traced here: 112 us
  blocking collectives  39.5 us (35%)
  starting transfers between devices  26 us (23%)
  waiting for transfers between devices  21 us (19%)
  Pallas kernels  17 us (15%)
  local copies, waits for them, and re-layouts  7.29 us (6%)
  other arithmetic  1.41 us (1%)
    all_to_all x1, blocking collectives, on_device(): lax.all_to_all(packed, 'head', split_axis=0, concat_axis=0, tiled=True)  39.5 us
    all_to_all x1, starting transfers between devices, on_device(): lax.all_to_all(summary.astype(F16), 'seq', split_axis=0, concat_axis=0, t...  18.8 us
    all_to_all x1, waiting for transfers between devices, on_device(): lax.all_to_all(summary.astype(F16), 'seq', split_axis=0, concat_axis=0, t...  15.7 us
    unnamed x16, local copies, waits for them, and re-layouts  6.43 us
    pallas_call x1, Pallas kernels, on_device(): pl.pallas_call(inside_kernel, in_specs=[NEAR, NEAR, FAR, FAR, FAR], out_s...  5.35 us
    all_to_all x1, waiting for transfers between devices, on_device(): lax.all_to_all(before.astype(F16), 'seq', split_axis=0, concat_axis=0, ti...  5.25 us
    all_to_all x1, starting transfers between devices, on_device(): lax.all_to_all(before.astype(F16), 'seq', split_axis=0, concat_axis=0, ti...  4.96 us
    pallas_call x1, Pallas kernels, on_device(): pl.pallas_call(finish_kernel, grid=(FINISH_STEPS,), in_specs=[pl.BlockSpe...  4.7 us
  transfers between devices with their start and end apart: 3, of which 2 were waited for; matrix products, arithmetic and copies ran while one was open for 1% of the time, Pallas kernels for 9%

profile of v3, /device:TPU:1, one launch (start us, length us, event | category | flops | bytes accessed | tf_op | source)
XLA Modules:
  0.0 112.3 jit_solution(6057043192927043687)
XLA Ops:
  0.0 0.0 copy-start.3
  0.0 1.2 %copy-done.3 = bf16[128,4096]{1,0:T(8,128)(2,1)S(1)} copy-done((bf16[128,4096]{1,0:T(8,128)(2,1)S(1)}, bf16[128,4096]{1,0:T(8,128)(2,1)}, u32[]{:S(2)}) %copy-start.3) | copy-done | bytes 1048600
  1.2 0.0 copy-start.4
  1.2 1.0 copy-done.4
  2.3 0.0 copy-start.5
  2.3 1.0 copy-done.5
  3.3 0.0 copy-start.6
  3.3 0.7 copy-done.6
  4.0 0.0 copy-start.7
  4.0 0.7 copy-done.7
  4.7 0.6 pack.1
  5.3 39.5 %all_to_all.15.r_ref.own_ref = bf16[16,648,128]{2,1,0:T(8,128)(2,1)S(1)} all-to-all(bf16[16,648,128]{2,1,0:T(8,128)(2,1)S(1)} %pack.1), channel_id=1, replica_groups=mesh['seq'=32,'head'=16] {'head'}, dimensions={0} | all-to-all | bytes 5308416 | tf_op jit(solution)/shard_map/all_to_all | solution.py:339
  44.8 0.0 copy-start
  44.8 1.2 %summary.1 = f32[32,8,384]{2,1,0:T(8,128)S(1)} custom-call(bf16[16,648,128]{2,1,0:T(8,128)(2,1)S(1)} %all_to_all.15.r_ref.own_ref), custom_call_target="tpu_custom_call" | custom-call | tf_op jit(solution)/shard_map/summary/pallas_call | solution.py:341
  46.0 0.7 convert_element_type.14
  46.7 18.8 %all-to-all-start.1 = ((f16[32,8,384]{2,1,0:T(8,128)(2,1)}), f16[32,8,384]{2,1,0:T(8,128)(2,1)S(1)}, u32[]{:S(2)}, u32[]{:S(2)}) async-start(f16[32,8,384]{2,1,0:T(8,128)(2,1)} %convert_element_type.14), calls=%async_computation.1 | async-start | bytes 393216 | tf_op jit(solution)/shard_map/all_to_all | solution.py:350
  65.5 0.9 slice.4
  66.4 2.2 %collective-permute-start = (bf16[16,128,128]{2,1,0:T(8,128)(2,1)}, bf16[16,128,128]{2,1,0:T(8,128)(2,1)S(1)}, u32[]{:S(2)}, u32[]{:S(2)}) collective-permute-start(bf16[16,128,128]{2,1,0:T(8,128)(2,1)} %slice.4), channel_id=1, source_target_pairs={{0,1},{1,0},{2,3},{3,2},{4,5},{5,4},{6,7},{7,6},{8,9},{9,8},{10,11... | collective-permute-start | bytes 1572872 | tf_op jit(solution)/shard_map/ppermute | solution.py:352
  68.6 15.7 %all-to-all-done.1 = f16[32,8,384]{2,1,0:T(8,128)(2,1)S(1)} async-done(((f16[32,8,384]{2,1,0:T(8,128)(2,1)}), f16[32,8,384]{2,1,0:T(8,128)(2,1)S(1)}, u32[]{:S(2)}, u32[]{:S(2)}) %all-to-all-start.1) | async-done | bytes 196640 | tf_op jit(solution)/shard_map/all_to_all | solution.py:350
  84.4 0.0 copy-done
  84.4 1.3 %prefix.1 = (f32[32,8,256]{2,1,0:T(8,128)S(1)}, f32[8,256]{1,0:T(8,128)}) custom-call(s32[1]{0:T(128)} %bitcast.2.own_ref, f32[32,8,384]{2,1,0:T(8,128)S(1)} %convert_element_type.15.z_ref), custom_call_target="tpu_custom_call" | custom-call | tf_op jit(solution)/shard_map/prefix/pallas_call | solution.py:367
  85.7 0.7 convert_element_type.16
  86.4 5.0 %all-to-all-start.2 = ((f16[32,8,256]{2,1,0:T(8,128)(2,1)}), f16[32,8,256]{2,1,0:T(8,128)(2,1)S(1)}, u32[]{:S(2)}, u32[]{:S(2)}) async-start(f16[32,8,256]{2,1,0:T(8,128)(2,1)} %convert_element_type.16), calls=%async_computation.2 | async-start | bytes 262144 | tf_op jit(solution)/shard_map/all_to_all | solution.py:379
  91.3 0.0 copy-start.1
  91.3 1.7 %copy-done.1 = bf16[16,648,128]{2,1,0:T(8,128)(2,1)S(1)} copy-done((bf16[16,648,128]{2,1,0:T(8,128)(2,1)S(1)}, bf16[16,648,128]{2,1,0:T(8,128)(2,1)}, u32[]{:S(2)}) %copy-start.1) | copy-done | bytes 2654232
  93.1 3.8 %entries.1 = (bf16[8,256,256]{2,1,0:T(8,128)(2,1)}, bf16[8,256,256]{2,1,0:T(8,128)(2,1)}, f32[8,8,256]{2,1,0:T(8,128)}) custom-call(bf16[16,648,128]{2,1,0:T(8,128)(2,1)S(1)} %copy-done.1), custom_call_target="tpu_custom_call" | custom-call | tf_op jit(solution)/shard_map/entries/pallas_call | solution.py:354
  96.9 0.0 collective-permute-done.other_ref
  96.9 0.0 copy-start.2
  96.9 5.3 %inside.1 = (f32[8,256,256]{2,1,0:T(8,128)}, f32[8,8,256]{2,1,0:T(8,128)}) custom-call(bf16[16,648,128]{2,1,0:T(8,128)(2,1)S(1)} %copy-done.1, bf16[16,128,128]{2,1,0:T(8,128)(2,1)S(1)} %collective-permute-done.other_ref, bf16[8,256,256]{2,1,0:T(8,128)(2,1)} %get-tuple-element.12.top_ref, bf16[8,256,256]{2,1,0:T(8,128)(2,1)} %get-tuple-element.13.low_ref, ...), custom_call_target="tpu_custom_call" | custom-call | tf_op jit(solution)/shard_map/inside/pallas_call | solution.py:381
  102.3 0.0 copy-done.2
  102.3 5.2 %all-to-all-done.2 = f16[32,8,256]{2,1,0:T(8,128)(2,1)S(1)} async-done(((f16[32,8,256]{2,1,0:T(8,128)(2,1)}), f16[32,8,256]{2,1,0:T(8,128)(2,1)S(1)}, u32[]{:S(2)}, u32[]{:S(2)}) %all-to-all-start.2) | async-done | bytes 131104 | tf_op jit(solution)/shard_map/all_to_all | solution.py:379
  107.6 4.7 %finish.1 = bf16[2048,256]{1,0:T(8,128)(2,1)} custom-call(bf16[16,648,128]{2,1,0:T(8,128)(2,1)} %copy-done, bf16[16,128,128]{2,1,0:T(8,128)(2,1)} %copy-done.2, f32[8,256,256]{2,1,0:T(8,128)} %get-tuple-element.15.num_ref, f32[8,8,256]{2,1,0:T(8,128)} %get-tuple-element.16.row_ref, f32[256,256]{1,0:T(8,128)S(1)} %bitcast_convert_fusion.c_ref, ...), custom_call_target="tpu_custom_call" | custom-call | tf_op jit(solution)/shard_map/finish/pallas_call | solution.py:392
  (2 shorter events, 0.0 us)
Async XLA Ops:
  0.0 1.2 %copy-start.3 = (bf16[128,4096]{1,0:T(8,128)(2,1)S(1)}, bf16[128,4096]{1,0:T(8,128)(2,1)}, u32[]{:S(2)}) copy-start(bf16[128,4096]{1,0:T(8,128)(2,1)} %v_ref.1) | copy-start | bytes 3145732
  1.2 1.0 copy-start.4
  2.3 1.0 copy-start.5
  3.3 0.7 copy-start.6
  4.0 0.7 copy-start.7
  44.8 39.6 %copy-start = (bf16[16,648,128]{2,1,0:T(8,128)(2,1)}, bf16[16,648,128]{2,1,0:T(8,128)(2,1)S(1)}, u32[]{:S(2)}) copy-start(bf16[16,648,128]{2,1,0:T(8,128)(2,1)S(1)} %all_to_all.15.r_ref.own_ref) | copy-start | bytes 7962628
  46.7 37.6 %all-to-all-start.1 = ((f16[32,8,384]{2,1,0:T(8,128)(2,1)}), f16[32,8,384]{2,1,0:T(8,128)(2,1)S(1)}, u32[]{:S(2)}, u32[]{:S(2)}) async-start(f16[32,8,384]{2,1,0:T(8,128)(2,1)} %convert_element_type.14), calls=%async_computation.1 | async-start | bytes 393216 | tf_op jit(solution)/shard_map/all_to_all | solution.py:350
  66.4 30.5 %collective-permute-start = (bf16[16,128,128]{2,1,0:T(8,128)(2,1)}, bf16[16,128,128]{2,1,0:T(8,128)(2,1)S(1)}, u32[]{:S(2)}, u32[]{:S(2)}) collective-permute-start(bf16[16,128,128]{2,1,0:T(8,128)(2,1)} %slice.4), channel_id=1, source_target_pairs={{0,1},{1,0},{2,3},{3,2},{4,5},{5,4},{6,7},{7,6},{8,9},{9,8},{10,11... | collective-permute-start | bytes 1572872 | tf_op jit(solution)/shard_map/ppermute | solution.py:352
  86.4 21.2 %all-to-all-start.2 = ((f16[32,8,256]{2,1,0:T(8,128)(2,1)}), f16[32,8,256]{2,1,0:T(8,128)(2,1)S(1)}, u32[]{:S(2)}, u32[]{:S(2)}) async-start(f16[32,8,256]{2,1,0:T(8,128)(2,1)} %convert_element_type.16), calls=%async_computation.2 | async-start | bytes 262144 | tf_op jit(solution)/shard_map/all_to_all | solution.py:379
  91.3 1.8 %copy-start.1 = (bf16[16,648,128]{2,1,0:T(8,128)(2,1)S(1)}, bf16[16,648,128]{2,1,0:T(8,128)(2,1)}, u32[]{:S(2)}) copy-start(bf16[16,648,128]{2,1,0:T(8,128)(2,1)} %copy-done) | copy-start | bytes 7962628
  96.9 5.4 %copy-start.2 = (bf16[16,128,128]{2,1,0:T(8,128)(2,1)}, bf16[16,128,128]{2,1,0:T(8,128)(2,1)S(1)}, u32[]{:S(2)}) copy-start(bf16[16,128,128]{2,1,0:T(8,128)(2,1)S(1)} %collective-permute-done.other_ref) | copy-start | bytes 1572868

commit v4 on v3

--- a/solution.py
+++ b/solution.py
@@ -8,12 +8,12 @@
 VERY_NEGATIVE = -1e30
 CHUNK = 256
 PIECE = 256
-FINISH_STEPS = 4
 HALF = PIECE // 2
 KEYS = PIECE
 ASKED = 2 * PIECE
 GATES = ASKED + HALF
 VMEM_LIMIT = 24 << 20
+INSIDE_LIMIT = 48 << 20
 EXTRA = 128
 GATE_ROWS = 8
 F32 = jnp.float32
@@ -42,11 +42,19 @@
     return lax.broadcasted_iota(jnp.int32, shape, dim)
 
 
-def pack_kernel(q_ref, k_ref, v_ref, gate_ref, forget_ref, out_ref):
+def pack_kernel(q_in, k_in, v_in, gate_in, forget_in, out_ref, q_ref, k_ref, v_ref, gate_ref, forget_ref, sem):
     rows = k_ref.shape[0]
+    pairs = (gate_in, gate_ref), (forget_in, forget_ref), (v_in, v_ref), (k_in, k_ref), (q_in, q_ref)
+    copies = [pltpu.make_async_copy(a, b, sem.at[n]) for n, (a, b) in enumerate(pairs)]
+    for copy in copies:
+        copy.start()
+    copies[0].wait()
+    copies[1].wait()
     parts = []
     for x in (-jnp.log1p(jnp.exp(-forget_ref[...])), gate_ref[...]):
         parts += thirds(x, 1.0)
+    for copy in copies[2:]:
+        copy.wait()
     row = iota((GATE_ROWS, rows), 0)
     for h in range(k_ref.shape[1] // PIECE):
         area = jnp.zeros((GATE_ROWS, rows), F32)
@@ -228,14 +236,17 @@
     for h in range(PIECE // EXTRA):
         n = joined(*(z_ref[:, 2 * p + h, PIECE:] for p in range(3)))
         n = jnp.sum(column * n, axis=0, keepdims=True)
-        area = jnp.where(row == 3, own_top, jnp.where(row == 4, own_bound, 0.0))
+        area = jnp.where(row == 6, own_top, jnp.where(row == 7, own_bound, 0.0))
         for p, part in enumerate(thirds(n, 1.0)):
-            area = jnp.where(row == p, part, area)
+            area = jnp.where(row == 3 + p, part, area)
         nin_ref[:, h * EXTRA : (h + 1) * EXTRA] = area
 
 
-def inside_kernel(r_ref, other_ref, top_ref, low_ref, aux_ref, num_ref, row_ref):
+def inside_kernel(r_ref, other_ref, top_ref, low_ref, aux_ref, nin_ref, num_ref, row_ref):
     factor = PIECE**-0.5
+    before = nin_ref[...]
+    before_m = before[6:7, 0:1]
+    bound = before[7:8, 0:1]
     causal = iota((CHUNK, CHUNK), 0) <= iota((CHUNK, CHUNK), 1)
     row = iota((8, CHUNK), 0)
     for step in range(num_ref.shape[0]):
@@ -250,11 +261,19 @@
         top = jnp.maximum(carried, jnp.max(gap, axis=0, keepdims=True))
         weighted = jnp.exp(gap - top) * score
         outside = jnp.exp(carried - top)
-        normal = jnp.zeros((8, CHUNK), F32)
+        normal = jnp.where((row >= 3) & (row < 6), before, 0.0)
         for p, part in enumerate(thirds(aux[0:1], 1.0)):
             normal = jnp.where(row == p, part, normal)
-        reached = jnp.sum(dot(normal.astype(BF16), asked, (1, 0)), axis=0, keepdims=True)
-        den = jnp.sum(weighted, axis=0, keepdims=True) + outside * reached
+        reached = dot(normal.astype(BF16), asked, (1, 0))
+        den = jnp.sum(weighted, axis=0, keepdims=True)
+        den = factor * (den + outside * (reached[0:1] + reached[1:2] + reached[2:3]))
+        carried = cum + aux[2:3] + before_m
+        new_m = jnp.maximum(top, carried)
+        inside = jnp.exp(top - new_m)
+        ahead = jnp.exp(carried - new_m) * factor
+        den = den * inside + ahead * (reached[3:4] + reached[4:5] + reached[5:6])
+        over = 1.0 / jnp.maximum(jnp.abs(den), 1.0)
+        inside = inside * over * factor
         num = dot(
             jnp.concatenate([turned, turned], axis=1),
             jnp.concatenate(halves(weighted), axis=0),
@@ -265,47 +284,26 @@
             jnp.concatenate([asked, asked], axis=0),
             (1, 0),
         )
-        num_ref[step] = num + outside * read
-        row_ref[step] = jnp.where(row == 0, top, jnp.where(row == 1, den * factor, cum + aux[2:3]))
-
-
-def finish_kernel(own_ref, other_ref, num_ref, row_ref, c_ref, nin_ref, out_ref, both_ref):
-    factor = PIECE**-0.5
-    at = pl.program_id(0)
-
-    @pl.when(at == 0)
-    def _():
-        both_ref[...] = jnp.concatenate(halves(c_ref[...]), axis=1)
-
-    place = iota((8, PIECE), 0)
-    normal = jnp.where(place < 3, nin_ref[...], 0.0).astype(BF16)
-    before_m = nin_ref[3:4, 0:1]
-    bound = nin_ref[4:5, 0:1]
+        num_ref[step] = inside * num + (inside * outside) * read
+        row_ref[step] = jnp.broadcast_to(ahead * bound * over, (8, CHUNK))
+
+
+def finish_kernel(own_ref, other_ref, num_ref, row_ref, c_ref, out_ref, buffer_ref, sem):
+    both = jnp.concatenate(halves(c_ref[...]), axis=1)
+    copies = []
     for step in range(num_ref.shape[0]):
         blocks = chunk_blocks(own_ref, step)
         asked = jnp.concatenate(
             [beside(own_ref, blocks, 0, HALF), beside(other_ref, blocks, 0, HALF)], axis=0
         )
-        rows = row_ref[step]
-        m, den, cum = rows[0:1], rows[1:2], rows[2:3]
-        reached = jnp.sum(dot(normal, asked, (1, 0)), axis=0, keepdims=True)
-        carried = cum + before_m
-        new_m = jnp.maximum(m, carried)
-        inside = jnp.exp(m - new_m)
-        outside = jnp.exp(carried - new_m) * factor
-        den = den * inside + outside * reached
-        over = 1.0 / jnp.maximum(jnp.abs(den), 1.0)
-        read = dot(both_ref[...], jnp.concatenate([asked, asked], axis=0), (1, 0))
-        out = num_ref[step] * (inside * over * factor) + read * (outside * bound * over)
-        out_ref[step * CHUNK : (step + 1) * CHUNK, :] = out.astype(BF16).T
-
-
-def whole(shape):
-    return pl.BlockSpec(shape, lambda i: (0,) * len(shape))
-
-
-def stepped(shape, at=0):
-    return pl.BlockSpec(shape, lambda i: tuple(i if d == at else 0 for d in range(len(shape))))
+        read = dot(both, jnp.concatenate([asked, asked], axis=0), (1, 0))
+        out = num_ref[step] + read * row_ref[step, 0:1, :]
+        here = pl.ds(step * CHUNK, CHUNK)
+        buffer_ref[here, :] = out.astype(BF16).T
+        copies.append(pltpu.make_async_copy(buffer_ref.at[here], out_ref.at[here], sem.at[step]))
+        copies[-1].start()
+    for copy in copies:
+        copy.wait()
 
 
 def near(x):
@@ -329,12 +327,20 @@
 
     packed = pl.pallas_call(
         pack_kernel,
-        in_specs=[FAR] * 5,
+        in_specs=[pl.BlockSpec(memory_space=pltpu.HBM)] * 5,
         out_specs=NEAR,
         out_shape=pltpu.VMEM((pieces, tall, rows), BF16),
+        scratch_shapes=[
+            pltpu.VMEM(queries.shape, BF16),
+            pltpu.VMEM(keys.shape, BF16),
+            pltpu.VMEM(values.shape, BF16),
+            pltpu.VMEM((input_pre.shape[1], rows), F32),
+            pltpu.VMEM((input_pre.shape[1], rows), F32),
+            pltpu.SemaphoreType.DMA((5,)),
+        ],
         compiler_params=PARAMS,
         name="pack",
-    )(queries, keys, values, input_pre.T, forget_pre.T)
+    )(*(pltpu.with_memory_space_constraint(x, pltpu.HBM) for x in (queries, keys, values, input_pre.T, forget_pre.T)))
 
     received = lax.all_to_all(packed, "head", split_axis=0, concat_axis=0, tiled=True)
 
@@ -349,7 +355,8 @@
 
     spread = lax.all_to_all(summary.astype(F16), "seq", split_axis=0, concat_axis=0, tiled=True)
 
-    other = lax.ppermute(received[:, ASKED:GATES, :], "head", [(i, i ^ 1) for i in range(pieces)])
+    ours = received[:, ASKED:GATES, :]
+    other = lax.ppermute(ours, "head", [(i, i ^ 1) for i in range(pieces)])
 
     entry_top, entry_low, aux = pl.pallas_call(
         entries_kernel,
@@ -380,37 +387,28 @@
 
     num, line = pl.pallas_call(
         inside_kernel,
-        in_specs=[NEAR, NEAR, FAR, FAR, FAR],
-        out_specs=[FAR] * 2,
+        in_specs=[NEAR, NEAR, FAR, FAR, FAR, FAR],
+        out_specs=[NEAR] * 2,
         out_shape=[
-            jax.ShapeDtypeStruct((steps, PIECE, CHUNK), F32),
-            jax.ShapeDtypeStruct((steps, 8, CHUNK), F32),
+            pltpu.VMEM((steps, PIECE, CHUNK), F32),
+            pltpu.VMEM((steps, 8, CHUNK), F32),
         ],
+        compiler_params=pltpu.CompilerParams(vmem_limit_bytes=INSIDE_LIMIT),
         name="inside",
-    )(near(received), near(other), entry_top, entry_low, aux)
+    )(near(received), near(other), entry_top, entry_low, aux, normal)
 
     return pl.pallas_call(
         finish_kernel,
-        grid=(FINISH_STEPS,),
-        in_specs=[
-            pl.BlockSpec((pieces // FINISH_STEPS, HALF, rows), lambda i: (i, ASKED // HALF, 0)),
-            stepped((pieces // FINISH_STEPS, HALF, rows)),
-            stepped((steps // FINISH_STEPS, PIECE, CHUNK)),
-            stepped((steps // FINISH_STEPS, 8, CHUNK)),
-            NEAR,
-            whole((8, PIECE)),
-        ],
-        out_specs=stepped((tokens // FINISH_STEPS, PIECE)),
+        in_specs=[NEAR] * 5,
+        out_specs=pl.BlockSpec(memory_space=pltpu.HBM),
         out_shape=jax.ShapeDtypeStruct((tokens, PIECE), BF16),
-        scratch_shapes=[pltpu.VMEM((PIECE, 2 * PIECE), BF16)],
-        compiler_params=pltpu.CompilerParams(vmem_limit_bytes=60 << 20),
+        scratch_shapes=[pltpu.VMEM((tokens, PIECE), BF16), pltpu.SemaphoreType.DMA((steps,))],
+        compiler_params=PARAMS,
         name="finish",
-    )(received, other, num, line, near(back.reshape(PIECE, PIECE).astype(F32)), normal)
+    )(near(ours), near(other), num, line, near(back.reshape(PIECE, PIECE).astype(F32)))
 
 
 def solution(mesh):
     spec = P(("seq", "head"), None)
 
-    return jax.shard_map(
-        on_device, mesh=mesh, in_specs=(spec,) * 5, out_specs=P("seq", "head"), check_vma=False
-    )
+    return jax.shard_map(on_device, mesh=mesh, in_specs=(spec,) * 5, out_specs=P("seq", "head"), check_vma=False)

time: 113 us -> 109 us (0.965)
  local copies, waits for them, and re-layouts: 7.29 us -> 5.54 us
  Pallas kernels: 17 us -> 15.8 us
    all_to_all x1, waiting for transfers between devices: 5.25 us -> 3.74 us  [on_device(): lax.all_to_all(before.astype(F16), 'seq', split_axis=0, concat_axis=0, ti...]
    pallas_call x3, Pallas kernels: 10.6 us -> 9.47 us  [the longest x1 4.7 us: on_device(): pl.pallas_call(inside_kernel, in_specs=[NEAR, NEAR, FAR, FAR, FAR, FAR],...]
    unnamed x16 -> x12, local copies, waits for them, and re-layouts: 6.43 us -> 5.49 us
where the time goes in v4:
time: 109 us
  blocking collectives  39.5 us (36%)
  starting transfers between devices  26 us (24%)
  waiting for transfers between devices  20.3 us (19%)
  Pallas kernels  15.8 us (14%)
  local copies, waits for them, and re-layouts  5.54 us (5%)
  other arithmetic  1.42 us (1%)
    all_to_all x1, blocking collectives, on_device(): lax.all_to_all(packed, 'head', split_axis=0, concat_axis=0, tiled=True)  39.5 us
    all_to_all x1, starting transfers between devices, on_device(): lax.all_to_all(summary.astype(F16), 'seq', split_axis=0, concat_axis=0, t...  18.9 us
    all_to_all x1, waiting for transfers between devices, on_device(): lax.all_to_all(summary.astype(F16), 'seq', split_axis=0, concat_axis=0, t...  16.5 us
    unnamed x12, local copies, waits for them, and re-layouts  5.49 us
    all_to_all x1, starting transfers between devices, on_device(): lax.all_to_all(before.astype(F16), 'seq', split_axis=0, concat_axis=0, ti...  4.95 us
    pallas_call x1, Pallas kernels, on_device(): pl.pallas_call(inside_kernel, in_specs=[NEAR, NEAR, FAR, FAR, FAR, FAR],...  4.7 us
    pallas_call x1, Pallas kernels, on_device(): pl.pallas_call(entries_kernel, in_specs=[NEAR], out_specs=[FAR] * 3, out_...  3.82 us
    all_to_all x1, waiting for transfers between devices, on_device(): lax.all_to_all(before.astype(F16), 'seq', split_axis=0, concat_axis=0, ti...  3.74 us
  transfers between devices with their start and end apart: 3, of which 2 were waited for; matrix products, arithmetic and copies ran while one was open for 1% of the time, Pallas kernels for 9%

profile of v4, /device:TPU:1, one launch (start us, length us, event | category | flops | bytes accessed | tf_op | source)
XLA Modules:
  0.0 108.7 jit_solution(18093801191094693831)
XLA Ops:
  0.0 2.2 %pack.1 = bf16[16,648,128]{2,1,0:T(8,128)(2,1)S(1)} custom-call(bf16[128,2048]{1,0:T(8,128)(2,1)} %q_in.1, bf16[128,2048]{1,0:T(8,128)(2,1)} %k_in.1, bf16[128,4096]{1,0:T(8,128)(2,1)} %v_in.1, f32[8,128]{1,0:T(8,128)} %bitcast.6, f32[8,128]{1,0:T(8,128)} %bitcast.7), custom_call_target="tpu_custom_call" | custom-call | tf_op jit(solution)/shard_map/pack/pallas_call | solution.py:328
  2.2 39.5 %all_to_all.15.r_ref = bf16[16,648,128]{2,1,0:T(8,128)(2,1)S(1)} all-to-all(bf16[16,648,128]{2,1,0:T(8,128)(2,1)S(1)} %pack.1), channel_id=1, replica_groups=mesh['seq'=32,'head'=16] {'head'}, dimensions={0} | all-to-all | bytes 5308416 | tf_op jit(solution)/shard_map/all_to_all | solution.py:345
  41.7 0.0 copy-start
  41.7 1.2 %summary.1 = f32[32,8,384]{2,1,0:T(8,128)S(1)} custom-call(bf16[16,648,128]{2,1,0:T(8,128)(2,1)S(1)} %all_to_all.15.r_ref), custom_call_target="tpu_custom_call" | custom-call | tf_op jit(solution)/shard_map/summary/pallas_call | solution.py:347
  42.9 0.7 convert_element_type.14
  43.6 18.9 %all-to-all-start.1 = ((f16[32,8,384]{2,1,0:T(8,128)(2,1)}), f16[32,8,384]{2,1,0:T(8,128)(2,1)S(1)}, u32[]{:S(2)}, u32[]{:S(2)}) async-start(f16[32,8,384]{2,1,0:T(8,128)(2,1)} %convert_element_type.14), calls=%async_computation.1 | async-start | bytes 393216 | tf_op jit(solution)/shard_map/all_to_all | solution.py:356
  62.5 2.2 %collective-permute-start = (bf16[16,128,128]{2,1,0:T(8,128)(2,1)S(1)}, bf16[16,128,128]{2,1,0:T(8,128)(2,1)}, u32[]{:S(2)}, u32[]{:S(2)}) collective-permute-start(bf16[16,128,128]{2,1,0:T(8,128)(2,1)S(1)} %slice.4.own_ref), channel_id=1, source_target_pairs={{0,1},{1,0},{2,3},{3,2},{4,5},{5,4},{6,7},{7,6},{8,9},{9,8},{10,11... | collective-permute-start | bytes 1572872 | tf_op jit(solution)/shard_map/ppermute | solution.py:359
  64.7 16.5 %all-to-all-done.1 = f16[32,8,384]{2,1,0:T(8,128)(2,1)S(1)} async-done(((f16[32,8,384]{2,1,0:T(8,128)(2,1)}), f16[32,8,384]{2,1,0:T(8,128)(2,1)S(1)}, u32[]{:S(2)}, u32[]{:S(2)}) %all-to-all-start.1) | async-done | bytes 196640 | tf_op jit(solution)/shard_map/all_to_all | solution.py:356
  81.3 0.0 copy-done
  81.3 1.4 %prefix.1 = (f32[32,8,256]{2,1,0:T(8,128)S(1)}, f32[8,256]{1,0:T(8,128)}) custom-call(s32[1]{0:T(128)} %bitcast.2.own_ref, f32[32,8,384]{2,1,0:T(8,128)S(1)} %convert_element_type.15.z_ref), custom_call_target="tpu_custom_call" | custom-call | tf_op jit(solution)/shard_map/prefix/pallas_call | solution.py:374
  82.7 0.0 copy-start.5
  82.7 0.7 convert_element_type.16
  83.3 5.0 %all-to-all-start.2 = ((f16[32,8,256]{2,1,0:T(8,128)(2,1)}), f16[32,8,256]{2,1,0:T(8,128)(2,1)S(1)}, u32[]{:S(2)}, u32[]{:S(2)}) async-start(f16[32,8,256]{2,1,0:T(8,128)(2,1)} %convert_element_type.16), calls=%async_computation.2 | async-start | bytes 262144 | tf_op jit(solution)/shard_map/all_to_all | solution.py:386
  88.3 0.0 copy-start.1
  88.3 1.7 %copy-done.1 = bf16[16,648,128]{2,1,0:T(8,128)(2,1)S(1)} copy-done((bf16[16,648,128]{2,1,0:T(8,128)(2,1)S(1)}, bf16[16,648,128]{2,1,0:T(8,128)(2,1)}, u32[]{:S(2)}) %copy-start.1) | copy-done | bytes 2654232
  90.0 3.8 %entries.1 = (bf16[8,256,256]{2,1,0:T(8,128)(2,1)}, bf16[8,256,256]{2,1,0:T(8,128)(2,1)}, f32[8,8,256]{2,1,0:T(8,128)}) custom-call(bf16[16,648,128]{2,1,0:T(8,128)(2,1)S(1)} %copy-done.1), custom_call_target="tpu_custom_call" | custom-call | tf_op jit(solution)/shard_map/entries/pallas_call | solution.py:361
  93.9 0.0 collective-permute-done.other_ref
  93.9 0.0 copy-done.5
  93.9 0.0 copy-start.4
  93.9 0.8 copy-done.4
  94.7 4.7 %inside.1 = (f32[8,256,256]{2,1,0:T(8,128)S(1)}, f32[8,8,256]{2,1,0:T(8,128)S(1)}) custom-call(bf16[16,648,128]{2,1,0:T(8,128)(2,1)S(1)} %copy-done.1, bf16[16,128,128]{2,1,0:T(8,128)(2,1)} %collective-permute-done.other_ref, bf16[8,256,256]{2,1,0:T(8,128)(2,1)} %get-tuple-element.12.top_ref, bf16[8,256,256]{2,1,0:T(8,128)(2,1)} %get-tuple-element.13.low_ref, ...), custom_call_target="tpu_custom_call" | custom-call | tf_op jit(solution)/shard_map/inside/pallas_call | solution.py:388
  99.4 0.0 copy-start.2
  99.4 1.3 %copy-done.2 = f32[8,256,256]{2,1,0:T(8,128)} copy-done((f32[8,256,256]{2,1,0:T(8,128)}, f32[8,256,256]{2,1,0:T(8,128)S(1)}, u32[]{:S(2)}) %copy-start.2) | copy-done | bytes 2097176
  100.7 3.7 %all-to-all-done.2 = f16[32,8,256]{2,1,0:T(8,128)(2,1)S(1)} async-done(((f16[32,8,256]{2,1,0:T(8,128)(2,1)}), f16[32,8,256]{2,1,0:T(8,128)(2,1)S(1)}, u32[]{:S(2)}, u32[]{:S(2)}) %all-to-all-start.2) | async-done | bytes 131104 | tf_op jit(solution)/shard_map/all_to_all | solution.py:386
  104.5 0.0 copy-start.3
  104.5 1.6 %copy-done.3 = f32[8,256,256]{2,1,0:T(8,128)S(1)} copy-done((f32[8,256,256]{2,1,0:T(8,128)S(1)}, f32[8,256,256]{2,1,0:T(8,128)}, u32[]{:S(2)}) %copy-start.3) | copy-done | bytes 2097176
  106.1 2.6 %finish.1 = bf16[2048,256]{1,0:T(8,128)(2,1)} custom-call(bf16[16,128,128]{2,1,0:T(8,128)(2,1)S(1)} %slice.4.own_ref, bf16[16,128,128]{2,1,0:T(8,128)(2,1)} %collective-permute-done.other_ref, f32[8,256,256]{2,1,0:T(8,128)S(1)} %copy-done.3, f32[8,8,256]{2,1,0:T(8,128)S(1)} %get-tuple-element.17.row_ref, f32[256,256]{1,0:T(8,128)S(1)} %bitcast_convert_fusion.c_ref), custom_call_target="tpu_custom_call" | custom-call | tf_op jit(solution)/shard_map/finish/pallas_call | solution.py:400
  (3 shorter events, 0.1 us)
Async XLA Ops:
  41.7 39.6 %copy-start = (bf16[16,648,128]{2,1,0:T(8,128)(2,1)}, bf16[16,648,128]{2,1,0:T(8,128)(2,1)S(1)}, u32[]{:S(2)}) copy-start(bf16[16,648,128]{2,1,0:T(8,128)(2,1)S(1)} %all_to_all.15.r_ref) | copy-start | bytes 7962628
  43.6 37.6 %all-to-all-start.1 = ((f16[32,8,384]{2,1,0:T(8,128)(2,1)}), f16[32,8,384]{2,1,0:T(8,128)(2,1)S(1)}, u32[]{:S(2)}, u32[]{:S(2)}) async-start(f16[32,8,384]{2,1,0:T(8,128)(2,1)} %convert_element_type.14), calls=%async_computation.1 | async-start | bytes 393216 | tf_op jit(solution)/shard_map/all_to_all | solution.py:356
  62.5 31.3 %collective-permute-start = (bf16[16,128,128]{2,1,0:T(8,128)(2,1)S(1)}, bf16[16,128,128]{2,1,0:T(8,128)(2,1)}, u32[]{:S(2)}, u32[]{:S(2)}) collective-permute-start(bf16[16,128,128]{2,1,0:T(8,128)(2,1)S(1)} %slice.4.own_ref), channel_id=1, source_target_pairs={{0,1},{1,0},{2,3},{3,2},{4,5},{5,4},{6,7},{7,6},{8,9},{9,8},{10,11... | collective-permute-start | bytes 1572872 | tf_op jit(solution)/shard_map/ppermute | solution.py:359
  82.7 11.2 %copy-start.5 = (f32[8,256]{1,0:T(8,128)S(1)}, f32[8,256]{1,0:T(8,128)}, u32[]{:S(2)}) copy-start(f32[8,256]{1,0:T(8,128)} %get-tuple-element.15.nin_ref) | copy-start | bytes 24580
  83.3 21.2 %all-to-all-start.2 = ((f16[32,8,256]{2,1,0:T(8,128)(2,1)}), f16[32,8,256]{2,1,0:T(8,128)(2,1)S(1)}, u32[]{:S(2)}, u32[]{:S(2)}) async-start(f16[32,8,256]{2,1,0:T(8,128)(2,1)} %convert_element_type.16), calls=%async_computation.2 | async-start | bytes 262144 | tf_op jit(solution)/shard_map/all_to_all | solution.py:386
  88.3 1.8 %copy-start.1 = (bf16[16,648,128]{2,1,0:T(8,128)(2,1)S(1)}, bf16[16,648,128]{2,1,0:T(8,128)(2,1)}, u32[]{:S(2)}) copy-start(bf16[16,648,128]{2,1,0:T(8,128)(2,1)} %copy-done) | copy-start | bytes 7962628
  93.9 0.8 copy-start.4
  99.4 1.3 %copy-start.2 = (f32[8,256,256]{2,1,0:T(8,128)}, f32[8,256,256]{2,1,0:T(8,128)S(1)}, u32[]{:S(2)}) copy-start(f32[8,256,256]{2,1,0:T(8,128)S(1)} %get-tuple-element.16.num_ref) | copy-start | bytes 6291460
  104.5 1.6 %copy-start.3 = (f32[8,256,256]{2,1,0:T(8,128)S(1)}, f32[8,256,256]{2,1,0:T(8,128)}, u32[]{:S(2)}) copy-start(f32[8,256,256]{2,1,0:T(8,128)} %copy-done.2) | copy-start | bytes 6291460

commit v5 on v4

--- a/solution.py
+++ b/solution.py
@@ -13,7 +13,6 @@
 ASKED = 2 * PIECE
 GATES = ASKED + HALF
 VMEM_LIMIT = 24 << 20
-INSIDE_LIMIT = 48 << 20
 EXTRA = 128
 GATE_ROWS = 8
 F32 = jnp.float32
@@ -40,6 +39,10 @@
 
 def iota(shape, dim):
     return lax.broadcasted_iota(jnp.int32, shape, dim)
+
+
+def first_core():
+    return lax.rem(lax.axis_index("seq"), 2) == 0
 
 
 def pack_kernel(q_in, k_in, v_in, gate_in, forget_in, out_ref, q_ref, k_ref, v_ref, gate_ref, forget_ref, sem):
@@ -106,7 +109,7 @@
     )
 
 
-def summary_kernel(r_ref, z_ref):
+def summary_kernel(r_ref, mine_ref, send_ref):
     sources, rows = r_ref.shape[0], r_ref.shape[2]
     decay = [r_ref[:, GATES + p, :] for p in range(3)]
     gate = [r_ref[:, GATES + 3 + p, :].astype(F32) for p in range(3)]
@@ -132,6 +135,30 @@
     c_new = state[0:PIECE]
     n_new = state[PIECE : PIECE + 1] + state[PIECE + 1 : PIECE + 2]
 
+    place = iota((8, PIECE), 0)
+    rest = jnp.where(place == 0, n_new, jnp.where(place == 1, new_m, total))
+    first = first_core()
+    low, high = c_new[0:HALF], c_new[HALF:PIECE]
+    mine_ref[0:HALF, :] = jnp.where(first, low, high)
+    send_ref[0:HALF, :] = jnp.where(first, high, low)
+    mine_ref[HALF:, :] = rest
+    send_ref[HALF:, :] = rest
+
+
+def pair_kernel(mine_ref, theirs_ref, z_ref, first_ref):
+    first = first_core()
+    mine, theirs = mine_ref[...], theirs_ref[...]
+    early = jnp.where(first, mine, theirs)
+    late = jnp.where(first, theirs, mine)
+    first_ref[...] = early
+    late_f = late[HALF + 2 : HALF + 3, 0:1]
+    moved = early[HALF + 1 : HALF + 2, 0:1] + late_f
+    late_m = late[HALF + 1 : HALF + 2, 0:1]
+    new_m = jnp.maximum(moved, late_m)
+    joined = jnp.exp(moved - new_m) * early + jnp.exp(late_m - new_m) * late
+    c_new = joined[0:HALF]
+    n_new = joined[HALF : HALF + 1]
+    total = early[HALF + 2 : HALF + 3, 0:1] + late_f
     count, slab = z_ref.shape[0], z_ref.shape[1]
     most = jnp.max(jnp.max(jnp.abs(c_new), axis=1, keepdims=True), axis=0, keepdims=True)
     scaled = c_new * jnp.where(most > 0.0, 1.0 / most, 0.0)
@@ -185,9 +212,10 @@
             start = start + total
 
 
-def prefix_kernel(own_ref, z_ref, y_ref, nin_ref):
+def prefix_kernel(z_ref, first_ref, y_ref, nin_ref):
     count, slab, _ = z_ref.shape
-    own = own_ref[0]
+    own = lax.axis_index("seq") // 2
+    second = jnp.logical_not(first_core())
     small = 1.0 / 256.0
 
     def joined(a, b, c):
@@ -233,20 +261,36 @@
     row = iota((8, EXTRA), 0)
     own_top = jnp.sum(jnp.where(mine, top, 0.0), axis=1, keepdims=True)
     own_bound = jnp.sum(jnp.where(mine, bound, 0.0), axis=1, keepdims=True)
+    first_m = first_ref[HALF + 1 : HALF + 2, 0:1]
+    moved = own_top + first_ref[HALF + 2 : HALF + 3, 0:1]
+    next_top = jnp.maximum(moved, first_m)
+    old_share = jnp.exp(moved - next_top)
+    new_share = jnp.exp(first_m - next_top)
     for h in range(PIECE // EXTRA):
+        lanes = slice(h * EXTRA, (h + 1) * EXTRA)
         n = joined(*(z_ref[:, 2 * p + h, PIECE:] for p in range(3)))
         n = jnp.sum(column * n, axis=0, keepdims=True)
-        area = jnp.where(row == 6, own_top, jnp.where(row == 7, own_bound, 0.0))
+        n = jnp.where(second, old_share * n + new_share * first_ref[HALF : HALF + 1, lanes], n)
+        area = jnp.where(row == 6, jnp.where(second, next_top, own_top), own_bound)
+        for p, part in enumerate((old_share, new_share)):
+            area = jnp.where(row == p, part, area)
         for p, part in enumerate(thirds(n, 1.0)):
             area = jnp.where(row == 3 + p, part, area)
-        nin_ref[:, h * EXTRA : (h + 1) * EXTRA] = area
+        nin_ref[:, lanes] = area
+
+
+def mix_kernel(p_ref, first_ref, nin_ref, keep_ref, send_ref):
+    before = p_ref[...] * nin_ref[2:3, 0:1]
+    after = before * nin_ref[0:1, 0:1] + first_ref[0:HALF, :] * nin_ref[1:2, 0:1]
+    first = first_core()
+    keep_ref[...] = jnp.where(first, before, after)
+    send_ref[...] = jnp.where(first, after, before)
 
 
 def inside_kernel(r_ref, other_ref, top_ref, low_ref, aux_ref, nin_ref, num_ref, row_ref):
     factor = PIECE**-0.5
     before = nin_ref[...]
     before_m = before[6:7, 0:1]
-    bound = before[7:8, 0:1]
     causal = iota((CHUNK, CHUNK), 0) <= iota((CHUNK, CHUNK), 1)
     row = iota((8, CHUNK), 0)
     for step in range(num_ref.shape[0]):
@@ -285,13 +329,39 @@
             (1, 0),
         )
         num_ref[step] = inside * num + (inside * outside) * read
-        row_ref[step] = jnp.broadcast_to(ahead * bound * over, (8, CHUNK))
-
-
-def finish_kernel(own_ref, other_ref, num_ref, row_ref, c_ref, out_ref, buffer_ref, sem):
-    both = jnp.concatenate(halves(c_ref[...]), axis=1)
-    copies = []
-    for step in range(num_ref.shape[0]):
+        row_ref[step] = jnp.broadcast_to(ahead * over, (8, CHUNK))
+
+
+def finish_kernel(
+    own_in, other_in, num_in, row_in, keep_ref, came_ref, out_ref,
+    own_ref, other_ref, num_ref, row_ref, buffer_ref, in_sem, out_sem,
+):
+    steps = num_ref.shape[0]
+    group = own_ref.shape[0] // steps
+    row_copy = pltpu.make_async_copy(row_in, row_ref, in_sem.at[3 * steps])
+    row_copy.start()
+    arriving = []
+    for step in range(steps):
+        blocks = pl.ds(step * group, group)
+        pairs = (
+            (own_in.at[blocks], own_ref.at[blocks]),
+            (other_in.at[blocks], other_ref.at[blocks]),
+            (num_in.at[step], num_ref.at[step]),
+        )
+        arriving.append(
+            [pltpu.make_async_copy(a, b, in_sem.at[3 * step + n]) for n, (a, b) in enumerate(pairs)]
+        )
+        for copy in arriving[-1]:
+            copy.start()
+    first = first_core()
+    keep, came = keep_ref[...], came_ref[...]
+    state = jnp.concatenate([jnp.where(first, keep, came), jnp.where(first, came, keep)], axis=0)
+    both = jnp.concatenate(halves(state), axis=1)
+    row_copy.wait()
+    leaving = []
+    for step in range(steps):
+        for copy in arriving[step]:
+            copy.wait()
         blocks = chunk_blocks(own_ref, step)
         asked = jnp.concatenate(
             [beside(own_ref, blocks, 0, HALF), beside(other_ref, blocks, 0, HALF)], axis=0
@@ -300,10 +370,14 @@
         out = num_ref[step] + read * row_ref[step, 0:1, :]
         here = pl.ds(step * CHUNK, CHUNK)
         buffer_ref[here, :] = out.astype(BF16).T
-        copies.append(pltpu.make_async_copy(buffer_ref.at[here], out_ref.at[here], sem.at[step]))
-        copies[-1].start()
-    for copy in copies:
+        leaving.append(pltpu.make_async_copy(buffer_ref.at[here], out_ref.at[here], out_sem.at[step]))
+        leaving[-1].start()
+    for copy in leaving:
         copy.wait()
+
+
+def far(x):
+    return pltpu.with_memory_space_constraint(x, pltpu.HBM)
 
 
 def near(x):
@@ -322,7 +396,10 @@
     tokens = pieces * rows
     steps = tokens // CHUNK
     tall = GATES + GATE_ROWS
-    slab = PIECE // shards
+    chips = shards // 2
+    slab = HALF // chips
+    pairs = [(i, i ^ 1) for i in range(shards)]
+    columns = [[2 * z + c for z in range(chips)] for c in range(2)]
     wide = PIECE + EXTRA
 
     packed = pl.pallas_call(
@@ -340,20 +417,42 @@
         ],
         compiler_params=PARAMS,
         name="pack",
-    )(*(pltpu.with_memory_space_constraint(x, pltpu.HBM) for x in (queries, keys, values, input_pre.T, forget_pre.T)))
+    )(*(far(x) for x in (queries, keys, values, input_pre.T, forget_pre.T)))
 
     received = lax.all_to_all(packed, "head", split_axis=0, concat_axis=0, tiled=True)
 
-    summary = pl.pallas_call(
+    half = pltpu.VMEM((HALF + 8, PIECE), F32)
+    mine, send = pl.pallas_call(
         summary_kernel,
         in_specs=[NEAR],
-        out_specs=NEAR,
-        out_shape=pltpu.VMEM((shards, slab, wide), F32),
+        out_specs=[NEAR] * 2,
+        out_shape=[half] * 2,
         compiler_params=PARAMS,
         name="summary",
     )(near(received))
 
-    spread = lax.all_to_all(summary.astype(F16), "seq", split_axis=0, concat_axis=0, tiled=True)
+    theirs = lax.ppermute(send, "seq", pairs)
+
+    summary, first = pl.pallas_call(
+        pair_kernel,
+        in_specs=[NEAR, NEAR],
+        out_specs=[NEAR, FAR],
+        out_shape=[
+            pltpu.VMEM((chips, slab, wide), F32),
+            jax.ShapeDtypeStruct((HALF + 8, PIECE), F32),
+        ],
+        compiler_params=PARAMS,
+        name="pair",
+    )(mine, near(theirs))
+
+    spread = lax.all_to_all(
+        summary.astype(F16),
+        "seq",
+        split_axis=0,
+        concat_axis=0,
+        tiled=True,
+        axis_index_groups=columns,
+    )
 
     ours = received[:, ASKED:GATES, :]
     other = lax.ppermute(ours, "head", [(i, i ^ 1) for i in range(pieces)])
@@ -370,42 +469,58 @@
         name="entries",
     )(near(received))
 
-    own = lax.axis_index("seq").astype(jnp.int32).reshape(1)
     before, normal = pl.pallas_call(
         prefix_kernel,
-        in_specs=[pl.BlockSpec(memory_space=pltpu.SMEM), NEAR],
+        in_specs=[NEAR, NEAR],
         out_specs=[NEAR, FAR],
         out_shape=[
-            pltpu.VMEM((shards, slab, PIECE), F32),
+            pltpu.VMEM((chips, slab, PIECE), F32),
             jax.ShapeDtypeStruct((8, PIECE), F32),
         ],
         compiler_params=pltpu.CompilerParams(vmem_limit_bytes=60 << 20),
         name="prefix",
-    )(own, near(spread.astype(F32)))
-
-    back = lax.all_to_all(before.astype(F16), "seq", split_axis=0, concat_axis=0, tiled=True)
+    )(near(spread.astype(F32)), near(first))
+
+    back = lax.all_to_all(before.astype(F16), "seq", split_axis=0, concat_axis=0, tiled=True, axis_index_groups=columns)
+
+    keep, lend = pl.pallas_call(
+        mix_kernel,
+        in_specs=[NEAR] * 3,
+        out_specs=[NEAR] * 2,
+        out_shape=[pltpu.VMEM((HALF, PIECE), F32)] * 2,
+        compiler_params=PARAMS,
+        name="mix",
+    )(near(back.reshape(HALF, PIECE).astype(F32)), near(first), near(normal))
+    came = lax.ppermute(lend, "seq", pairs)
 
     num, line = pl.pallas_call(
         inside_kernel,
         in_specs=[NEAR, NEAR, FAR, FAR, FAR, FAR],
-        out_specs=[NEAR] * 2,
+        out_specs=[FAR] * 2,
         out_shape=[
-            pltpu.VMEM((steps, PIECE, CHUNK), F32),
-            pltpu.VMEM((steps, 8, CHUNK), F32),
-        ],
-        compiler_params=pltpu.CompilerParams(vmem_limit_bytes=INSIDE_LIMIT),
+            jax.ShapeDtypeStruct((steps, PIECE, CHUNK), F32),
+            jax.ShapeDtypeStruct((steps, 8, CHUNK), F32),
+        ],
         name="inside",
     )(near(received), near(other), entry_top, entry_low, aux, normal)
 
     return pl.pallas_call(
         finish_kernel,
-        in_specs=[NEAR] * 5,
+        in_specs=[pl.BlockSpec(memory_space=pltpu.HBM)] * 4 + [NEAR] * 2,
         out_specs=pl.BlockSpec(memory_space=pltpu.HBM),
         out_shape=jax.ShapeDtypeStruct((tokens, PIECE), BF16),
-        scratch_shapes=[pltpu.VMEM((tokens, PIECE), BF16), pltpu.SemaphoreType.DMA((steps,))],
+        scratch_shapes=[
+            pltpu.VMEM(ours.shape, BF16),
+            pltpu.VMEM(ours.shape, BF16),
+            pltpu.VMEM(num.shape, F32),
+            pltpu.VMEM(line.shape, F32),
+            pltpu.VMEM((tokens, PIECE), BF16),
+            pltpu.SemaphoreType.DMA((3 * steps + 1,)),
+            pltpu.SemaphoreType.DMA((steps,)),
+        ],
         compiler_params=PARAMS,
         name="finish",
-    )(near(ours), near(other), num, line, near(back.reshape(PIECE, PIECE).astype(F32)))
+    )(far(ours), far(other), far(num), far(line), keep, near(came))
 
 
 def solution(mesh):

time: 109 us -> 115 us (1.055)
  blocking collectives: 39.5 us -> 66.5 us
  waiting for transfers between devices: 20.3 us -> 9.52 us
  starting transfers between devices: 26 us -> 16.6 us
  Pallas kernels: 15.8 us -> 20 us
  local copies, waits for them, and re-layouts: 5.54 us -> 1.56 us
    all_to_all x0 -> x1, blocking collectives: none -> 27 us  [on_device(): lax.all_to_all(summary.astype(F16), 'seq', split_axis=0, concat_axis=0, t...]
    all_to_all x1 -> x0, starting transfers between devices: 18.9 us -> none  [on_device(): lax.all_to_all(summary.astype(F16), 'seq', split_axis=0, concat_axis=0, t...]
    all_to_all x1 -> x0, waiting for transfers between devices: 16.5 us -> none  [on_device(): lax.all_to_all(summary.astype(F16), 'seq', split_axis=0, concat_axis=0, t...]
    ppermute x0 -> x2, starting transfers between devices: none -> 9.36 us  [the longest x1 5.16 us: on_device(): theirs = lax.ppermute(send, 'seq', pairs)]
    unnamed x12 -> x4, local copies, waits for them, and re-layouts: 5.49 us -> 0.69 us
    all_to_all x1, waiting for transfers between devices: 3.74 us -> 8.54 us  [on_device(): lax.all_to_all(before.astype(F16), 'seq', split_axis=0, concat_axis=0, ti...]
    pallas_call x3 -> x5, Pallas kernels: 5.09 us -> 7.86 us  [the longest x1 4.77 us: on_device(): pl.pallas_call(finish_kernel, in_specs=[pl.BlockSpec(memory_space=pltpu.H...]
    pallas_call x1, Pallas kernels: 4.7 us -> 6.1 us  [on_device(): pl.pallas_call(inside_kernel, in_specs=[NEAR, NEAR, FAR, FAR, FAR, FAR],...]
  transfers between devices with their start and end apart: 3 -> 4, of which waited for: 2 -> 2; matrix products, arithmetic and copies ran while one was open for 1% -> 1% of each run, Pallas kernels for 9% -> 9%
where the time goes in v5:
time: 115 us
  blocking collectives  66.5 us (58%)
  Pallas kernels  20 us (17%)
  starting transfers between devices  16.6 us (14%)
  waiting for transfers between devices  9.52 us (8%)
  local copies, waits for them, and re-layouts  1.56 us (1%)
    all_to_all x1, blocking collectives, on_device(): lax.all_to_all(packed, 'head', split_axis=0, concat_axis=0, tiled=True)  39.5 us
    all_to_all x1, blocking collectives, on_device(): lax.all_to_all(summary.astype(F16), 'seq', split_axis=0, concat_axis=0, t...  27 us
    all_to_all x1, waiting for transfers between devices, on_device(): lax.all_to_all(before.astype(F16), 'seq', split_axis=0, concat_axis=0, ti...  8.54 us
    pallas_call x1, Pallas kernels, on_device(): pl.pallas_call(inside_kernel, in_specs=[NEAR, NEAR, FAR, FAR, FAR, FAR],...  6.1 us
    ppermute x1, starting transfers between devices, on_device(): theirs = lax.ppermute(send, 'seq', pairs)  5.16 us
    all_to_all x1, starting transfers between devices, on_device(): lax.all_to_all(before.astype(F16), 'seq', split_axis=0, concat_axis=0, ti...  5.03 us
    pallas_call x1, Pallas kernels, on_device(): pl.pallas_call(finish_kernel, in_specs=[pl.BlockSpec(memory_space=pltpu.H...  4.77 us
    ppermute x1, starting transfers between devices, on_device(): came = lax.ppermute(lend, 'seq', pairs)  4.2 us
  transfers between devices with their start and end apart: 4, of which 2 were waited for; matrix products, arithmetic and copies ran while one was open for 1% of the time, Pallas kernels for 9%

profile of v5, /device:TPU:1, one launch (start us, length us, event | category | flops | bytes accessed | tf_op | source)
XLA Modules:
  0.0 114.9 jit_solution(1589583729278696633)
XLA Ops:
  0.0 2.2 %pack.1 = bf16[16,648,128]{2,1,0:T(8,128)(2,1)S(1)} custom-call(bf16[128,2048]{1,0:T(8,128)(2,1)} %q_in.1, bf16[128,2048]{1,0:T(8,128)(2,1)} %k_in.1, bf16[128,4096]{1,0:T(8,128)(2,1)} %v_in.1, f32[8,128]{1,0:T(8,128)} %bitcast.5, f32[8,128]{1,0:T(8,128)} %bitcast.6), custom_call_target="tpu_custom_call" | custom-call | tf_op jit(solution)/shard_map/pack/pallas_call | solution.py:405
  2.2 39.5 %all_to_all.15.r_ref = bf16[16,648,128]{2,1,0:T(8,128)(2,1)S(1)} all-to-all(bf16[16,648,128]{2,1,0:T(8,128)(2,1)S(1)} %pack.1), channel_id=1, replica_groups=mesh['seq'=32,'head'=16] {'head'}, dimensions={0} | all-to-all | bytes 5308416 | tf_op jit(solution)/shard_map/all_to_all | solution.py:422
  41.7 1.1 summary.1
  42.8 5.2 %collective-permute-start.1 = (f32[136,256]{1,0:T(8,128)S(1)}, f32[136,256]{1,0:T(8,128)S(1)}, u32[]{:S(2)}, u32[]{:S(2)}) collective-permute-start(f32[136,256]{1,0:T(8,128)S(1)} %get-tuple-element.22), channel_id=1, source_target_pairs={{0,16},{16,0},{32,48},{48,32},{64,80},{80,64},{96,112},{112,96},{1... | collective-permute-start | bytes 417800 | tf_op jit(solution)/shard_map/ppermute | solution.py:434
  48.0 1.0 collective-permute-done.1.theirs_ref
  48.9 0.2 pair.1
  49.2 27.0 %all_to_all.16 = f16[16,8,384]{2,1,0:T(8,128)(2,1)S(1)} all-to-all(f16[16,8,384]{2,1,0:T(8,128)(2,1)S(1)} %convert_element_type.14), channel_id=1, replica_groups={{0,32,64,96,128,160,192,224,256,288,320,352,384,416,448,480},{16,48,80,..., dimensions={0} | all-to-all | bytes 196608 | tf_op jit(solution)/shard_map/all_to_all | solution.py:448
  76.1 1.1 prefix.1
  77.2 0.6 convert_element_type.16
  77.9 5.0 %all-to-all-start.2 = ((f16[16,8,256]{2,1,0:T(8,128)(2,1)}), f16[16,8,256]{2,1,0:T(8,128)(2,1)S(1)}, u32[]{:S(2)}, u32[]{:S(2)}) async-start(f16[16,8,256]{2,1,0:T(8,128)(2,1)} %convert_element_type.16), calls=%async_computation.2 | async-start | bytes 131072 | tf_op jit(solution)/shard_map/all_to_all | solution.py:484
  82.9 0.9 slice.4.own_in
  83.8 2.2 %collective-permute-start = (bf16[16,128,128]{2,1,0:T(8,128)(2,1)}, bf16[16,128,128]{2,1,0:T(8,128)(2,1)S(1)}, u32[]{:S(2)}, u32[]{:S(2)}) collective-permute-start(bf16[16,128,128]{2,1,0:T(8,128)(2,1)} %slice.4.own_in), channel_id=1, source_target_pairs={{0,1},{1,0},{2,3},{3,2},{4,5},{5,4},{6,7},{7,6},{8,9},{9,8},{10,11... | collective-permute-start | bytes 1572872 | tf_op jit(solution)/shard_map/ppermute | solution.py:458
  86.0 8.5 %all-to-all-done.2 = f16[16,8,256]{2,1,0:T(8,128)(2,1)S(1)} async-done(((f16[16,8,256]{2,1,0:T(8,128)(2,1)}), f16[16,8,256]{2,1,0:T(8,128)(2,1)S(1)}, u32[]{:S(2)}, u32[]{:S(2)}) %all-to-all-start.2) | async-done | bytes 65568 | tf_op jit(solution)/shard_map/all_to_all | solution.py:484
  94.5 0.0 copy-start.1
  94.5 0.7 copy-done.1
  95.2 0.8 mix.1
  96.0 4.2 %collective-permute-start.2 = (f32[128,256]{1,0:T(8,128)}, f32[128,256]{1,0:T(8,128)S(1)}, u32[]{:S(2)}, u32[]{:S(2)}) collective-permute-start(f32[128,256]{1,0:T(8,128)} %get-tuple-element.30), channel_id=1, source_target_pairs={{0,16},{16,0},{32,48},{48,32},{64,80},{80,64},{96,112},{112,96},{1... | collective-permute-start | bytes 393224 | tf_op jit(solution)/shard_map/ppermute | solution.py:494
  100.2 3.8 %entries.1 = (bf16[8,256,256]{2,1,0:T(8,128)(2,1)}, bf16[8,256,256]{2,1,0:T(8,128)(2,1)}, f32[8,8,256]{2,1,0:T(8,128)}) custom-call(bf16[16,648,128]{2,1,0:T(8,128)(2,1)S(1)} %all_to_all.15.r_ref), custom_call_target="tpu_custom_call" | custom-call | tf_op jit(solution)/shard_map/entries/pallas_call | solution.py:460
  104.0 0.0 collective-permute-done.other_ref.other_in
  104.0 0.0 copy-start
  104.0 6.1 %inside.1 = (f32[8,256,256]{2,1,0:T(8,128)}, f32[8,8,256]{2,1,0:T(8,128)}) custom-call(bf16[16,648,128]{2,1,0:T(8,128)(2,1)S(1)} %all_to_all.15.r_ref, bf16[16,128,128]{2,1,0:T(8,128)(2,1)S(1)} %collective-permute-done.other_ref.other_in, bf16[8,256,256]{2,1,0:T(8,128)(2,1)} %get-tuple-element.18.top_ref, bf16[8,256,256]{2,1,0:T(8,128)(2,1)} %get-tuple-element.19.low_ref, ...), custom_call_target="tpu_custom_call" | custom-call | tf_op jit(solution)/shard_map/inside/pallas_call | solution.py:496
  110.1 0.0 copy-done
  110.1 0.0 collective-permute-done.2.came_ref
  110.1 4.8 %finish.1 = bf16[2048,256]{1,0:T(8,128)(2,1)} custom-call(bf16[16,128,128]{2,1,0:T(8,128)(2,1)} %slice.4.own_in, bf16[16,128,128]{2,1,0:T(8,128)(2,1)} %copy-done, f32[8,256,256]{2,1,0:T(8,128)} %get-tuple-element.26.num_in, f32[8,8,256]{2,1,0:T(8,128)} %get-tuple-element.27.row_in, f32[128,256]{1,0:T(8,128)S(1)} %get-tuple-element.29.keep_ref, ...), custom_call_target="tpu_custom_call" | custom-call | tf_op jit(solution)/shard_map/finish/pallas_call | solution.py:507
  (3 shorter events, 0.0 us)
Async XLA Ops:
  42.8 6.1 %collective-permute-start.1 = (f32[136,256]{1,0:T(8,128)S(1)}, f32[136,256]{1,0:T(8,128)S(1)}, u32[]{:S(2)}, u32[]{:S(2)}) collective-permute-start(f32[136,256]{1,0:T(8,128)S(1)} %get-tuple-element.22), channel_id=1, source_target_pairs={{0,16},{16,0},{32,48},{48,32},{64,80},{80,64},{96,112},{112,96},{1... | collective-permute-start | bytes 417800 | tf_op jit(solution)/shard_map/ppermute | solution.py:434
  77.9 16.6 %all-to-all-start.2 = ((f16[16,8,256]{2,1,0:T(8,128)(2,1)}), f16[16,8,256]{2,1,0:T(8,128)(2,1)S(1)}, u32[]{:S(2)}, u32[]{:S(2)}) async-start(f16[16,8,256]{2,1,0:T(8,128)(2,1)} %convert_element_type.16), calls=%async_computation.2 | async-start | bytes 131072 | tf_op jit(solution)/shard_map/all_to_all | solution.py:484
  83.8 20.2 %collective-permute-start = (bf16[16,128,128]{2,1,0:T(8,128)(2,1)}, bf16[16,128,128]{2,1,0:T(8,128)(2,1)S(1)}, u32[]{:S(2)}, u32[]{:S(2)}) collective-permute-start(bf16[16,128,128]{2,1,0:T(8,128)(2,1)} %slice.4.own_in), channel_id=1, source_target_pairs={{0,1},{1,0},{2,3},{3,2},{4,5},{5,4},{6,7},{7,6},{8,9},{9,8},{10,11... | collective-permute-start | bytes 1572872 | tf_op jit(solution)/shard_map/ppermute | solution.py:458
  94.5 0.7 copy-start.1
  96.0 14.1 %collective-permute-start.2 = (f32[128,256]{1,0:T(8,128)}, f32[128,256]{1,0:T(8,128)S(1)}, u32[]{:S(2)}, u32[]{:S(2)}) collective-permute-start(f32[128,256]{1,0:T(8,128)} %get-tuple-element.30), channel_id=1, source_target_pairs={{0,16},{16,0},{32,48},{48,32},{64,80},{80,64},{96,112},{112,96},{1... | collective-permute-start | bytes 393224 | tf_op jit(solution)/shard_map/ppermute | solution.py:494
  104.0 6.1 %copy-start = (bf16[16,128,128]{2,1,0:T(8,128)(2,1)}, bf16[16,128,128]{2,1,0:T(8,128)(2,1)S(1)}, u32[]{:S(2)}) copy-start(bf16[16,128,128]{2,1,0:T(8,128)(2,1)S(1)} %collective-permute-done.other_ref.other_in) | copy-start | bytes 1572868

commit v6 on v5

--- a/solution.py
+++ b/solution.py
@@ -13,11 +13,12 @@
 ASKED = 2 * PIECE
 GATES = ASKED + HALF
 VMEM_LIMIT = 24 << 20
-EXTRA = 128
+INSIDE_LIMIT = 56 << 20
+FAR_LIMIT = 59 << 20
+NEAR_CHIPS = 4
 GATE_ROWS = 8
 F32 = jnp.float32
 BF16 = jnp.bfloat16
-F16 = jnp.float16
 
 
 def dot(a, b, contract):
@@ -145,34 +146,28 @@
     send_ref[HALF:, :] = rest
 
 
+def scalar(rows, n):
+    return rows[n : n + 1, 0:1]
+
+
 def pair_kernel(mine_ref, theirs_ref, z_ref, first_ref):
     first = first_core()
     mine, theirs = mine_ref[...], theirs_ref[...]
     early = jnp.where(first, mine, theirs)
     late = jnp.where(first, theirs, mine)
     first_ref[...] = early
-    late_f = late[HALF + 2 : HALF + 3, 0:1]
-    moved = early[HALF + 1 : HALF + 2, 0:1] + late_f
-    late_m = late[HALF + 1 : HALF + 2, 0:1]
+    late_f = scalar(late, HALF + 2)
+    moved = scalar(early, HALF + 1) + late_f
+    late_m = scalar(late, HALF + 1)
     new_m = jnp.maximum(moved, late_m)
     joined = jnp.exp(moved - new_m) * early + jnp.exp(late_m - new_m) * late
-    c_new = joined[0:HALF]
-    n_new = joined[HALF : HALF + 1]
-    total = early[HALF + 2 : HALF + 3, 0:1] + late_f
-    count, slab = z_ref.shape[0], z_ref.shape[1]
-    most = jnp.max(jnp.max(jnp.abs(c_new), axis=1, keepdims=True), axis=0, keepdims=True)
-    scaled = c_new * jnp.where(most > 0.0, 1.0 / most, 0.0)
-    z_ref[:, :, 0:PIECE] = scaled.reshape(count, slab, PIECE)
-    place = iota((slab, EXTRA), 0)
-    lane = iota((slab, EXTRA), 1)
-    extra = jnp.zeros((slab, EXTRA), F32)
-    for p, part in enumerate(thirds(n_new, 256.0)):
-        for h in range(PIECE // EXTRA):
-            extra = jnp.where(place == 2 * p + h, part[:, h * EXTRA : (h + 1) * EXTRA], extra)
-    for n, x in enumerate((new_m, total, most * 0.25)):
-        for p, part in enumerate(thirds(x, 256.0)):
-            extra = jnp.where((place == 6) & (lane == 3 * n + p), part, extra)
-    z_ref[:, :, PIECE:] = jnp.broadcast_to(extra[None], (count, slab, EXTRA))
+    count, slab = z_ref.shape[0], z_ref.shape[1] - 8
+    place = iota((8, PIECE), 0)
+    rest = jnp.where(place == 1, new_m, scalar(early, HALF + 2) + late_f)
+    rest = jnp.where(place == 0, joined[HALF : HALF + 1], rest)
+    for i in range(count):
+        z_ref[i, 0:slab, :] = joined[i * slab : (i + 1) * slab]
+        z_ref[i, slab:, :] = rest
 
 
 def entries_kernel(r_ref, top_ref, low_ref, aux_ref):
@@ -212,75 +207,74 @@
             start = start + total
 
 
-def prefix_kernel(z_ref, first_ref, y_ref, nin_ref):
-    count, slab, _ = z_ref.shape
-    own = lax.axis_index("seq") // 2
+def near_kernel(z_ref, sum_ref, y_ref, meta_ref):
+    count, slab = z_ref.shape[0], z_ref.shape[1] - 8
+    state = jnp.zeros((slab, PIECE), F32)
+    normal = jnp.zeros((1, PIECE), F32)
+    old_m = jnp.full((1, 1), VERY_NEGATIVE, F32)
+    total = jnp.zeros((1, 1), F32)
+    for i in range(count):
+        y_ref[i] = state
+        for n, x in enumerate((old_m, total, normal)):
+            meta_ref[n * count + i : n * count + i + 1, :] = jnp.broadcast_to(x, (1, PIECE))
+        rest = z_ref[i, slab:, :]
+        m, f = scalar(rest, 1), scalar(rest, 2)
+        new_m = jnp.maximum(old_m + f, m)
+        keep, take = jnp.exp(old_m + f - new_m), jnp.exp(m - new_m)
+        state = keep * state + take * z_ref[i, 0:slab, :]
+        normal = keep * normal + take * rest[0:1]
+        old_m = new_m
+        total = total + f
+    place = iota((8, PIECE), 0)
+    sum_ref[0:slab, :] = state
+    sum_ref[slab:, :] = jnp.where(place == 0, normal, jnp.where(place == 1, old_m, total))
+
+
+def far_kernel(*refs):
+    y_ref, meta_ref, first_ref, *ahead, out_ref, nin_ref = refs
+    count, slab = y_ref.shape[0], y_ref.shape[1]
+    chip = lax.axis_index("seq") // 2
+    near_at, group = lax.rem(chip, count), chip // count
     second = jnp.logical_not(first_core())
-    small = 1.0 / 256.0
-
-    def joined(a, b, c):
-        return a + (b + c * small) * small
-
-    scalars = z_ref[:, 6, PIECE:]
-    columns = [scalars[:, p : p + 1] for p in range(9)]
-    m = joined(*columns[0:3])
-    most = joined(*columns[6:9]) * 4.0
-    shard = iota((count, EXTRA), 0)
-    later = iota((count, EXTRA), 1)
-    before = shard < later
-    after = (iota((count, count), 1) > iota((count, count), 0)).astype(BF16)
-    gap = joined(
-        *(dot(after, jnp.where(before, c, 0.0).astype(BF16), (1, 0)) for c in columns[3:6])
-    )
-    reach = jnp.where(before, m + gap, VERY_NEGATIVE)
-    top = jnp.max(reach, axis=0, keepdims=True)
-    weight = jnp.where(before, jnp.exp(reach - top), 0.0)
-    heavy = weight * most
-    bound = jnp.sum(heavy, axis=0, keepdims=True)
-    heavy = heavy * jnp.where(bound > 0.0, 1.0 / bound, 0.0)
-    size = count * slab
-    shift = slab.bit_length() - 1
-    down = (iota((size, count), 0) >> shift == iota((size, count), 1)).astype(BF16)
-    right = (iota((count, size), 0) == iota((count, size), 1) >> shift).astype(BF16)
-    same = (iota((size, size), 0) & (slab - 1)) == (iota((size, size), 1) & (slab - 1))
-    turned = heavy.T[0:count, :]
-    wide = []
-    for x in halves(turned):
-        x = dot(dot(down, x, (1, 0)).astype(BF16), right, (1, 0))
-        wide.append(jnp.where(same, x, 0.0).astype(BF16))
-    x_top, x_low = halves(z_ref[:, :, 0:PIECE].reshape(size, PIECE))
-    y = dot(
-        jnp.concatenate([wide[0], wide[1], wide[0]], axis=1),
-        jnp.concatenate([x_top, x_top, x_low], axis=0),
-        (1, 0),
-    )
-    y_ref[...] = y.reshape(count, slab, PIECE)
-
-    mine = iota((1, EXTRA), 1) == own
-    column = jnp.sum(jnp.where(mine, weight, 0.0), axis=1, keepdims=True)
-    row = iota((8, EXTRA), 0)
-    own_top = jnp.sum(jnp.where(mine, top, 0.0), axis=1, keepdims=True)
-    own_bound = jnp.sum(jnp.where(mine, bound, 0.0), axis=1, keepdims=True)
-    first_m = first_ref[HALF + 1 : HALF + 2, 0:1]
-    moved = own_top + first_ref[HALF + 2 : HALF + 3, 0:1]
-    next_top = jnp.maximum(moved, first_m)
-    old_share = jnp.exp(moved - next_top)
-    new_share = jnp.exp(first_m - next_top)
-    for h in range(PIECE // EXTRA):
-        lanes = slice(h * EXTRA, (h + 1) * EXTRA)
-        n = joined(*(z_ref[:, 2 * p + h, PIECE:] for p in range(3)))
-        n = jnp.sum(column * n, axis=0, keepdims=True)
-        n = jnp.where(second, old_share * n + new_share * first_ref[HALF : HALF + 1, lanes], n)
-        area = jnp.where(row == 6, jnp.where(second, next_top, own_top), own_bound)
-        for p, part in enumerate((old_share, new_share)):
-            area = jnp.where(row == p, part, area)
-        for p, part in enumerate(thirds(n, 1.0)):
-            area = jnp.where(row == 3 + p, part, area)
-        nin_ref[:, lanes] = area
+    state = jnp.zeros((slab, PIECE), F32)
+    normal = jnp.zeros((1, PIECE), F32)
+    old_m = jnp.full((1, 1), VERY_NEGATIVE, F32)
+    for d in range(len(ahead), 0, -1):
+        there = group >= d
+        rest = ahead[d - 1][slab:, :]
+        m = jnp.where(there, scalar(rest, 1), VERY_NEGATIVE)
+        f = jnp.where(there, scalar(rest, 2), 0.0)
+        new_m = jnp.maximum(old_m + f, m)
+        keep, take = jnp.exp(old_m + f - new_m), jnp.exp(m - new_m)
+        state = keep * state + take * ahead[d - 1][0:slab, :]
+        normal = keep * normal + take * rest[0:1]
+        old_m = new_m
+    meta = meta_ref[...]
+    own_m = jnp.full((1, 1), VERY_NEGATIVE, F32)
+    own_n = jnp.zeros((1, PIECE), F32)
+    for i in range(count):
+        m, f = scalar(meta, i), scalar(meta, count + i)
+        new_m = jnp.maximum(old_m + f, m)
+        keep, take = jnp.exp(old_m + f - new_m), jnp.exp(m - new_m)
+        out_ref[i] = keep * state + take * y_ref[i]
+        n = keep * normal + take * meta[2 * count + i : 2 * count + i + 1]
+        own_m = jnp.where(near_at == i, new_m, own_m)
+        own_n = jnp.where(near_at == i, n, own_n)
+    first_m = scalar(first_ref, HALF + 1)
+    moved = own_m + scalar(first_ref, HALF + 2)
+    next_m = jnp.maximum(moved, first_m)
+    old_share, new_share = jnp.exp(moved - next_m), jnp.exp(first_m - next_m)
+    next_n = old_share * own_n + new_share * first_ref[HALF : HALF + 1, :]
+    place = iota((8, PIECE), 0)
+    area = jnp.where(place == 0, old_share, new_share)
+    area = jnp.where(place == 6, jnp.where(second, next_m, own_m), area)
+    for p, part in enumerate(thirds(jnp.where(second, next_n, own_n), 1.0)):
+        area = jnp.where(place == 3 + p, part, area)
+    nin_ref[...] = area
 
 
 def mix_kernel(p_ref, first_ref, nin_ref, keep_ref, send_ref):
-    before = p_ref[...] * nin_ref[2:3, 0:1]
+    before = p_ref[...]
     after = before * nin_ref[0:1, 0:1] + first_ref[0:HALF, :] * nin_ref[1:2, 0:1]
     first = first_core()
     keep_ref[...] = jnp.where(first, before, after)
@@ -333,23 +327,20 @@
 
 
 def finish_kernel(
-    own_in, other_in, num_in, row_in, keep_ref, came_ref, out_ref,
-    own_ref, other_ref, num_ref, row_ref, buffer_ref, in_sem, out_sem,
+    own_in, other_in, num_ref, row_ref, keep_ref, came_ref, out_ref,
+    own_ref, other_ref, buffer_ref, in_sem, out_sem,
 ):
     steps = num_ref.shape[0]
     group = own_ref.shape[0] // steps
-    row_copy = pltpu.make_async_copy(row_in, row_ref, in_sem.at[3 * steps])
-    row_copy.start()
     arriving = []
     for step in range(steps):
         blocks = pl.ds(step * group, group)
         pairs = (
             (own_in.at[blocks], own_ref.at[blocks]),
             (other_in.at[blocks], other_ref.at[blocks]),
-            (num_in.at[step], num_ref.at[step]),
         )
         arriving.append(
-            [pltpu.make_async_copy(a, b, in_sem.at[3 * step + n]) for n, (a, b) in enumerate(pairs)]
+            [pltpu.make_async_copy(a, b, in_sem.at[2 * step + n]) for n, (a, b) in enumerate(pairs)]
         )
         for copy in arriving[-1]:
             copy.start()
@@ -357,7 +348,6 @@
     keep, came = keep_ref[...], came_ref[...]
     state = jnp.concatenate([jnp.where(first, keep, came), jnp.where(first, came, keep)], axis=0)
     both = jnp.concatenate(halves(state), axis=1)
-    row_copy.wait()
     leaving = []
     for step in range(steps):
         for copy in arriving[step]:
@@ -397,10 +387,12 @@
     steps = tokens // CHUNK
     tall = GATES + GATE_ROWS
     chips = shards // 2
-    slab = HALF // chips
+    close = NEAR_CHIPS
+    slab = HALF // close
     pairs = [(i, i ^ 1) for i in range(shards)]
-    columns = [[2 * z + c for z in range(chips)] for c in range(2)]
-    wide = PIECE + EXTRA
+    groups = [
+        [2 * (g + z) + c for z in range(close)] for g in range(0, chips, close) for c in range(2)
+    ]
 
     packed = pl.pallas_call(
         pack_kernel,
@@ -438,7 +430,7 @@
         in_specs=[NEAR, NEAR],
         out_specs=[NEAR, FAR],
         out_shape=[
-            pltpu.VMEM((chips, slab, wide), F32),
+            pltpu.VMEM((close, slab + 8, PIECE), F32),
             jax.ShapeDtypeStruct((HALF + 8, PIECE), F32),
         ],
         compiler_params=PARAMS,
@@ -446,12 +438,7 @@
     )(mine, near(theirs))
 
     spread = lax.all_to_all(
-        summary.astype(F16),
-        "seq",
-        split_axis=0,
-        concat_axis=0,
-        tiled=True,
-        axis_index_groups=columns,
+        summary, "seq", split_axis=0, concat_axis=0, tiled=True, axis_index_groups=groups
     )
 
     ours = received[:, ASKED:GATES, :]
@@ -469,19 +456,39 @@
         name="entries",
     )(near(received))
 
+    group_sum, local, meta = pl.pallas_call(
+        near_kernel,
+        in_specs=[NEAR],
+        out_specs=[NEAR, FAR, FAR],
+        out_shape=[
+            pltpu.VMEM((slab + 8, PIECE), F32),
+            jax.ShapeDtypeStruct((close, slab, PIECE), F32),
+            jax.ShapeDtypeStruct((16, PIECE), F32),
+        ],
+        compiler_params=pltpu.CompilerParams(vmem_limit_bytes=FAR_LIMIT),
+        name="near",
+    )(near(spread))
+
+    ahead = []
+    for d in range(1, chips // close):
+        step = 2 * close * d
+        ahead.append(lax.ppermute(group_sum, "seq", [(i, i + step) for i in range(shards - step)]))
+
     before, normal = pl.pallas_call(
-        prefix_kernel,
-        in_specs=[NEAR, NEAR],
-        out_specs=[NEAR, FAR],
+        far_kernel,
+        in_specs=[FAR, FAR] + [NEAR] * (1 + len(ahead)),
+        out_specs=[FAR] * 2,
         out_shape=[
-            pltpu.VMEM((chips, slab, PIECE), F32),
+            jax.ShapeDtypeStruct((close, slab, PIECE), F32),
             jax.ShapeDtypeStruct((8, PIECE), F32),
         ],
-        compiler_params=pltpu.CompilerParams(vmem_limit_bytes=60 << 20),
-        name="prefix",
-    )(near(spread.astype(F32)), near(first))
-
-    back = lax.all_to_all(before.astype(F16), "seq", split_axis=0, concat_axis=0, tiled=True, axis_index_groups=columns)
+        compiler_params=pltpu.CompilerParams(vmem_limit_bytes=FAR_LIMIT),
+        name="far",
+    )(local, meta, near(first), *(near(a) for a in ahead))
+
+    back = lax.all_to_all(
+        before, "seq", split_axis=0, concat_axis=0, tiled=True, axis_index_groups=groups
+    )
 
     keep, lend = pl.pallas_call(
         mix_kernel,
@@ -490,37 +497,36 @@
         out_shape=[pltpu.VMEM((HALF, PIECE), F32)] * 2,
         compiler_params=PARAMS,
         name="mix",
-    )(near(back.reshape(HALF, PIECE).astype(F32)), near(first), near(normal))
+    )(near(back.reshape(HALF, PIECE)), near(first), near(normal))
     came = lax.ppermute(lend, "seq", pairs)
 
     num, line = pl.pallas_call(
         inside_kernel,
-        in_specs=[NEAR, NEAR, FAR, FAR, FAR, FAR],
-        out_specs=[FAR] * 2,
+        in_specs=[FAR] * 6,
+        out_specs=[NEAR] * 2,
         out_shape=[
-            jax.ShapeDtypeStruct((steps, PIECE, CHUNK), F32),
-            jax.ShapeDtypeStruct((steps, 8, CHUNK), F32),
-        ],
+            pltpu.VMEM((steps, PIECE, CHUNK), F32),
+            pltpu.VMEM((steps, 8, CHUNK), F32),
+        ],
+        compiler_params=pltpu.CompilerParams(vmem_limit_bytes=INSIDE_LIMIT),
         name="inside",
-    )(near(received), near(other), entry_top, entry_low, aux, normal)
+    )(far(received), far(other), entry_top, entry_low, aux, normal)
 
     return pl.pallas_call(
         finish_kernel,
-        in_specs=[pl.BlockSpec(memory_space=pltpu.HBM)] * 4 + [NEAR] * 2,
+        in_specs=[pl.BlockSpec(memory_space=pltpu.HBM)] * 2 + [NEAR] * 4,
         out_specs=pl.BlockSpec(memory_space=pltpu.HBM),
         out_shape=jax.ShapeDtypeStruct((tokens, PIECE), BF16),
         scratch_shapes=[
             pltpu.VMEM(ours.shape, BF16),
             pltpu.VMEM(ours.shape, BF16),
-            pltpu.VMEM(num.shape, F32),
-            pltpu.VMEM(line.shape, F32),
             pltpu.VMEM((tokens, PIECE), BF16),
-            pltpu.SemaphoreType.DMA((3 * steps + 1,)),
+            pltpu.SemaphoreType.DMA((2 * steps,)),
             pltpu.SemaphoreType.DMA((steps,)),
         ],
         compiler_params=PARAMS,
         name="finish",
-    )(far(ours), far(other), far(num), far(line), keep, near(came))
+    )(far(ours), far(other), num, line, keep, near(came))
 
 
 def solution(mesh):

time: 115 us -> 115 us (level)
  starting transfers between devices: 16.6 us -> 30.8 us
  waiting for transfers between devices: 9.52 us -> 0.99 us
  blocking collectives: 66.5 us -> 59.5 us
  local copies, waits for them, and re-layouts: 1.56 us -> 3.3 us
    ppermute x0 -> x3, starting transfers between devices: none -> 18 us  [on_device(): lax.ppermute(group_sum, 'seq', [(i, i + step) for i in range(shards - ste...]
    all_to_all x1 -> x0, waiting for transfers between devices: 8.54 us -> none  [on_device(): lax.all_to_all(before.astype(F16), 'seq', split_axis=0, concat_axis=0, ti...]
    all_to_all x1 -> x2, blocking collectives: 27 us -> 19.9 us  [the longest x1 11.7 us: on_device(): lax.all_to_all(summary, 'seq', split_axis=0, concat_axis=0, tiled=True, a...]
    all_to_all x1 -> x0, starting transfers between devices: 5.03 us -> none  [on_device(): lax.all_to_all(before.astype(F16), 'seq', split_axis=0, concat_axis=0, ti...]
    unnamed x4 -> x6, local copies, waits for them, and re-layouts: 0.69 us -> 2.44 us
    ppermute x1, starting transfers between devices: 4.2 us -> 5.47 us  [on_device(): came = lax.ppermute(lend, 'seq', pairs)]
    pallas_call x2 -> x3, Pallas kernels: 7.19 us -> 7.88 us  [the longest x1 5.52 us: on_device(): pl.pallas_call(inside_kernel, in_specs=[FAR] * 6, out_specs=[NEAR] * 2, o...]
  transfers between devices with their start and end apart: 4 -> 6, of which waited for: 2 -> 1; matrix products, arithmetic and copies ran while one was open for 1% -> 1% of each run, Pallas kernels for 9% -> 10%
where the time goes in v6:
time: 115 us; the launch traced here: 114 us
  blocking collectives  59.5 us (52%)
  starting transfers between devices  30.8 us (27%)
  Pallas kernels  19.7 us (17%)
  local copies, waits for them, and re-layouts  3.3 us (3%)
    all_to_all x1, blocking collectives, on_device(): lax.all_to_all(packed, 'head', split_axis=0, concat_axis=0, tiled=True)  39.5 us
    ppermute x3, starting transfers between devices, on_device(): lax.ppermute(group_sum, 'seq', [(i, i + step) for i in range(shards - ste...  18 us
    all_to_all x1, blocking collectives, on_device(): lax.all_to_all(summary, 'seq', split_axis=0, concat_axis=0, tiled=True, a...  11.7 us
    all_to_all x1, blocking collectives, on_device(): lax.all_to_all(before, 'seq', split_axis=0, concat_axis=0, tiled=True, ax...  8.25 us
    pallas_call x1, Pallas kernels, on_device(): pl.pallas_call(inside_kernel, in_specs=[FAR] * 6, out_specs=[NEAR] * 2, o...  5.52 us
    ppermute x1, starting transfers between devices, on_device(): came = lax.ppermute(lend, 'seq', pairs)  5.47 us
    ppermute x1, starting transfers between devices, on_device(): theirs = lax.ppermute(send, 'seq', pairs)  5.16 us
    pallas_call x1, Pallas kernels, on_device(): pl.pallas_call(finish_kernel, in_specs=[pl.BlockSpec(memory_space=pltpu.H...  4.49 us
  transfers between devices with their start and end apart: 6, of which 1 were waited for; matrix products, arithmetic and copies ran while one was open for 1% of the time, Pallas kernels for 10%

profile of v6, /device:TPU:1, one launch (start us, length us, event | category | flops | bytes accessed | tf_op | source)
XLA Modules:
  0.0 114.4 jit_solution(11281271650015317158)
XLA Ops:
  0.0 2.2 %pack.1 = bf16[16,648,128]{2,1,0:T(8,128)(2,1)S(1)} custom-call(bf16[128,2048]{1,0:T(8,128)(2,1)} %q_in.1, bf16[128,2048]{1,0:T(8,128)(2,1)} %k_in.1, bf16[128,4096]{1,0:T(8,128)(2,1)} %v_in.1, f32[8,128]{1,0:T(8,128)} %bitcast.4, f32[8,128]{1,0:T(8,128)} %bitcast.5), custom_call_target="tpu_custom_call" | custom-call | tf_op jit(solution)/shard_map/pack/pallas_call | solution.py:397
  2.2 39.5 %all_to_all.15.r_ref = bf16[16,648,128]{2,1,0:T(8,128)(2,1)S(1)} all-to-all(bf16[16,648,128]{2,1,0:T(8,128)(2,1)S(1)} %pack.1), channel_id=1, replica_groups=mesh['seq'=32,'head'=16] {'head'}, dimensions={0} | all-to-all | bytes 5308416 | tf_op jit(solution)/shard_map/all_to_all | solution.py:414
  41.7 0.0 copy-start
  41.7 1.1 summary.1
  42.8 5.2 %collective-permute-start.1 = (f32[136,256]{1,0:T(8,128)S(1)}, f32[136,256]{1,0:T(8,128)S(1)}, u32[]{:S(2)}, u32[]{:S(2)}) collective-permute-start(f32[136,256]{1,0:T(8,128)S(1)} %get-tuple-element.25), channel_id=1, source_target_pairs={{0,16},{16,0},{32,48},{48,32},{64,80},{80,64},{96,112},{112,96},{1... | collective-permute-start | bytes 417800 | tf_op jit(solution)/shard_map/ppermute | solution.py:426
  48.0 1.0 collective-permute-done.1.theirs_ref
  49.0 0.1 pair.1
  49.1 11.7 %all_to_all.16.z_ref = f32[4,40,256]{2,1,0:T(8,128)S(1)} all-to-all(f32[4,40,256]{2,1,0:T(8,128)S(1)} %get-tuple-element.26), channel_id=1, replica_groups={{0,32,64,96},{16,48,80,112},{128,160,192,224},{144,176,208,240},{256,28..., dimensions={0} | all-to-all | bytes 327680 | tf_op jit(solution)/shard_map/all_to_all | solution.py:440
  60.8 0.7 near.1
  61.5 9.7 %collective-permute-start.4 = (f32[40,256]{1,0:T(8,128)S(1)}, f32[40,256]{1,0:T(8,128)S(1)}, u32[]{:S(2)}, u32[]{:S(2)}) collective-permute-start(f32[40,256]{1,0:T(8,128)S(1)} %get-tuple-element.30), channel_id=1, source_target_pairs={{0,384},{16,400},{32,416},{48,432},{64,448},{80,464},{96,480},{112... | collective-permute-start | bytes 122888 | tf_op jit(solution)/shard_map/ppermute | solution.py:475
  71.2 3.7 %collective-permute-start.3 = (f32[40,256]{1,0:T(8,128)S(1)}, f32[40,256]{1,0:T(8,128)S(1)}, u32[]{:S(2)}, u32[]{:S(2)}) collective-permute-start(f32[40,256]{1,0:T(8,128)S(1)} %get-tuple-element.30), channel_id=1, source_target_pairs={{0,256},{16,272},{32,288},{48,304},{64,320},{80,336},{96,352},{112... | collective-permute-start | bytes 122888 | tf_op jit(solution)/shard_map/ppermute | solution.py:475
  74.9 4.6 %collective-permute-start.2 = (f32[40,256]{1,0:T(8,128)S(1)}, f32[40,256]{1,0:T(8,128)S(1)}, u32[]{:S(2)}, u32[]{:S(2)}) collective-permute-start(f32[40,256]{1,0:T(8,128)S(1)} %get-tuple-element.30), channel_id=1, source_target_pairs={{0,128},{16,144},{32,160},{48,176},{64,192},{80,208},{96,224},{112... | collective-permute-start | bytes 122888 | tf_op jit(solution)/shard_map/ppermute | solution.py:475
  79.5 0.0 copy-done
  79.5 0.9 slice.4.own_in
  80.4 2.2 %collective-permute-start = (bf16[16,128,128]{2,1,0:T(8,128)(2,1)}, bf16[16,128,128]{2,1,0:T(8,128)(2,1)}, u32[]{:S(2)}, u32[]{:S(2)}) collective-permute-start(bf16[16,128,128]{2,1,0:T(8,128)(2,1)} %slice.4.own_in), channel_id=1, source_target_pairs={{0,1},{1,0},{2,3},{3,2},{4,5},{5,4},{6,7},{7,6},{8,9},{9,8},{10,11... | collective-permute-start | bytes 1572872 | tf_op jit(solution)/shard_map/ppermute | solution.py:445
  82.6 0.0 collective-permute-done.4.refs_5_
  82.6 0.0 collective-permute-done.3.refs_4_
  82.6 0.0 collective-permute-done.2.refs_3_
  82.6 1.6 %far.1 = (f32[4,32,256]{2,1,0:T(8,128)}, f32[8,256]{1,0:T(8,128)}) custom-call(f32[4,32,256]{2,1,0:T(8,128)} %get-tuple-element.27.refs_0_, f32[16,256]{1,0:T(8,128)} %get-tuple-element.28.refs_1_, f32[136,256]{1,0:T(8,128)S(1)} %get-tuple-element.29.refs_2_.first_ref, f32[40,256]{1,0:T(8,128)S(1)} %collective-permute-done.2.refs_3_, ...), custom_call_target="tpu_custom_call" | custom-call | tf_op jit(solution)/shard_map/far/pallas_call | solution.py:477
  84.3 8.3 %all_to_all.17 = f32[4,32,256]{2,1,0:T(8,128)S(1)} all-to-all(f32[4,32,256]{2,1,0:T(8,128)} %get-tuple-element.34), channel_id=1, replica_groups={{0,32,64,96},{16,48,80,112},{128,160,192,224},{144,176,208,240},{256,28..., dimensions={0} | all-to-all | bytes 262144 | tf_op jit(solution)/shard_map/all_to_all | solution.py:489
  92.5 0.0 copy-start.2
  92.5 0.7 copy-done.2
  93.2 0.1 mix.1
  93.3 5.5 %collective-permute-start.5 = (f32[128,256]{1,0:T(8,128)S(1)}, f32[128,256]{1,0:T(8,128)S(1)}, u32[]{:S(2)}, u32[]{:S(2)}) collective-permute-start(f32[128,256]{1,0:T(8,128)S(1)} %get-tuple-element.36), channel_id=1, source_target_pairs={{0,16},{16,0},{32,48},{48,32},{64,80},{80,64},{96,112},{112,96},{1... | collective-permute-start | bytes 393224 | tf_op jit(solution)/shard_map/ppermute | solution.py:501
  98.8 0.0 copy-start.1
  98.8 1.7 %copy-done.1 = bf16[16,648,128]{2,1,0:T(8,128)(2,1)S(1)} copy-done((bf16[16,648,128]{2,1,0:T(8,128)(2,1)S(1)}, bf16[16,648,128]{2,1,0:T(8,128)(2,1)}, u32[]{:S(2)}) %copy-start.1) | copy-done | bytes 2654232
  100.5 3.8 %entries.1 = (bf16[8,256,256]{2,1,0:T(8,128)(2,1)}, bf16[8,256,256]{2,1,0:T(8,128)(2,1)}, f32[8,8,256]{2,1,0:T(8,128)}) custom-call(bf16[16,648,128]{2,1,0:T(8,128)(2,1)S(1)} %copy-done.1), custom_call_target="tpu_custom_call" | custom-call | tf_op jit(solution)/shard_map/entries/pallas_call | solution.py:447
  104.4 0.0 collective-permute-done.other_ref.other_in
  104.4 5.5 %inside.1 = (f32[8,256,256]{2,1,0:T(8,128)S(1)}, f32[8,8,256]{2,1,0:T(8,128)S(1)}) custom-call(bf16[16,648,128]{2,1,0:T(8,128)(2,1)} %copy-done, bf16[16,128,128]{2,1,0:T(8,128)(2,1)} %collective-permute-done.other_ref.other_in, bf16[8,256,256]{2,1,0:T(8,128)(2,1)} %get-tuple-element.21.top_ref, bf16[8,256,256]{2,1,0:T(8,128)(2,1)} %get-tuple-element.22.low_ref, ...), custom_call_target="tpu_custom_call" | custom-call | tf_op jit(solution)/shard_map/inside/pallas_call | solution.py:503
  109.9 0.0 collective-permute-done.5.came_ref
  109.9 4.5 %finish.1 = bf16[2048,256]{1,0:T(8,128)(2,1)} custom-call(bf16[16,128,128]{2,1,0:T(8,128)(2,1)} %slice.4.own_in, bf16[16,128,128]{2,1,0:T(8,128)(2,1)} %collective-permute-done.other_ref.other_in, f32[8,256,256]{2,1,0:T(8,128)S(1)} %get-tuple-element.32.num_ref, f32[8,8,256]{2,1,0:T(8,128)S(1)} %get-tuple-element.33.row_ref, ...), custom_call_target="tpu_custom_call" | custom-call | tf_op jit(solution)/shard_map/finish/pallas_call | solution.py:515
Async XLA Ops:
  41.7 37.8 %copy-start = (bf16[16,648,128]{2,1,0:T(8,128)(2,1)}, bf16[16,648,128]{2,1,0:T(8,128)(2,1)S(1)}, u32[]{:S(2)}) copy-start(bf16[16,648,128]{2,1,0:T(8,128)(2,1)S(1)} %all_to_all.15.r_ref) | copy-start | bytes 7962628
  42.8 6.1 %collective-permute-start.1 = (f32[136,256]{1,0:T(8,128)S(1)}, f32[136,256]{1,0:T(8,128)S(1)}, u32[]{:S(2)}, u32[]{:S(2)}) collective-permute-start(f32[136,256]{1,0:T(8,128)S(1)} %get-tuple-element.25), channel_id=1, source_target_pairs={{0,16},{16,0},{32,48},{48,32},{64,80},{80,64},{96,112},{112,96},{1... | collective-permute-start | bytes 417800 | tf_op jit(solution)/shard_map/ppermute | solution.py:426
  61.5 21.1 %collective-permute-start.4 = (f32[40,256]{1,0:T(8,128)S(1)}, f32[40,256]{1,0:T(8,128)S(1)}, u32[]{:S(2)}, u32[]{:S(2)}) collective-permute-start(f32[40,256]{1,0:T(8,128)S(1)} %get-tuple-element.30), channel_id=1, source_target_pairs={{0,384},{16,400},{32,416},{48,432},{64,448},{80,464},{96,480},{112... | collective-permute-start | bytes 122888 | tf_op jit(solution)/shard_map/ppermute | solution.py:475
  71.2 11.4 %collective-permute-start.3 = (f32[40,256]{1,0:T(8,128)S(1)}, f32[40,256]{1,0:T(8,128)S(1)}, u32[]{:S(2)}, u32[]{:S(2)}) collective-permute-start(f32[40,256]{1,0:T(8,128)S(1)} %get-tuple-element.30), channel_id=1, source_target_pairs={{0,256},{16,272},{32,288},{48,304},{64,320},{80,336},{96,352},{112... | collective-permute-start | bytes 122888 | tf_op jit(solution)/shard_map/ppermute | solution.py:475
  74.9 7.7 %collective-permute-start.2 = (f32[40,256]{1,0:T(8,128)S(1)}, f32[40,256]{1,0:T(8,128)S(1)}, u32[]{:S(2)}, u32[]{:S(2)}) collective-permute-start(f32[40,256]{1,0:T(8,128)S(1)} %get-tuple-element.30), channel_id=1, source_target_pairs={{0,128},{16,144},{32,160},{48,176},{64,192},{80,208},{96,224},{112... | collective-permute-start | bytes 122888 | tf_op jit(solution)/shard_map/ppermute | solution.py:475
  80.4 24.0 %collective-permute-start = (bf16[16,128,128]{2,1,0:T(8,128)(2,1)}, bf16[16,128,128]{2,1,0:T(8,128)(2,1)}, u32[]{:S(2)}, u32[]{:S(2)}) collective-permute-start(bf16[16,128,128]{2,1,0:T(8,128)(2,1)} %slice.4.own_in), channel_id=1, source_target_pairs={{0,1},{1,0},{2,3},{3,2},{4,5},{5,4},{6,7},{7,6},{8,9},{9,8},{10,11... | collective-permute-start | bytes 1572872 | tf_op jit(solution)/shard_map/ppermute | solution.py:445
  92.5 0.7 copy-start.2
  93.3 16.6 %collective-permute-start.5 = (f32[128,256]{1,0:T(8,128)S(1)}, f32[128,256]{1,0:T(8,128)S(1)}, u32[]{:S(2)}, u32[]{:S(2)}) collective-permute-start(f32[128,256]{1,0:T(8,128)S(1)} %get-tuple-element.36), channel_id=1, source_target_pairs={{0,16},{16,0},{32,48},{48,32},{64,80},{80,64},{96,112},{112,96},{1... | collective-permute-start | bytes 393224 | tf_op jit(solution)/shard_map/ppermute | solution.py:501
  98.8 1.8 %copy-start.1 = (bf16[16,648,128]{2,1,0:T(8,128)(2,1)S(1)}, bf16[16,648,128]{2,1,0:T(8,128)(2,1)}, u32[]{:S(2)}) copy-start(bf16[16,648,128]{2,1,0:T(8,128)(2,1)} %copy-done) | copy-start | bytes 7962628

commit v7 on v6

--- a/solution.py
+++ b/solution.py
@@ -10,8 +10,7 @@
 PIECE = 256
 HALF = PIECE // 2
 KEYS = PIECE
-ASKED = 2 * PIECE
-GATES = ASKED + HALF
+GATES = 2 * PIECE
 VMEM_LIMIT = 24 << 20
 INSIDE_LIMIT = 56 << 20
 FAR_LIMIT = 59 << 20
@@ -46,9 +45,9 @@
     return lax.rem(lax.axis_index("seq"), 2) == 0
 
 
-def pack_kernel(q_in, k_in, v_in, gate_in, forget_in, out_ref, q_ref, k_ref, v_ref, gate_ref, forget_ref, sem):
+def pack_kernel(k_in, v_in, gate_in, forget_in, out_ref, k_ref, v_ref, gate_ref, forget_ref, sem):
     rows = k_ref.shape[0]
-    pairs = (gate_in, gate_ref), (forget_in, forget_ref), (v_in, v_ref), (k_in, k_ref), (q_in, q_ref)
+    pairs = (gate_in, gate_ref), (forget_in, forget_ref), (v_in, v_ref), (k_in, k_ref)
     copies = [pltpu.make_async_copy(a, b, sem.at[n]) for n, (a, b) in enumerate(pairs)]
     for copy in copies:
         copy.start()
@@ -69,11 +68,16 @@
             n = 2 * h + u
             out_ref[n, 0:PIECE, :] = v_ref[:, n * PIECE : (n + 1) * PIECE].T
             for c in range(2):
-                left = h * PIECE + (c ^ u) * HALF
+                left = h * PIECE + c * HALF
                 out_ref[n, KEYS + c * HALF : KEYS + (c + 1) * HALF, :] = k_ref[:, left : left + HALF]
-            left = h * PIECE + u * HALF
-            out_ref[n, ASKED:GATES, :] = q_ref[:, left : left + HALF].T
             out_ref[n, GATES : GATES + GATE_ROWS, :] = area
+
+
+def turn_kernel(q_ref, out_ref):
+    for h in range(q_ref.shape[1] // PIECE):
+        turned = q_ref[:, h * PIECE : (h + 1) * PIECE].T
+        out_ref[2 * h] = turned
+        out_ref[2 * h + 1] = turned
 
 
 def beside(ref, blocks, low, high):
@@ -88,10 +92,6 @@
         ],
         axis=0,
     )
-
-
-def asked_rows(ref, other_ref, blocks):
-    return jnp.concatenate([beside(ref, blocks, ASKED, GATES), beside(other_ref, blocks, 0, HALF)], axis=0)
 
 
 def chunk_blocks(ref, chunk):
@@ -281,7 +281,7 @@
     send_ref[...] = jnp.where(first, after, before)
 
 
-def inside_kernel(r_ref, other_ref, top_ref, low_ref, aux_ref, nin_ref, num_ref, row_ref):
+def inside_kernel(r_ref, asked_ref, top_ref, low_ref, aux_ref, nin_ref, num_ref, row_ref):
     factor = PIECE**-0.5
     before = nin_ref[...]
     before_m = before[6:7, 0:1]
@@ -289,7 +289,7 @@
     row = iota((8, CHUNK), 0)
     for step in range(num_ref.shape[0]):
         mine = chunk_blocks(r_ref, step)
-        asked = asked_rows(r_ref, other_ref, mine)
+        asked = beside(asked_ref, mine, 0, PIECE)
         turned = beside(r_ref, mine, 0, PIECE)
         aux = aux_ref[step]
         cum = aux[3:4]
@@ -327,41 +327,35 @@
 
 
 def finish_kernel(
-    own_in, other_in, num_ref, row_ref, keep_ref, came_ref, out_ref,
-    own_ref, other_ref, buffer_ref, in_sem, out_sem,
+    asked_in, num_ref, row_ref, keep_ref, came_ref, out_ref, asked_ref, buffer_ref, in_sem, out_sem,
 ):
     steps = num_ref.shape[0]
-    group = own_ref.shape[0] // steps
+    parts = in_sem.shape[0]
+    share = asked_ref.shape[0] // parts
     arriving = []
-    for step in range(steps):
-        blocks = pl.ds(step * group, group)
-        pairs = (
-            (own_in.at[blocks], own_ref.at[blocks]),
-            (other_in.at[blocks], other_ref.at[blocks]),
-        )
-        arriving.append(
-            [pltpu.make_async_copy(a, b, in_sem.at[2 * step + n]) for n, (a, b) in enumerate(pairs)]
-        )
-        for copy in arriving[-1]:
-            copy.start()
+    for p in range(parts):
+        blocks = pl.ds(p * share, share)
+        arriving.append(pltpu.make_async_copy(asked_in.at[blocks], asked_ref.at[blocks], in_sem.at[p]))
+        arriving[-1].start()
     first = first_core()
     keep, came = keep_ref[...], came_ref[...]
     state = jnp.concatenate([jnp.where(first, keep, came), jnp.where(first, came, keep)], axis=0)
     both = jnp.concatenate(halves(state), axis=1)
+    each = steps // out_sem.shape[0]
     leaving = []
     for step in range(steps):
-        for copy in arriving[step]:
-            copy.wait()
-        blocks = chunk_blocks(own_ref, step)
-        asked = jnp.concatenate(
-            [beside(own_ref, blocks, 0, HALF), beside(other_ref, blocks, 0, HALF)], axis=0
-        )
+        if step % (steps // parts) == 0:
+            arriving[step // (steps // parts)].wait()
+        asked = beside(asked_ref, chunk_blocks(asked_ref, step), 0, PIECE)
         read = dot(both, jnp.concatenate([asked, asked], axis=0), (1, 0))
         out = num_ref[step] + read * row_ref[step, 0:1, :]
-        here = pl.ds(step * CHUNK, CHUNK)
-        buffer_ref[here, :] = out.astype(BF16).T
-        leaving.append(pltpu.make_async_copy(buffer_ref.at[here], out_ref.at[here], out_sem.at[step]))
-        leaving[-1].start()
+        buffer_ref[pl.ds(step * CHUNK, CHUNK), :] = out.astype(BF16).T
+        if step % each == each - 1:
+            here = pl.ds((step - each + 1) * CHUNK, each * CHUNK)
+            leaving.append(
+                pltpu.make_async_copy(buffer_ref.at[here], out_ref.at[here], out_sem.at[step // each])
+            )
+            leaving[-1].start()
     for copy in leaving:
         copy.wait()
 
@@ -396,20 +390,19 @@
 
     packed = pl.pallas_call(
         pack_kernel,
-        in_specs=[pl.BlockSpec(memory_space=pltpu.HBM)] * 5,
+        in_specs=[pl.BlockSpec(memory_space=pltpu.HBM)] * 4,
         out_specs=NEAR,
         out_shape=pltpu.VMEM((pieces, tall, rows), BF16),
         scratch_shapes=[
-            pltpu.VMEM(queries.shape, BF16),
             pltpu.VMEM(keys.shape, BF16),
             pltpu.VMEM(values.shape, BF16),
             pltpu.VMEM((input_pre.shape[1], rows), F32),
             pltpu.VMEM((input_pre.shape[1], rows), F32),
-            pltpu.SemaphoreType.DMA((5,)),
+            pltpu.SemaphoreType.DMA((4,)),
         ],
         compiler_params=PARAMS,
         name="pack",
-    )(*(far(x) for x in (queries, keys, values, input_pre.T, forget_pre.T)))
+    )(*(far(x) for x in (keys, values, input_pre.T, forget_pre.T)))
 
     received = lax.all_to_all(packed, "head", split_axis=0, concat_axis=0, tiled=True)
 
@@ -441,12 +434,18 @@
         summary, "seq", split_axis=0, concat_axis=0, tiled=True, axis_index_groups=groups
     )
 
-    ours = received[:, ASKED:GATES, :]
-    other = lax.ppermute(ours, "head", [(i, i ^ 1) for i in range(pieces)])
+    turned = pl.pallas_call(
+        turn_kernel,
+        in_specs=[FAR],
+        out_specs=FAR,
+        out_shape=jax.ShapeDtypeStruct((pieces, PIECE, rows), BF16),
+        name="turn",
+    )(far(queries))
+    asked = lax.all_to_all(turned, "head", split_axis=0, concat_axis=0, tiled=True)
 
     entry_top, entry_low, aux = pl.pallas_call(
         entries_kernel,
-        in_specs=[NEAR],
+        in_specs=[FAR],
         out_specs=[FAR] * 3,
         out_shape=[
             jax.ShapeDtypeStruct((steps, PIECE, PIECE), BF16),
@@ -454,7 +453,7 @@
             jax.ShapeDtypeStruct((steps, 8, CHUNK), F32),
         ],
         name="entries",
-    )(near(received))
+    )(far(received))
 
     group_sum, local, meta = pl.pallas_call(
         near_kernel,
@@ -510,23 +509,22 @@
         ],
         compiler_params=pltpu.CompilerParams(vmem_limit_bytes=INSIDE_LIMIT),
         name="inside",
-    )(far(received), far(other), entry_top, entry_low, aux, normal)
+    )(far(received), far(asked), entry_top, entry_low, aux, normal)
 
     return pl.pallas_call(
         finish_kernel,
-        in_specs=[pl.BlockSpec(memory_space=pltpu.HBM)] * 2 + [NEAR] * 4,
+        in_specs=[pl.BlockSpec(memory_space=pltpu.HBM)] + [NEAR] * 4,
         out_specs=pl.BlockSpec(memory_space=pltpu.HBM),
         out_shape=jax.ShapeDtypeStruct((tokens, PIECE), BF16),
         scratch_shapes=[
-            pltpu.VMEM(ours.shape, BF16),
-            pltpu.VMEM(ours.shape, BF16),
+            pltpu.VMEM(asked.shape, BF16),
             pltpu.VMEM((tokens, PIECE), BF16),
-            pltpu.SemaphoreType.DMA((2 * steps,)),
-            pltpu.SemaphoreType.DMA((steps,)),
+            pltpu.SemaphoreType.DMA((2,)),
+            pltpu.SemaphoreType.DMA((steps // 2,)),
         ],
         compiler_params=PARAMS,
         name="finish",
-    )(far(ours), far(other), num, line, keep, near(came))
+    )(far(asked), num, line, keep, near(came))
 
 
 def solution(mesh):

time: 115 us -> 115 us (level)
  the two profiles are of different devices: /device:TPU:1 before, /device:TPU:128 now
where the time goes in v7:
time: 115 us
  blocking collectives  48.7 us (42%)
  starting transfers between devices  22.4 us (19%)
  Pallas kernels  21.6 us (19%)
  waiting for transfers between devices  21.1 us (18%)
    all_to_all x1, blocking collectives, on_device(): lax.all_to_all(packed, 'head', split_axis=0, concat_axis=0, tiled=True)  36 us
    all_to_all x1, blocking collectives, on_device(): lax.all_to_all(summary, 'seq', split_axis=0, concat_axis=0, tiled=True, a...  12.7 us
    ppermute x3, starting transfers between devices, on_device(): lax.ppermute(group_sum, 'seq', [(i, i + step) for i in range(shards - ste...  11.4 us
    all_to_all x1, waiting for transfers between devices, on_device(): lax.all_to_all(turned, 'head', split_axis=0, concat_axis=0, tiled=True)  8.09 us
    ppermute x3, waiting for transfers between devices, on_device(): lax.ppermute(group_sum, 'seq', [(i, i + step) for i in range(shards - ste...  7.87 us
    pallas_call x1, Pallas kernels, on_device(): pl.pallas_call(entries_kernel, in_specs=[FAR], out_specs=[FAR] * 3, out_s...  5.53 us
    pallas_call x1, Pallas kernels, on_device(): pl.pallas_call(inside_kernel, in_specs=[FAR] * 6, out_specs=[NEAR] * 2, o...  5.52 us
    all_to_all x1, waiting for transfers between devices, on_device(): lax.all_to_all(before, 'seq', split_axis=0, concat_axis=0, tiled=True, ax...  3.83 us
  transfers between devices with their start and end apart: 7, of which 5 were waited for; matrix products, arithmetic and copies ran while one was open for 0% of the time, Pallas kernels for 12%

profile of v7, /device:TPU:128, one launch (start us, length us, event | category | flops | bytes accessed | tf_op | source)
XLA Modules:
  0.0 114.8 jit_solution(8670773002160455184)
XLA Ops:
  0.0 1.9 %pack.1 = bf16[16,520,128]{2,1,0:T(8,128)(2,1)S(1)} custom-call(bf16[128,2048]{1,0:T(8,128)(2,1)} %k_in.1, bf16[128,4096]{1,0:T(8,128)(2,1)} %v_in.1, f32[8,128]{1,0:T(8,128)} %bitcast.4, f32[8,128]{1,0:T(8,128)} %bitcast.5), custom_call_target="tpu_custom_call" | custom-call | tf_op jit(solution)/shard_map/pack/pallas_call | solution.py:391
  1.9 36.0 %all_to_all.20.r_ref = bf16[16,520,128]{2,1,0:T(8,128)(2,1)S(1)} all-to-all(bf16[16,520,128]{2,1,0:T(8,128)(2,1)S(1)} %pack.1), channel_id=1, replica_groups=mesh['seq'=32,'head'=16] {'head'}, dimensions={0} | all-to-all | bytes 4259840 | tf_op jit(solution)/shard_map/all_to_all | solution.py:407
  37.9 0.0 copy-start
  37.9 1.1 summary.1
  38.9 1.9 %collective-permute-start = (f32[136,256]{1,0:T(8,128)S(1)}, f32[136,256]{1,0:T(8,128)S(1)}, u32[]{:S(2)}, u32[]{:S(2)}) collective-permute-start(f32[136,256]{1,0:T(8,128)S(1)} %get-tuple-element.25), channel_id=1, source_target_pairs={{0,16},{16,0},{32,48},{48,32},{64,80},{80,64},{96,112},{112,96},{1... | collective-permute-start | bytes 417800 | tf_op jit(solution)/shard_map/ppermute | solution.py:419
  40.8 1.3 %collective-permute-done.theirs_ref = f32[136,256]{1,0:T(8,128)S(1)} collective-permute-done((f32[136,256]{1,0:T(8,128)S(1)}, f32[136,256]{1,0:T(8,128)S(1)}, u32[]{:S(2)}, u32[]{:S(2)}) %collective-permute-start) | collective-permute-done | bytes 139296 | tf_op jit(solution)/shard_map/ppermute | solution.py:419
  42.2 0.1 pair.1
  42.3 12.7 %all_to_all.21.z_ref = f32[4,40,256]{2,1,0:T(8,128)S(1)} all-to-all(f32[4,40,256]{2,1,0:T(8,128)S(1)} %get-tuple-element.26), channel_id=1, replica_groups={{0,32,64,96},{16,48,80,112},{128,160,192,224},{144,176,208,240},{256,28..., dimensions={0} | all-to-all | bytes 327680 | tf_op jit(solution)/shard_map/all_to_all | solution.py:433
  55.0 0.7 near.1
  55.7 0.7 collective-permute-start.3
  56.4 8.8 %collective-permute-start.2 = (f32[40,256]{1,0:T(8,128)S(1)}, f32[40,256]{1,0:T(8,128)S(1)}, u32[]{:S(2)}, u32[]{:S(2)}) collective-permute-start(f32[40,256]{1,0:T(8,128)S(1)} %get-tuple-element.30), channel_id=1, source_target_pairs={{0,256},{16,272},{32,288},{48,304},{64,320},{80,336},{96,352},{112... | collective-permute-start | bytes 122888 | tf_op jit(solution)/shard_map/ppermute | solution.py:474
  65.2 1.9 %collective-permute-start.1 = (f32[40,256]{1,0:T(8,128)S(1)}, f32[40,256]{1,0:T(8,128)S(1)}, u32[]{:S(2)}, u32[]{:S(2)}) collective-permute-start(f32[40,256]{1,0:T(8,128)S(1)} %get-tuple-element.30), channel_id=1, source_target_pairs={{0,128},{16,144},{32,160},{48,176},{64,192},{80,208},{96,224},{112... | collective-permute-start | bytes 122888 | tf_op jit(solution)/shard_map/ppermute | solution.py:474
  67.1 0.0 collective-permute-done.3.refs_5_
  67.1 0.6 collective-permute-done.2.refs_4_
  67.8 7.2 %collective-permute-done.1.refs_3_ = f32[40,256]{1,0:T(8,128)S(1)} collective-permute-done((f32[40,256]{1,0:T(8,128)S(1)}, f32[40,256]{1,0:T(8,128)S(1)}, u32[]{:S(2)}, u32[]{:S(2)}) %collective-permute-start.1) | collective-permute-done | bytes 40992 | tf_op jit(solution)/shard_map/ppermute | solution.py:474
  75.0 1.6 %far.1 = (f32[4,32,256]{2,1,0:T(8,128)}, f32[8,256]{1,0:T(8,128)}) custom-call(f32[4,32,256]{2,1,0:T(8,128)} %get-tuple-element.27.refs_0_, f32[16,256]{1,0:T(8,128)} %get-tuple-element.28.refs_1_, f32[136,256]{1,0:T(8,128)S(1)} %get-tuple-element.29.refs_2_.first_ref, f32[40,256]{1,0:T(8,128)S(1)} %collective-permute-done.1.refs_3_, ...), custom_call_target="tpu_custom_call" | custom-call | tf_op jit(solution)/shard_map/far/pallas_call | solution.py:476
  76.7 0.0 copy-start.1
  76.7 3.5 %all-to-all-start.3 = ((f32[4,32,256]{2,1,0:T(8,128)}), f32[4,32,256]{2,1,0:T(8,128)S(1)}, u32[]{:S(2)}, u32[]{:S(2)}) async-start(f32[4,32,256]{2,1,0:T(8,128)} %get-tuple-element.34), calls=%async_computation.3 | async-start | bytes 262144 | tf_op jit(solution)/shard_map/all_to_all | solution.py:488
  80.1 2.2 %turn.1 = bf16[16,256,128]{2,1,0:T(8,128)(2,1)} custom-call(bf16[128,2048]{1,0:T(8,128)(2,1)} %q_ref.1), custom_call_target="tpu_custom_call" | custom-call | tf_op jit(solution)/shard_map/turn/pallas_call | solution.py:437
  82.3 0.0 copy-done
  82.3 3.8 %all-to-all-done.3 = f32[4,32,256]{2,1,0:T(8,128)S(1)} async-done(((f32[4,32,256]{2,1,0:T(8,128)}), f32[4,32,256]{2,1,0:T(8,128)S(1)}, u32[]{:S(2)}, u32[]{:S(2)}) %all-to-all-start.3) | async-done | bytes 131104 | tf_op jit(solution)/shard_map/all_to_all | solution.py:488
  86.2 3.7 %all-to-all-start = ((bf16[16,256,128]{2,1,0:T(8,128)(2,1)}), bf16[16,256,128]{2,1,0:T(8,128)(2,1)S(1)}, u32[]{:S(2)}, u32[]{:S(2)}) async-start(bf16[16,256,128]{2,1,0:T(8,128)(2,1)} %turn.1), calls=%async_computation | async-start | bytes 2097152 | tf_op jit(solution)/shard_map/all_to_all | solution.py:444
  89.8 0.0 copy-done.1
  89.8 0.1 mix.1
  89.9 1.9 %collective-permute-start.4 = (f32[128,256]{1,0:T(8,128)S(1)}, f32[128,256]{1,0:T(8,128)S(1)}, u32[]{:S(2)}, u32[]{:S(2)}) collective-permute-start(f32[128,256]{1,0:T(8,128)S(1)} %get-tuple-element.36), channel_id=1, source_target_pairs={{0,16},{16,0},{32,48},{48,32},{64,80},{80,64},{96,112},{112,96},{1... | collective-permute-start | bytes 393224 | tf_op jit(solution)/shard_map/ppermute | solution.py:500
  91.9 5.5 %entries.1 = (bf16[8,256,256]{2,1,0:T(8,128)(2,1)}, bf16[8,256,256]{2,1,0:T(8,128)(2,1)}, f32[8,8,256]{2,1,0:T(8,128)}) custom-call(bf16[16,520,128]{2,1,0:T(8,128)(2,1)} %copy-done), custom_call_target="tpu_custom_call" | custom-call | tf_op jit(solution)/shard_map/entries/pallas_call | solution.py:446
  97.4 8.1 %all-to-all-done.asked_ref.asked_in = bf16[16,256,128]{2,1,0:T(8,128)(2,1)S(1)} async-done(((bf16[16,256,128]{2,1,0:T(8,128)(2,1)}), bf16[16,256,128]{2,1,0:T(8,128)(2,1)S(1)}, u32[]{:S(2)}, u32[]{:S(2)}) %all-to-all-start) | async-done | bytes 1048608 | tf_op jit(solution)/shard_map/all_to_all | solution.py:444
  105.5 0.0 copy-start.2
  105.5 1.0 copy-done.2
  106.5 5.5 %inside.1 = (f32[8,256,256]{2,1,0:T(8,128)S(1)}, f32[8,8,256]{2,1,0:T(8,128)S(1)}) custom-call(bf16[16,520,128]{2,1,0:T(8,128)(2,1)} %copy-done, bf16[16,256,128]{2,1,0:T(8,128)(2,1)} %copy-done.2, bf16[8,256,256]{2,1,0:T(8,128)(2,1)} %get-tuple-element.21.top_ref, bf16[8,256,256]{2,1,0:T(8,128)(2,1)} %get-tuple-element.22.low_ref, ...), custom_call_target="tpu_custom_call" | custom-call | tf_op jit(solution)/shard_map/inside/pallas_call | solution.py:502
  112.0 0.0 collective-permute-done.4.came_ref
  112.0 2.8 %finish.1 = bf16[2048,256]{1,0:T(8,128)(2,1)} custom-call(bf16[16,256,128]{2,1,0:T(8,128)(2,1)} %copy-done.2, f32[8,256,256]{2,1,0:T(8,128)S(1)} %get-tuple-element.32.num_ref, f32[8,8,256]{2,1,0:T(8,128)S(1)} %get-tuple-element.33.row_ref, f32[128,256]{1,0:T(8,128)S(1)} %get-tuple-element.35.keep_ref, f32[128,256]{1,0:T(8,128)S(1)} %collective-permute-done.4.came_ref), custom_call_target="tpu_custom_call" | custom-call | tf_op jit(solution)/shard_map/finish/pallas_call | solution.py:514
Async XLA Ops:
  37.9 44.5 %copy-start = (bf16[16,520,128]{2,1,0:T(8,128)(2,1)}, bf16[16,520,128]{2,1,0:T(8,128)(2,1)S(1)}, u32[]{:S(2)}) copy-start(bf16[16,520,128]{2,1,0:T(8,128)(2,1)S(1)} %all_to_all.20.r_ref) | copy-start | bytes 6389764
  38.9 3.3 %collective-permute-start = (f32[136,256]{1,0:T(8,128)S(1)}, f32[136,256]{1,0:T(8,128)S(1)}, u32[]{:S(2)}, u32[]{:S(2)}) collective-permute-start(f32[136,256]{1,0:T(8,128)S(1)} %get-tuple-element.25), channel_id=1, source_target_pairs={{0,16},{16,0},{32,48},{48,32},{64,80},{80,64},{96,112},{112,96},{1... | collective-permute-start | bytes 417800 | tf_op jit(solution)/shard_map/ppermute | solution.py:419
  55.7 11.4 %collective-permute-start.3 = (f32[40,256]{1,0:T(8,128)S(1)}, f32[40,256]{1,0:T(8,128)S(1)}, u32[]{:S(2)}, u32[]{:S(2)}) collective-permute-start(f32[40,256]{1,0:T(8,128)S(1)} %get-tuple-element.30), channel_id=1, source_target_pairs={{0,384},{16,400},{32,416},{48,432},{64,448},{80,464},{96,480},{112... | collective-permute-start | bytes 122888 | tf_op jit(solution)/shard_map/ppermute | solution.py:474
  56.4 11.4 %collective-permute-start.2 = (f32[40,256]{1,0:T(8,128)S(1)}, f32[40,256]{1,0:T(8,128)S(1)}, u32[]{:S(2)}, u32[]{:S(2)}) collective-permute-start(f32[40,256]{1,0:T(8,128)S(1)} %get-tuple-element.30), channel_id=1, source_target_pairs={{0,256},{16,272},{32,288},{48,304},{64,320},{80,336},{96,352},{112... | collective-permute-start | bytes 122888 | tf_op jit(solution)/shard_map/ppermute | solution.py:474
  65.2 9.8 %collective-permute-start.1 = (f32[40,256]{1,0:T(8,128)S(1)}, f32[40,256]{1,0:T(8,128)S(1)}, u32[]{:S(2)}, u32[]{:S(2)}) collective-permute-start(f32[40,256]{1,0:T(8,128)S(1)} %get-tuple-element.30), channel_id=1, source_target_pairs={{0,128},{16,144},{32,160},{48,176},{64,192},{80,208},{96,224},{112... | collective-permute-start | bytes 122888 | tf_op jit(solution)/shard_map/ppermute | solution.py:474
  76.7 13.2 %copy-start.1 = (f32[8,256]{1,0:T(8,128)S(1)}, f32[8,256]{1,0:T(8,128)}, u32[]{:S(2)}) copy-start(f32[8,256]{1,0:T(8,128)} %get-tuple-element.31.nin_ref) | copy-start | bytes 24580
  76.7 9.5 %all-to-all-start.3 = ((f32[4,32,256]{2,1,0:T(8,128)}), f32[4,32,256]{2,1,0:T(8,128)S(1)}, u32[]{:S(2)}, u32[]{:S(2)}) async-start(f32[4,32,256]{2,1,0:T(8,128)} %get-tuple-element.34), calls=%async_computation.3 | async-start | bytes 262144 | tf_op jit(solution)/shard_map/all_to_all | solution.py:488
  86.2 19.3 %all-to-all-start = ((bf16[16,256,128]{2,1,0:T(8,128)(2,1)}), bf16[16,256,128]{2,1,0:T(8,128)(2,1)S(1)}, u32[]{:S(2)}, u32[]{:S(2)}) async-start(bf16[16,256,128]{2,1,0:T(8,128)(2,1)} %turn.1), calls=%async_computation | async-start | bytes 2097152 | tf_op jit(solution)/shard_map/all_to_all | solution.py:444
  89.9 22.1 %collective-permute-start.4 = (f32[128,256]{1,0:T(8,128)S(1)}, f32[128,256]{1,0:T(8,128)S(1)}, u32[]{:S(2)}, u32[]{:S(2)}) collective-permute-start(f32[128,256]{1,0:T(8,128)S(1)} %get-tuple-element.36), channel_id=1, source_target_pairs={{0,16},{16,0},{32,48},{48,32},{64,80},{80,64},{96,112},{112,96},{1... | collective-permute-start | bytes 393224 | tf_op jit(solution)/shard_map/ppermute | solution.py:500
  105.5 1.0 copy-start.2

commit v8 on v7

--- a/solution.py
+++ b/solution.py
@@ -15,6 +15,7 @@
 INSIDE_LIMIT = 56 << 20
 FAR_LIMIT = 59 << 20
 NEAR_CHIPS = 4
+PARTS = 2
 GATE_ROWS = 8
 F32 = jnp.float32
 BF16 = jnp.bfloat16
@@ -170,17 +171,41 @@
         z_ref[i, slab:, :] = rest
 
 
-def entries_kernel(r_ref, top_ref, low_ref, aux_ref):
+def in_parts(pairs, sem, parts):
+    started = []
+    for p in range(parts):
+        copies = []
+        for n, (a, b) in enumerate(pairs):
+            share = a.shape[0] // parts
+            here = pl.ds(p * share, share)
+            copies.append(pltpu.make_async_copy(a.at[here], b.at[here], sem.at[len(pairs) * p + n]))
+            copies[-1].start()
+        started.append(copies)
+    return started
+
+
+def entries_kernel(r_in, entry_out, aux_ref, r_ref, entry_ref, in_sem, out_sem):
     upper = (iota((CHUNK, CHUNK), 0) <= iota((CHUNK, CHUNK), 1)).astype(BF16)
     row = iota((8, CHUNK), 0)
     state = jnp.zeros((PIECE, PIECE), F32)
     normal = jnp.zeros((1, PIECE), F32)
     old_m = jnp.full((1, 1), VERY_NEGATIVE, F32)
     start = jnp.zeros((1, 1), F32)
-    steps = top_ref.shape[0]
+    steps = entry_ref.shape[0]
+    arriving = in_parts([(r_in, r_ref)], in_sem, PARTS)
+    leaving = []
     for step in range(steps):
+        if step % (steps // PARTS) == 0:
+            arriving[step // (steps // PARTS)][0].wait()
         mine = chunk_blocks(r_ref, step)
-        top_ref[step], low_ref[step] = halves(state)
+        entry_ref[step] = jnp.concatenate(halves(state), axis=1)
+        if (step + 1) % (steps // PARTS) == 0:
+            part = step // (steps // PARTS)
+            here = pl.ds(part * (steps // PARTS), steps // PARTS)
+            leaving.append(
+                pltpu.make_async_copy(entry_ref.at[here], entry_out.at[here], out_sem.at[part])
+            )
+            leaving[-1].start()
         gates = beside(r_ref, mine, GATES, GATES + GATE_ROWS)
         cum = dot(gates, upper, (1, 0))
         cum = cum[0:1] + cum[1:2] + cum[2:3]
@@ -205,6 +230,8 @@
             normal = keep * normal + fresh[PIECE : PIECE + 1] + fresh[PIECE + 1 : PIECE + 2]
             old_m = new_m
             start = start + total
+    for copy in leaving:
+        copy.wait()
 
 
 def near_kernel(z_ref, sum_ref, y_ref, meta_ref):
@@ -281,13 +308,21 @@
     send_ref[...] = jnp.where(first, after, before)
 
 
-def inside_kernel(r_ref, asked_ref, top_ref, low_ref, aux_ref, nin_ref, num_ref, row_ref):
+def inside_kernel(
+    r_in, asked_in, entry_in, aux_ref, nin_ref, num_ref, row_ref, r_ref, asked_ref, entry_ref, in_sem
+):
     factor = PIECE**-0.5
     before = nin_ref[...]
     before_m = before[6:7, 0:1]
     causal = iota((CHUNK, CHUNK), 0) <= iota((CHUNK, CHUNK), 1)
     row = iota((8, CHUNK), 0)
-    for step in range(num_ref.shape[0]):
+    steps = num_ref.shape[0]
+    pairs = [(r_in, r_ref), (asked_in, asked_ref), (entry_in, entry_ref)]
+    arriving = in_parts(pairs, in_sem, PARTS)
+    for step in range(steps):
+        if step % (steps // PARTS) == 0:
+            for copy in arriving[step // (steps // PARTS)]:
+                copy.wait()
         mine = chunk_blocks(r_ref, step)
         asked = beside(asked_ref, mine, 0, PIECE)
         turned = beside(r_ref, mine, 0, PIECE)
@@ -318,7 +353,7 @@
             (1, 0),
         )
         read = dot(
-            jnp.concatenate([top_ref[step], low_ref[step]], axis=1),
+            entry_ref[step],
             jnp.concatenate([asked, asked], axis=0),
             (1, 0),
         )
@@ -443,14 +478,21 @@
     )(far(queries))
     asked = lax.all_to_all(turned, "head", split_axis=0, concat_axis=0, tiled=True)
 
-    entry_top, entry_low, aux = pl.pallas_call(
+    far_spec = pl.BlockSpec(memory_space=pltpu.HBM)
+    entries = (steps, PIECE, 2 * PIECE)
+    entry, aux = pl.pallas_call(
         entries_kernel,
-        in_specs=[FAR],
-        out_specs=[FAR] * 3,
+        in_specs=[far_spec],
+        out_specs=[far_spec, FAR],
         out_shape=[
-            jax.ShapeDtypeStruct((steps, PIECE, PIECE), BF16),
-            jax.ShapeDtypeStruct((steps, PIECE, PIECE), BF16),
+            jax.ShapeDtypeStruct(entries, BF16),
             jax.ShapeDtypeStruct((steps, 8, CHUNK), F32),
+        ],
+        scratch_shapes=[
+            pltpu.VMEM(received.shape, BF16),
+            pltpu.VMEM(entries, BF16),
+            pltpu.SemaphoreType.DMA((PARTS,)),
+            pltpu.SemaphoreType.DMA((PARTS,)),
         ],
         name="entries",
     )(far(received))
@@ -501,15 +543,21 @@
 
     num, line = pl.pallas_call(
         inside_kernel,
-        in_specs=[FAR] * 6,
+        in_specs=[far_spec] * 3 + [FAR] * 2,
         out_specs=[NEAR] * 2,
         out_shape=[
             pltpu.VMEM((steps, PIECE, CHUNK), F32),
             pltpu.VMEM((steps, 8, CHUNK), F32),
         ],
+        scratch_shapes=[
+            pltpu.VMEM(received.shape, BF16),
+            pltpu.VMEM(asked.shape, BF16),
+            pltpu.VMEM(entries, BF16),
+            pltpu.SemaphoreType.DMA((3 * PARTS,)),
+        ],
         compiler_params=pltpu.CompilerParams(vmem_limit_bytes=INSIDE_LIMIT),
         name="inside",
-    )(far(received), far(asked), entry_top, entry_low, aux, normal)
+    )(far(received), far(asked), far(entry), aux, normal)
 
     return pl.pallas_call(
         finish_kernel,

time: 115 us -> 116 us (level)
  no operation moved by 1% of the time
where the time goes in v8:
time: 116 us; the launch traced here: 115 us
  blocking collectives  48.7 us (42%)
  starting transfers between devices  22.4 us (19%)
  Pallas kernels  21.8 us (19%)
  waiting for transfers between devices  21.1 us (18%)
    all_to_all x1, blocking collectives, on_device(): lax.all_to_all(packed, 'head', split_axis=0, concat_axis=0, tiled=True)  36 us
    all_to_all x1, blocking collectives, on_device(): lax.all_to_all(summary, 'seq', split_axis=0, concat_axis=0, tiled=True, a...  12.7 us
    ppermute x3, starting transfers between devices, on_device(): lax.ppermute(group_sum, 'seq', [(i, i + step) for i in range(shards - ste...  11.4 us
    all_to_all x1, waiting for transfers between devices, on_device(): lax.all_to_all(turned, 'head', split_axis=0, concat_axis=0, tiled=True)  8.11 us
    ppermute x3, waiting for transfers between devices, on_device(): lax.ppermute(group_sum, 'seq', [(i, i + step) for i in range(shards - ste...  7.87 us
    pallas_call x1, Pallas kernels, on_device(): pl.pallas_call(inside_kernel, in_specs=[far_spec] * 3 + [FAR] * 2, out_sp...  5.77 us
    pallas_call x1, Pallas kernels, on_device(): pl.pallas_call(entries_kernel, in_specs=[far_spec], out_specs=[far_spec,...  5.51 us
    all_to_all x1, waiting for transfers between devices, on_device(): lax.all_to_all(before, 'seq', split_axis=0, concat_axis=0, tiled=True, ax...  3.83 us
  transfers between devices with their start and end apart: 7, of which 5 were waited for; matrix products, arithmetic and copies ran while one was open for 0% of the time, Pallas kernels for 12%

profile of v8, /device:TPU:128, one launch (start us, length us, event | category | flops | bytes accessed | tf_op | source)
XLA Modules:
  0.0 115.1 jit_solution(18050907032365197159)
XLA Ops:
  0.0 1.9 %pack.1 = bf16[16,520,128]{2,1,0:T(8,128)(2,1)S(1)} custom-call(bf16[128,2048]{1,0:T(8,128)(2,1)} %k_in.1, bf16[128,4096]{1,0:T(8,128)(2,1)} %v_in.1, f32[8,128]{1,0:T(8,128)} %bitcast.4, f32[8,128]{1,0:T(8,128)} %bitcast.5), custom_call_target="tpu_custom_call" | custom-call | tf_op jit(solution)/shard_map/pack/pallas_call | solution.py:426
  1.9 36.0 %all_to_all.20.r_in.r_ref = bf16[16,520,128]{2,1,0:T(8,128)(2,1)S(1)} all-to-all(bf16[16,520,128]{2,1,0:T(8,128)(2,1)S(1)} %pack.1), channel_id=1, replica_groups=mesh['seq'=32,'head'=16] {'head'}, dimensions={0} | all-to-all | bytes 4259840 | tf_op jit(solution)/shard_map/all_to_all | solution.py:442
  37.9 0.0 copy-start
  37.9 1.1 summary.1
  38.9 1.9 %collective-permute-start = (f32[136,256]{1,0:T(8,128)S(1)}, f32[136,256]{1,0:T(8,128)S(1)}, u32[]{:S(2)}, u32[]{:S(2)}) collective-permute-start(f32[136,256]{1,0:T(8,128)S(1)} %get-tuple-element.23), channel_id=1, source_target_pairs={{0,16},{16,0},{32,48},{48,32},{64,80},{80,64},{96,112},{112,96},{1... | collective-permute-start | bytes 417800 | tf_op jit(solution)/shard_map/ppermute | solution.py:454
  40.8 1.3 %collective-permute-done.theirs_ref = f32[136,256]{1,0:T(8,128)S(1)} collective-permute-done((f32[136,256]{1,0:T(8,128)S(1)}, f32[136,256]{1,0:T(8,128)S(1)}, u32[]{:S(2)}, u32[]{:S(2)}) %collective-permute-start) | collective-permute-done | bytes 139296 | tf_op jit(solution)/shard_map/ppermute | solution.py:454
  42.2 0.1 pair.1
  42.3 12.7 %all_to_all.21.z_ref = f32[4,40,256]{2,1,0:T(8,128)S(1)} all-to-all(f32[4,40,256]{2,1,0:T(8,128)S(1)} %get-tuple-element.24), channel_id=1, replica_groups={{0,32,64,96},{16,48,80,112},{128,160,192,224},{144,176,208,240},{256,28..., dimensions={0} | all-to-all | bytes 327680 | tf_op jit(solution)/shard_map/all_to_all | solution.py:468
  55.0 0.7 near.1
  55.7 0.7 collective-permute-start.3
  56.4 8.8 %collective-permute-start.2 = (f32[40,256]{1,0:T(8,128)S(1)}, f32[40,256]{1,0:T(8,128)S(1)}, u32[]{:S(2)}, u32[]{:S(2)}) collective-permute-start(f32[40,256]{1,0:T(8,128)S(1)} %get-tuple-element.28), channel_id=1, source_target_pairs={{0,256},{16,272},{32,288},{48,304},{64,320},{80,336},{96,352},{112... | collective-permute-start | bytes 122888 | tf_op jit(solution)/shard_map/ppermute | solution.py:516
  65.2 1.9 %collective-permute-start.1 = (f32[40,256]{1,0:T(8,128)S(1)}, f32[40,256]{1,0:T(8,128)S(1)}, u32[]{:S(2)}, u32[]{:S(2)}) collective-permute-start(f32[40,256]{1,0:T(8,128)S(1)} %get-tuple-element.28), channel_id=1, source_target_pairs={{0,128},{16,144},{32,160},{48,176},{64,192},{80,208},{96,224},{112... | collective-permute-start | bytes 122888 | tf_op jit(solution)/shard_map/ppermute | solution.py:516
  67.1 0.0 collective-permute-done.3.refs_5_
  67.1 0.6 collective-permute-done.2.refs_4_
  67.8 7.2 %collective-permute-done.1.refs_3_ = f32[40,256]{1,0:T(8,128)S(1)} collective-permute-done((f32[40,256]{1,0:T(8,128)S(1)}, f32[40,256]{1,0:T(8,128)S(1)}, u32[]{:S(2)}, u32[]{:S(2)}) %collective-permute-start.1) | collective-permute-done | bytes 40992 | tf_op jit(solution)/shard_map/ppermute | solution.py:516
  75.0 1.6 %far.1 = (f32[4,32,256]{2,1,0:T(8,128)}, f32[8,256]{1,0:T(8,128)}) custom-call(f32[4,32,256]{2,1,0:T(8,128)} %get-tuple-element.25.refs_0_, f32[16,256]{1,0:T(8,128)} %get-tuple-element.26.refs_1_, f32[136,256]{1,0:T(8,128)S(1)} %get-tuple-element.27.refs_2_.first_ref, f32[40,256]{1,0:T(8,128)S(1)} %collective-permute-done.1.refs_3_, ...), custom_call_target="tpu_custom_call" | custom-call | tf_op jit(solution)/shard_map/far/pallas_call | solution.py:518
  76.7 0.0 copy-start.1
  76.7 3.5 %all-to-all-start.3 = ((f32[4,32,256]{2,1,0:T(8,128)}), f32[4,32,256]{2,1,0:T(8,128)S(1)}, u32[]{:S(2)}, u32[]{:S(2)}) async-start(f32[4,32,256]{2,1,0:T(8,128)} %get-tuple-element.32), calls=%async_computation.3 | async-start | bytes 262144 | tf_op jit(solution)/shard_map/all_to_all | solution.py:530
  80.1 2.2 %turn.1 = bf16[16,256,128]{2,1,0:T(8,128)(2,1)} custom-call(bf16[128,2048]{1,0:T(8,128)(2,1)} %q_ref.1), custom_call_target="tpu_custom_call" | custom-call | tf_op jit(solution)/shard_map/turn/pallas_call | solution.py:472
  82.3 0.0 copy-done
  82.3 3.8 %all-to-all-done.3 = f32[4,32,256]{2,1,0:T(8,128)S(1)} async-done(((f32[4,32,256]{2,1,0:T(8,128)}), f32[4,32,256]{2,1,0:T(8,128)S(1)}, u32[]{:S(2)}, u32[]{:S(2)}) %all-to-all-start.3) | async-done | bytes 131104 | tf_op jit(solution)/shard_map/all_to_all | solution.py:530
  86.2 3.7 %all-to-all-start = ((bf16[16,256,128]{2,1,0:T(8,128)(2,1)}), bf16[16,256,128]{2,1,0:T(8,128)(2,1)S(1)}, u32[]{:S(2)}, u32[]{:S(2)}) async-start(bf16[16,256,128]{2,1,0:T(8,128)(2,1)} %turn.1), calls=%async_computation | async-start | bytes 2097152 | tf_op jit(solution)/shard_map/all_to_all | solution.py:479
  89.8 0.0 copy-done.1
  89.8 0.1 mix.1
  89.9 1.9 %collective-permute-start.4 = (f32[128,256]{1,0:T(8,128)S(1)}, f32[128,256]{1,0:T(8,128)S(1)}, u32[]{:S(2)}, u32[]{:S(2)}) collective-permute-start(f32[128,256]{1,0:T(8,128)S(1)} %get-tuple-element.34), channel_id=1, source_target_pairs={{0,16},{16,0},{32,48},{48,32},{64,80},{80,64},{96,112},{112,96},{1... | collective-permute-start | bytes 393224 | tf_op jit(solution)/shard_map/ppermute | solution.py:542
  91.9 5.5 %entries.1 = (bf16[8,256,512]{2,1,0:T(8,128)(2,1)}, f32[8,8,256]{2,1,0:T(8,128)}) custom-call(bf16[16,520,128]{2,1,0:T(8,128)(2,1)} %copy-done), custom_call_target="tpu_custom_call" | custom-call | tf_op jit(solution)/shard_map/entries/pallas_call | solution.py:483
  97.4 8.1 %all-to-all-done.asked_in = bf16[16,256,128]{2,1,0:T(8,128)(2,1)S(1)} async-done(((bf16[16,256,128]{2,1,0:T(8,128)(2,1)}), bf16[16,256,128]{2,1,0:T(8,128)(2,1)S(1)}, u32[]{:S(2)}, u32[]{:S(2)}) %all-to-all-start) | async-done | bytes 1048608 | tf_op jit(solution)/shard_map/all_to_all | solution.py:479
  105.5 0.0 copy-start.2
  105.5 1.0 copy-done.2
  106.5 5.8 %inside.1 = (f32[8,256,256]{2,1,0:T(8,128)S(1)}, f32[8,8,256]{2,1,0:T(8,128)S(1)}) custom-call(bf16[16,520,128]{2,1,0:T(8,128)(2,1)} %copy-done, bf16[16,256,128]{2,1,0:T(8,128)(2,1)} %copy-done.2, bf16[8,256,512]{2,1,0:T(8,128)(2,1)} %get-tuple-element.20.entry_in, f32[8,8,256]{2,1,0:T(8,128)} %get-tuple-element.21.aux_ref, f32[8,256]{1,0:T(8,128)} %get-tuple-element.29.nin_ref), custom_call_target="tpu_custom_call" | custom-call | tf_op jit(solution)/shard_map/inside/pallas_call | solution.py:544
  112.3 0.0 collective-permute-done.4.came_ref
  112.3 2.8 %finish.1 = bf16[2048,256]{1,0:T(8,128)(2,1)} custom-call(bf16[16,256,128]{2,1,0:T(8,128)(2,1)} %copy-done.2, f32[8,256,256]{2,1,0:T(8,128)S(1)} %get-tuple-element.30.num_ref, f32[8,8,256]{2,1,0:T(8,128)S(1)} %get-tuple-element.31.row_ref, f32[128,256]{1,0:T(8,128)S(1)} %get-tuple-element.33.keep_ref, f32[128,256]{1,0:T(8,128)S(1)} %collective-permute-done.4.came_ref), custom_call_target="tpu_custom_call" | custom-call | tf_op jit(solution)/shard_map/finish/pallas_call | solution.py:562
Async XLA Ops:
  37.9 44.5 %copy-start = (bf16[16,520,128]{2,1,0:T(8,128)(2,1)}, bf16[16,520,128]{2,1,0:T(8,128)(2,1)S(1)}, u32[]{:S(2)}) copy-start(bf16[16,520,128]{2,1,0:T(8,128)(2,1)S(1)} %all_to_all.20.r_in.r_ref) | copy-start | bytes 6389764
  38.9 3.3 %collective-permute-start = (f32[136,256]{1,0:T(8,128)S(1)}, f32[136,256]{1,0:T(8,128)S(1)}, u32[]{:S(2)}, u32[]{:S(2)}) collective-permute-start(f32[136,256]{1,0:T(8,128)S(1)} %get-tuple-element.23), channel_id=1, source_target_pairs={{0,16},{16,0},{32,48},{48,32},{64,80},{80,64},{96,112},{112,96},{1... | collective-permute-start | bytes 417800 | tf_op jit(solution)/shard_map/ppermute | solution.py:454
  55.7 11.4 %collective-permute-start.3 = (f32[40,256]{1,0:T(8,128)S(1)}, f32[40,256]{1,0:T(8,128)S(1)}, u32[]{:S(2)}, u32[]{:S(2)}) collective-permute-start(f32[40,256]{1,0:T(8,128)S(1)} %get-tuple-element.28), channel_id=1, source_target_pairs={{0,384},{16,400},{32,416},{48,432},{64,448},{80,464},{96,480},{112... | collective-permute-start | bytes 122888 | tf_op jit(solution)/shard_map/ppermute | solution.py:516
  56.4 11.4 %collective-permute-start.2 = (f32[40,256]{1,0:T(8,128)S(1)}, f32[40,256]{1,0:T(8,128)S(1)}, u32[]{:S(2)}, u32[]{:S(2)}) collective-permute-start(f32[40,256]{1,0:T(8,128)S(1)} %get-tuple-element.28), channel_id=1, source_target_pairs={{0,256},{16,272},{32,288},{48,304},{64,320},{80,336},{96,352},{112... | collective-permute-start | bytes 122888 | tf_op jit(solution)/shard_map/ppermute | solution.py:516
  65.2 9.8 %collective-permute-start.1 = (f32[40,256]{1,0:T(8,128)S(1)}, f32[40,256]{1,0:T(8,128)S(1)}, u32[]{:S(2)}, u32[]{:S(2)}) collective-permute-start(f32[40,256]{1,0:T(8,128)S(1)} %get-tuple-element.28), channel_id=1, source_target_pairs={{0,128},{16,144},{32,160},{48,176},{64,192},{80,208},{96,224},{112... | collective-permute-start | bytes 122888 | tf_op jit(solution)/shard_map/ppermute | solution.py:516
  76.7 13.2 %copy-start.1 = (f32[8,256]{1,0:T(8,128)S(1)}, f32[8,256]{1,0:T(8,128)}, u32[]{:S(2)}) copy-start(f32[8,256]{1,0:T(8,128)} %get-tuple-element.29.nin_ref) | copy-start | bytes 24580
  76.7 9.5 %all-to-all-start.3 = ((f32[4,32,256]{2,1,0:T(8,128)}), f32[4,32,256]{2,1,0:T(8,128)S(1)}, u32[]{:S(2)}, u32[]{:S(2)}) async-start(f32[4,32,256]{2,1,0:T(8,128)} %get-tuple-element.32), calls=%async_computation.3 | async-start | bytes 262144 | tf_op jit(solution)/shard_map/all_to_all | solution.py:530
  86.2 19.3 %all-to-all-start = ((bf16[16,256,128]{2,1,0:T(8,128)(2,1)}), bf16[16,256,128]{2,1,0:T(8,128)(2,1)S(1)}, u32[]{:S(2)}, u32[]{:S(2)}) async-start(bf16[16,256,128]{2,1,0:T(8,128)(2,1)} %turn.1), calls=%async_computation | async-start | bytes 2097152 | tf_op jit(solution)/shard_map/all_to_all | solution.py:479
  89.9 22.3 %collective-permute-start.4 = (f32[128,256]{1,0:T(8,128)S(1)}, f32[128,256]{1,0:T(8,128)S(1)}, u32[]{:S(2)}, u32[]{:S(2)}) collective-permute-start(f32[128,256]{1,0:T(8,128)S(1)} %get-tuple-element.34), channel_id=1, source_target_pairs={{0,16},{16,0},{32,48},{48,32},{64,80},{80,64},{96,112},{112,96},{1... | collective-permute-start | bytes 393224 | tf_op jit(solution)/shard_map/ppermute | solution.py:542
  105.5 1.0 copy-start.2

commit v9 on v8

--- a/solution.py
+++ b/solution.py
@@ -309,7 +309,7 @@
 
 
 def inside_kernel(
-    r_in, asked_in, entry_in, aux_ref, nin_ref, num_ref, row_ref, r_ref, asked_ref, entry_ref, in_sem
+    r_in, asked_ref, entry_in, aux_ref, nin_ref, num_ref, row_ref, r_ref, entry_ref, in_sem
 ):
     factor = PIECE**-0.5
     before = nin_ref[...]
@@ -317,7 +317,7 @@
     causal = iota((CHUNK, CHUNK), 0) <= iota((CHUNK, CHUNK), 1)
     row = iota((8, CHUNK), 0)
     steps = num_ref.shape[0]
-    pairs = [(r_in, r_ref), (asked_in, asked_ref), (entry_in, entry_ref)]
+    pairs = [(r_in, r_ref), (entry_in, entry_ref)]
     arriving = in_parts(pairs, in_sem, PARTS)
     for step in range(steps):
         if step % (steps // PARTS) == 0:
@@ -543,7 +543,7 @@
 
     num, line = pl.pallas_call(
         inside_kernel,
-        in_specs=[far_spec] * 3 + [FAR] * 2,
+        in_specs=[far_spec, NEAR, far_spec, FAR, FAR],
         out_specs=[NEAR] * 2,
         out_shape=[
             pltpu.VMEM((steps, PIECE, CHUNK), F32),
@@ -551,13 +551,12 @@
         ],
         scratch_shapes=[
             pltpu.VMEM(received.shape, BF16),
-            pltpu.VMEM(asked.shape, BF16),
             pltpu.VMEM(entries, BF16),
-            pltpu.SemaphoreType.DMA((3 * PARTS,)),
+            pltpu.SemaphoreType.DMA((2 * PARTS,)),
         ],
         compiler_params=pltpu.CompilerParams(vmem_limit_bytes=INSIDE_LIMIT),
         name="inside",
-    )(far(received), far(asked), far(entry), aux, normal)
+    )(far(received), near(asked), far(entry), aux, normal)
 
     return pl.pallas_call(
         finish_kernel,

time: 116 us -> 115 us (level)
  no operation moved by 1% of the time
where the time goes in v9:
time: 115 us; the launch traced here: 114 us
  blocking collectives  48.7 us (42%)
  starting transfers between devices  22.4 us (19%)
  Pallas kernels  21.7 us (19%)
  waiting for transfers between devices  21.1 us (18%)
    all_to_all x1, blocking collectives, on_device(): lax.all_to_all(packed, 'head', split_axis=0, concat_axis=0, tiled=True)  36 us
    all_to_all x1, blocking collectives, on_device(): lax.all_to_all(summary, 'seq', split_axis=0, concat_axis=0, tiled=True, a...  12.7 us
    ppermute x3, starting transfers between devices, on_device(): lax.ppermute(group_sum, 'seq', [(i, i + step) for i in range(shards - ste...  11.4 us
    all_to_all x1, waiting for transfers between devices, on_device(): lax.all_to_all(turned, 'head', split_axis=0, concat_axis=0, tiled=True)  8.11 us
    ppermute x3, waiting for transfers between devices, on_device(): lax.ppermute(group_sum, 'seq', [(i, i + step) for i in range(shards - ste...  7.87 us
    pallas_call x1, Pallas kernels, on_device(): pl.pallas_call(inside_kernel, in_specs=[far_spec, NEAR, far_spec, FAR, FA...  5.64 us
    pallas_call x1, Pallas kernels, on_device(): pl.pallas_call(entries_kernel, in_specs=[far_spec], out_specs=[far_spec,...  5.51 us
    all_to_all x1, waiting for transfers between devices, on_device(): lax.all_to_all(before, 'seq', split_axis=0, concat_axis=0, tiled=True, ax...  3.83 us
  transfers between devices with their start and end apart: 7, of which 5 were waited for; matrix products, arithmetic and copies ran while one was open for 0% of the time, Pallas kernels for 12%

profile of v9, /device:TPU:128, one launch (start us, length us, event | category | flops | bytes accessed | tf_op | source)
XLA Modules:
  0.0 114.0 jit_solution(18160298103009119169)
XLA Ops:
  0.0 1.9 %pack.1 = bf16[16,520,128]{2,1,0:T(8,128)(2,1)S(1)} custom-call(bf16[128,2048]{1,0:T(8,128)(2,1)} %k_in.1, bf16[128,4096]{1,0:T(8,128)(2,1)} %v_in.1, f32[8,128]{1,0:T(8,128)} %bitcast.4, f32[8,128]{1,0:T(8,128)} %bitcast.5), custom_call_target="tpu_custom_call" | custom-call | tf_op jit(solution)/shard_map/pack/pallas_call | solution.py:426
  1.9 36.0 %all_to_all.20.r_in.r_ref = bf16[16,520,128]{2,1,0:T(8,128)(2,1)S(1)} all-to-all(bf16[16,520,128]{2,1,0:T(8,128)(2,1)S(1)} %pack.1), channel_id=1, replica_groups=mesh['seq'=32,'head'=16] {'head'}, dimensions={0} | all-to-all | bytes 4259840 | tf_op jit(solution)/shard_map/all_to_all | solution.py:442
  37.9 0.0 copy-start
  37.9 1.1 summary.1
  38.9 1.9 %collective-permute-start = (f32[136,256]{1,0:T(8,128)S(1)}, f32[136,256]{1,0:T(8,128)S(1)}, u32[]{:S(2)}, u32[]{:S(2)}) collective-permute-start(f32[136,256]{1,0:T(8,128)S(1)} %get-tuple-element.23), channel_id=1, source_target_pairs={{0,16},{16,0},{32,48},{48,32},{64,80},{80,64},{96,112},{112,96},{1... | collective-permute-start | bytes 417800 | tf_op jit(solution)/shard_map/ppermute | solution.py:454
  40.8 1.3 %collective-permute-done.theirs_ref = f32[136,256]{1,0:T(8,128)S(1)} collective-permute-done((f32[136,256]{1,0:T(8,128)S(1)}, f32[136,256]{1,0:T(8,128)S(1)}, u32[]{:S(2)}, u32[]{:S(2)}) %collective-permute-start) | collective-permute-done | bytes 139296 | tf_op jit(solution)/shard_map/ppermute | solution.py:454
  42.2 0.1 pair.1
  42.3 12.7 %all_to_all.21.z_ref = f32[4,40,256]{2,1,0:T(8,128)S(1)} all-to-all(f32[4,40,256]{2,1,0:T(8,128)S(1)} %get-tuple-element.24), channel_id=1, replica_groups={{0,32,64,96},{16,48,80,112},{128,160,192,224},{144,176,208,240},{256,28..., dimensions={0} | all-to-all | bytes 327680 | tf_op jit(solution)/shard_map/all_to_all | solution.py:468
  55.0 0.7 near.1
  55.7 0.7 collective-permute-start.3
  56.4 8.8 %collective-permute-start.2 = (f32[40,256]{1,0:T(8,128)S(1)}, f32[40,256]{1,0:T(8,128)S(1)}, u32[]{:S(2)}, u32[]{:S(2)}) collective-permute-start(f32[40,256]{1,0:T(8,128)S(1)} %get-tuple-element.28), channel_id=1, source_target_pairs={{0,256},{16,272},{32,288},{48,304},{64,320},{80,336},{96,352},{112... | collective-permute-start | bytes 122888 | tf_op jit(solution)/shard_map/ppermute | solution.py:516
  65.2 1.9 %collective-permute-start.1 = (f32[40,256]{1,0:T(8,128)S(1)}, f32[40,256]{1,0:T(8,128)S(1)}, u32[]{:S(2)}, u32[]{:S(2)}) collective-permute-start(f32[40,256]{1,0:T(8,128)S(1)} %get-tuple-element.28), channel_id=1, source_target_pairs={{0,128},{16,144},{32,160},{48,176},{64,192},{80,208},{96,224},{112... | collective-permute-start | bytes 122888 | tf_op jit(solution)/shard_map/ppermute | solution.py:516
  67.1 0.0 collective-permute-done.3.refs_5_
  67.1 0.6 collective-permute-done.2.refs_4_
  67.8 7.2 %collective-permute-done.1.refs_3_ = f32[40,256]{1,0:T(8,128)S(1)} collective-permute-done((f32[40,256]{1,0:T(8,128)S(1)}, f32[40,256]{1,0:T(8,128)S(1)}, u32[]{:S(2)}, u32[]{:S(2)}) %collective-permute-start.1) | collective-permute-done | bytes 40992 | tf_op jit(solution)/shard_map/ppermute | solution.py:516
  75.0 1.6 %far.1 = (f32[4,32,256]{2,1,0:T(8,128)}, f32[8,256]{1,0:T(8,128)}) custom-call(f32[4,32,256]{2,1,0:T(8,128)} %get-tuple-element.25.refs_0_, f32[16,256]{1,0:T(8,128)} %get-tuple-element.26.refs_1_, f32[136,256]{1,0:T(8,128)S(1)} %get-tuple-element.27.refs_2_.first_ref, f32[40,256]{1,0:T(8,128)S(1)} %collective-permute-done.1.refs_3_, ...), custom_call_target="tpu_custom_call" | custom-call | tf_op jit(solution)/shard_map/far/pallas_call | solution.py:518
  76.7 0.0 copy-start.2
  76.7 3.5 %all-to-all-start.3 = ((f32[4,32,256]{2,1,0:T(8,128)}), f32[4,32,256]{2,1,0:T(8,128)S(1)}, u32[]{:S(2)}, u32[]{:S(2)}) async-start(f32[4,32,256]{2,1,0:T(8,128)} %get-tuple-element.32), calls=%async_computation.3 | async-start | bytes 262144 | tf_op jit(solution)/shard_map/all_to_all | solution.py:530
  80.1 2.2 %turn.1 = bf16[16,256,128]{2,1,0:T(8,128)(2,1)} custom-call(bf16[128,2048]{1,0:T(8,128)(2,1)} %q_ref.1), custom_call_target="tpu_custom_call" | custom-call | tf_op jit(solution)/shard_map/turn/pallas_call | solution.py:472
  82.3 0.0 copy-done
  82.3 3.8 %all-to-all-done.3 = f32[4,32,256]{2,1,0:T(8,128)S(1)} async-done(((f32[4,32,256]{2,1,0:T(8,128)}), f32[4,32,256]{2,1,0:T(8,128)S(1)}, u32[]{:S(2)}, u32[]{:S(2)}) %all-to-all-start.3) | async-done | bytes 131104 | tf_op jit(solution)/shard_map/all_to_all | solution.py:530
  86.2 3.7 %all-to-all-start = ((bf16[16,256,128]{2,1,0:T(8,128)(2,1)}), bf16[16,256,128]{2,1,0:T(8,128)(2,1)S(1)}, u32[]{:S(2)}, u32[]{:S(2)}) async-start(bf16[16,256,128]{2,1,0:T(8,128)(2,1)} %turn.1), calls=%async_computation | async-start | bytes 2097152 | tf_op jit(solution)/shard_map/all_to_all | solution.py:479
  89.8 0.0 copy-done.2
  89.8 0.1 mix.1
  89.9 1.9 %collective-permute-start.4 = (f32[128,256]{1,0:T(8,128)S(1)}, f32[128,256]{1,0:T(8,128)S(1)}, u32[]{:S(2)}, u32[]{:S(2)}) collective-permute-start(f32[128,256]{1,0:T(8,128)S(1)} %get-tuple-element.34), channel_id=1, source_target_pairs={{0,16},{16,0},{32,48},{48,32},{64,80},{80,64},{96,112},{112,96},{1... | collective-permute-start | bytes 393224 | tf_op jit(solution)/shard_map/ppermute | solution.py:542
  91.9 5.5 %entries.1 = (bf16[8,256,512]{2,1,0:T(8,128)(2,1)}, f32[8,8,256]{2,1,0:T(8,128)}) custom-call(bf16[16,520,128]{2,1,0:T(8,128)(2,1)} %copy-done), custom_call_target="tpu_custom_call" | custom-call | tf_op jit(solution)/shard_map/entries/pallas_call | solution.py:483
  97.4 8.1 %all-to-all-done.asked_ref.asked_in = bf16[16,256,128]{2,1,0:T(8,128)(2,1)S(1)} async-done(((bf16[16,256,128]{2,1,0:T(8,128)(2,1)}), bf16[16,256,128]{2,1,0:T(8,128)(2,1)S(1)}, u32[]{:S(2)}, u32[]{:S(2)}) %all-to-all-start) | async-done | bytes 1048608 | tf_op jit(solution)/shard_map/all_to_all | solution.py:479
  105.5 0.0 copy-start.1
  105.5 5.6 %inside.1 = (f32[8,256,256]{2,1,0:T(8,128)S(1)}, f32[8,8,256]{2,1,0:T(8,128)S(1)}) custom-call(bf16[16,520,128]{2,1,0:T(8,128)(2,1)} %copy-done, bf16[16,256,128]{2,1,0:T(8,128)(2,1)S(1)} %all-to-all-done.asked_ref.asked_in, bf16[8,256,512]{2,1,0:T(8,128)(2,1)} %get-tuple-element.20.entry_in, f32[8,8,256]{2,1,0:T(8,128)} %get-tuple-element.21.aux_ref, ...), custom_call_target="tpu_custom_call" | custom-call | tf_op jit(solution)/shard_map/inside/pallas_call | solution.py:544
  111.1 0.0 copy-done.1
  111.2 0.0 collective-permute-done.4.came_ref
  111.2 2.8 %finish.1 = bf16[2048,256]{1,0:T(8,128)(2,1)} custom-call(bf16[16,256,128]{2,1,0:T(8,128)(2,1)} %copy-done.1, f32[8,256,256]{2,1,0:T(8,128)S(1)} %get-tuple-element.30.num_ref, f32[8,8,256]{2,1,0:T(8,128)S(1)} %get-tuple-element.31.row_ref, f32[128,256]{1,0:T(8,128)S(1)} %get-tuple-element.33.keep_ref, f32[128,256]{1,0:T(8,128)S(1)} %collective-permute-done.4.came_ref), custom_call_target="tpu_custom_call" | custom-call | tf_op jit(solution)/shard_map/finish/pallas_call | solution.py:561
Async XLA Ops:
  37.9 44.5 %copy-start = (bf16[16,520,128]{2,1,0:T(8,128)(2,1)}, bf16[16,520,128]{2,1,0:T(8,128)(2,1)S(1)}, u32[]{:S(2)}) copy-start(bf16[16,520,128]{2,1,0:T(8,128)(2,1)S(1)} %all_to_all.20.r_in.r_ref) | copy-start | bytes 6389764
  38.9 3.3 %collective-permute-start = (f32[136,256]{1,0:T(8,128)S(1)}, f32[136,256]{1,0:T(8,128)S(1)}, u32[]{:S(2)}, u32[]{:S(2)}) collective-permute-start(f32[136,256]{1,0:T(8,128)S(1)} %get-tuple-element.23), channel_id=1, source_target_pairs={{0,16},{16,0},{32,48},{48,32},{64,80},{80,64},{96,112},{112,96},{1... | collective-permute-start | bytes 417800 | tf_op jit(solution)/shard_map/ppermute | solution.py:454
  55.7 11.4 %collective-permute-start.3 = (f32[40,256]{1,0:T(8,128)S(1)}, f32[40,256]{1,0:T(8,128)S(1)}, u32[]{:S(2)}, u32[]{:S(2)}) collective-permute-start(f32[40,256]{1,0:T(8,128)S(1)} %get-tuple-element.28), channel_id=1, source_target_pairs={{0,384},{16,400},{32,416},{48,432},{64,448},{80,464},{96,480},{112... | collective-permute-start | bytes 122888 | tf_op jit(solution)/shard_map/ppermute | solution.py:516
  56.4 11.4 %collective-permute-start.2 = (f32[40,256]{1,0:T(8,128)S(1)}, f32[40,256]{1,0:T(8,128)S(1)}, u32[]{:S(2)}, u32[]{:S(2)}) collective-permute-start(f32[40,256]{1,0:T(8,128)S(1)} %get-tuple-element.28), channel_id=1, source_target_pairs={{0,256},{16,272},{32,288},{48,304},{64,320},{80,336},{96,352},{112... | collective-permute-start | bytes 122888 | tf_op jit(solution)/shard_map/ppermute | solution.py:516
  65.2 9.8 %collective-permute-start.1 = (f32[40,256]{1,0:T(8,128)S(1)}, f32[40,256]{1,0:T(8,128)S(1)}, u32[]{:S(2)}, u32[]{:S(2)}) collective-permute-start(f32[40,256]{1,0:T(8,128)S(1)} %get-tuple-element.28), channel_id=1, source_target_pairs={{0,128},{16,144},{32,160},{48,176},{64,192},{80,208},{96,224},{112... | collective-permute-start | bytes 122888 | tf_op jit(solution)/shard_map/ppermute | solution.py:516
  76.7 13.2 %copy-start.2 = (f32[8,256]{1,0:T(8,128)S(1)}, f32[8,256]{1,0:T(8,128)}, u32[]{:S(2)}) copy-start(f32[8,256]{1,0:T(8,128)} %get-tuple-element.29.nin_ref) | copy-start | bytes 24580
  76.7 9.5 %all-to-all-start.3 = ((f32[4,32,256]{2,1,0:T(8,128)}), f32[4,32,256]{2,1,0:T(8,128)S(1)}, u32[]{:S(2)}, u32[]{:S(2)}) async-start(f32[4,32,256]{2,1,0:T(8,128)} %get-tuple-element.32), calls=%async_computation.3 | async-start | bytes 262144 | tf_op jit(solution)/shard_map/all_to_all | solution.py:530
  86.2 19.3 %all-to-all-start = ((bf16[16,256,128]{2,1,0:T(8,128)(2,1)}), bf16[16,256,128]{2,1,0:T(8,128)(2,1)S(1)}, u32[]{:S(2)}, u32[]{:S(2)}) async-start(bf16[16,256,128]{2,1,0:T(8,128)(2,1)} %turn.1), calls=%async_computation | async-start | bytes 2097152 | tf_op jit(solution)/shard_map/all_to_all | solution.py:479
  89.9 21.2 %collective-permute-start.4 = (f32[128,256]{1,0:T(8,128)S(1)}, f32[128,256]{1,0:T(8,128)S(1)}, u32[]{:S(2)}, u32[]{:S(2)}) collective-permute-start(f32[128,256]{1,0:T(8,128)S(1)} %get-tuple-element.34), channel_id=1, source_target_pairs={{0,16},{16,0},{32,48},{48,32},{64,80},{80,64},{96,112},{112,96},{1... | collective-permute-start | bytes 393224 | tf_op jit(solution)/shard_map/ppermute | solution.py:542
  105.5 5.7 %copy-start.1 = (bf16[16,256,128]{2,1,0:T(8,128)(2,1)}, bf16[16,256,128]{2,1,0:T(8,128)(2,1)S(1)}, u32[]{:S(2)}) copy-start(bf16[16,256,128]{2,1,0:T(8,128)(2,1)S(1)} %all-to-all-done.asked_ref.asked_in) | copy-start | bytes 3145732

commit v10 on v9

--- a/solution.py
+++ b/solution.py
@@ -234,16 +234,14 @@
         copy.wait()
 
 
-def near_kernel(z_ref, sum_ref, y_ref, meta_ref):
+def near_states(z_ref):
     count, slab = z_ref.shape[0], z_ref.shape[1] - 8
     state = jnp.zeros((slab, PIECE), F32)
     normal = jnp.zeros((1, PIECE), F32)
     old_m = jnp.full((1, 1), VERY_NEGATIVE, F32)
     total = jnp.zeros((1, 1), F32)
+    states = [(state, normal, old_m, total)]
     for i in range(count):
-        y_ref[i] = state
-        for n, x in enumerate((old_m, total, normal)):
-            meta_ref[n * count + i : n * count + i + 1, :] = jnp.broadcast_to(x, (1, PIECE))
         rest = z_ref[i, slab:, :]
         m, f = scalar(rest, 1), scalar(rest, 2)
         new_m = jnp.maximum(old_m + f, m)
@@ -252,14 +250,21 @@
         normal = keep * normal + take * rest[0:1]
         old_m = new_m
         total = total + f
+        states.append((state, normal, old_m, total))
+    return states
+
+
+def near_kernel(z_ref, sum_ref):
+    slab = z_ref.shape[1] - 8
+    state, normal, m, total = near_states(z_ref)[-1]
     place = iota((8, PIECE), 0)
     sum_ref[0:slab, :] = state
-    sum_ref[slab:, :] = jnp.where(place == 0, normal, jnp.where(place == 1, old_m, total))
+    sum_ref[slab:, :] = jnp.where(place == 0, normal, jnp.where(place == 1, m, total))
 
 
 def far_kernel(*refs):
-    y_ref, meta_ref, first_ref, *ahead, out_ref, nin_ref = refs
-    count, slab = y_ref.shape[0], y_ref.shape[1]
+    z_ref, first_ref, *ahead, out_ref, nin_ref = refs
+    count, slab = z_ref.shape[0], z_ref.shape[1] - 8
     chip = lax.axis_index("seq") // 2
     near_at, group = lax.rem(chip, count), chip // count
     second = jnp.logical_not(first_core())
@@ -276,15 +281,15 @@
         state = keep * state + take * ahead[d - 1][0:slab, :]
         normal = keep * normal + take * rest[0:1]
         old_m = new_m
-    meta = meta_ref[...]
+    local = near_states(z_ref)
     own_m = jnp.full((1, 1), VERY_NEGATIVE, F32)
     own_n = jnp.zeros((1, PIECE), F32)
     for i in range(count):
-        m, f = scalar(meta, i), scalar(meta, count + i)
+        near_state, near_normal, m, f = local[i]
         new_m = jnp.maximum(old_m + f, m)
         keep, take = jnp.exp(old_m + f - new_m), jnp.exp(m - new_m)
-        out_ref[i] = keep * state + take * y_ref[i]
-        n = keep * normal + take * meta[2 * count + i : 2 * count + i + 1]
+        out_ref[i] = keep * state + take * near_state
+        n = keep * normal + take * near_normal
         own_m = jnp.where(near_at == i, new_m, own_m)
         own_n = jnp.where(near_at == i, n, own_n)
     first_m = scalar(first_ref, HALF + 1)
@@ -497,16 +502,12 @@
         name="entries",
     )(far(received))
 
-    group_sum, local, meta = pl.pallas_call(
+    group_sum = pl.pallas_call(
         near_kernel,
         in_specs=[NEAR],
-        out_specs=[NEAR, FAR, FAR],
-        out_shape=[
-            pltpu.VMEM((slab + 8, PIECE), F32),
-            jax.ShapeDtypeStruct((close, slab, PIECE), F32),
-            jax.ShapeDtypeStruct((16, PIECE), F32),
-        ],
-        compiler_params=pltpu.CompilerParams(vmem_limit_bytes=FAR_LIMIT),
+        out_specs=NEAR,
+        out_shape=pltpu.VMEM((slab + 8, PIECE), F32),
+        compiler_params=PARAMS,
         name="near",
     )(near(spread))
 
@@ -517,7 +518,7 @@
 
     before, normal = pl.pallas_call(
         far_kernel,
-        in_specs=[FAR, FAR] + [NEAR] * (1 + len(ahead)),
+        in_specs=[FAR] + [NEAR] * (1 + len(ahead)),
         out_specs=[FAR] * 2,
         out_shape=[
             jax.ShapeDtypeStruct((close, slab, PIECE), F32),
@@ -525,7 +526,7 @@
         ],
         compiler_params=pltpu.CompilerParams(vmem_limit_bytes=FAR_LIMIT),
         name="far",
-    )(local, meta, near(first), *(near(a) for a in ahead))
+    )(spread, near(first), *(near(a) for a in ahead))
 
     back = lax.all_to_all(
         before, "seq", split_axis=0, concat_axis=0, tiled=True, axis_index_groups=groups

time: 115 us -> 114 us (level)
  no operation moved by 1% of the time
where the time goes in v10:
time: 114 us; the launch traced here: 113 us
  blocking collectives  48.7 us (43%)
  starting transfers between devices  22.4 us (20%)
  Pallas kernels  21.1 us (19%)
  waiting for transfers between devices  21.1 us (19%)
    all_to_all x1, blocking collectives, on_device(): lax.all_to_all(packed, 'head', split_axis=0, concat_axis=0, tiled=True)  36 us
    all_to_all x1, blocking collectives, on_device(): lax.all_to_all(summary, 'seq', split_axis=0, concat_axis=0, tiled=True, a...  12.7 us
    ppermute x3, starting transfers between devices, on_device(): lax.ppermute(group_sum, 'seq', [(i, i + step) for i in range(shards - ste...  11.4 us
    all_to_all x1, waiting for transfers between devices, on_device(): lax.all_to_all(turned, 'head', split_axis=0, concat_axis=0, tiled=True)  8.1 us
    ppermute x3, waiting for transfers between devices, on_device(): lax.ppermute(group_sum, 'seq', [(i, i + step) for i in range(shards - ste...  7.87 us
    pallas_call x1, Pallas kernels, on_device(): pl.pallas_call(inside_kernel, in_specs=[far_spec, NEAR, far_spec, FAR, FA...  5.64 us
    pallas_call x1, Pallas kernels, on_device(): pl.pallas_call(entries_kernel, in_specs=[far_spec], out_specs=[far_spec,...  5.51 us
    all_to_all x1, waiting for transfers between devices, on_device(): lax.all_to_all(before, 'seq', split_axis=0, concat_axis=0, tiled=True, ax...  3.83 us
  transfers between devices with their start and end apart: 7, of which 5 were waited for; matrix products, arithmetic and copies ran while one was open for 0% of the time, Pallas kernels for 12%

profile of v10, /device:TPU:128, one launch (start us, length us, event | category | flops | bytes accessed | tf_op | source)
XLA Modules:
  0.0 113.4 jit_solution(7977430707539831720)
XLA Ops:
  0.0 1.9 %pack.1 = bf16[16,520,128]{2,1,0:T(8,128)(2,1)S(1)} custom-call(bf16[128,2048]{1,0:T(8,128)(2,1)} %k_in.1, bf16[128,4096]{1,0:T(8,128)(2,1)} %v_in.1, f32[8,128]{1,0:T(8,128)} %bitcast.4, f32[8,128]{1,0:T(8,128)} %bitcast.5), custom_call_target="tpu_custom_call" | custom-call | tf_op jit(solution)/shard_map/pack/pallas_call | solution.py:431
  1.9 36.0 %all_to_all.20.r_in.r_ref = bf16[16,520,128]{2,1,0:T(8,128)(2,1)S(1)} all-to-all(bf16[16,520,128]{2,1,0:T(8,128)(2,1)S(1)} %pack.1), channel_id=1, replica_groups=mesh['seq'=32,'head'=16] {'head'}, dimensions={0} | all-to-all | bytes 4259840 | tf_op jit(solution)/shard_map/all_to_all | solution.py:447
  37.9 0.0 copy-start
  37.9 1.1 summary.1
  38.9 1.9 %collective-permute-start = (f32[136,256]{1,0:T(8,128)S(1)}, f32[136,256]{1,0:T(8,128)S(1)}, u32[]{:S(2)}, u32[]{:S(2)}) collective-permute-start(f32[136,256]{1,0:T(8,128)S(1)} %get-tuple-element.20), channel_id=1, source_target_pairs={{0,16},{16,0},{32,48},{48,32},{64,80},{80,64},{96,112},{112,96},{1... | collective-permute-start | bytes 417800 | tf_op jit(solution)/shard_map/ppermute | solution.py:459
  40.8 1.3 %collective-permute-done.theirs_ref = f32[136,256]{1,0:T(8,128)S(1)} collective-permute-done((f32[136,256]{1,0:T(8,128)S(1)}, f32[136,256]{1,0:T(8,128)S(1)}, u32[]{:S(2)}, u32[]{:S(2)}) %collective-permute-start) | collective-permute-done | bytes 139296 | tf_op jit(solution)/shard_map/ppermute | solution.py:459
  42.2 0.1 pair.1
  42.3 12.7 %all_to_all.21.z_ref.refs_0_ = f32[4,40,256]{2,1,0:T(8,128)S(1)} all-to-all(f32[4,40,256]{2,1,0:T(8,128)S(1)} %get-tuple-element.21), channel_id=1, replica_groups={{0,32,64,96},{16,48,80,112},{128,160,192,224},{144,176,208,240},{256,28..., dimensions={0} | all-to-all | bytes 327680 | tf_op jit(solution)/shard_map/all_to_all | solution.py:473
  55.0 0.0 copy-start.2
  55.0 0.1 near.1
  55.1 0.7 collective-permute-start.3
  55.7 8.8 %collective-permute-start.2 = (f32[40,256]{1,0:T(8,128)S(1)}, f32[40,256]{1,0:T(8,128)S(1)}, u32[]{:S(2)}, u32[]{:S(2)}) collective-permute-start(f32[40,256]{1,0:T(8,128)S(1)} %near.1), channel_id=1, source_target_pairs={{0,256},{16,272},{32,288},{48,304},{64,320},{80,336},{96,352},{112... | collective-permute-start | bytes 122888 | tf_op jit(solution)/shard_map/ppermute | solution.py:517
  64.6 1.9 %collective-permute-start.1 = (f32[40,256]{1,0:T(8,128)S(1)}, f32[40,256]{1,0:T(8,128)S(1)}, u32[]{:S(2)}, u32[]{:S(2)}) collective-permute-start(f32[40,256]{1,0:T(8,128)S(1)} %near.1), channel_id=1, source_target_pairs={{0,128},{16,144},{32,160},{48,176},{64,192},{80,208},{96,224},{112... | collective-permute-start | bytes 122888 | tf_op jit(solution)/shard_map/ppermute | solution.py:517
  66.5 0.0 collective-permute-done.3.refs_4_
  66.5 0.6 collective-permute-done.2.refs_3_
  67.2 7.2 %collective-permute-done.1.refs_2_ = f32[40,256]{1,0:T(8,128)S(1)} collective-permute-done((f32[40,256]{1,0:T(8,128)S(1)}, f32[40,256]{1,0:T(8,128)S(1)}, u32[]{:S(2)}, u32[]{:S(2)}) %collective-permute-start.1) | collective-permute-done | bytes 40992 | tf_op jit(solution)/shard_map/ppermute | solution.py:517
  74.4 0.0 copy-done.2
  74.4 1.7 %far.1 = (f32[4,32,256]{2,1,0:T(8,128)}, f32[8,256]{1,0:T(8,128)}) custom-call(f32[4,40,256]{2,1,0:T(8,128)} %copy-done.2, f32[136,256]{1,0:T(8,128)S(1)} %get-tuple-element.22.refs_1_.first_ref, f32[40,256]{1,0:T(8,128)S(1)} %collective-permute-done.1.refs_2_, f32[40,256]{1,0:T(8,128)S(1)} %collective-permute-done.2.refs_3_, ...), custom_call_target="tpu_custom_call" | custom-call | tf_op jit(solution)/shard_map/far/pallas_call | solution.py:519
  76.1 3.5 %all-to-all-start.3 = ((f32[4,32,256]{2,1,0:T(8,128)}), f32[4,32,256]{2,1,0:T(8,128)S(1)}, u32[]{:S(2)}, u32[]{:S(2)}) async-start(f32[4,32,256]{2,1,0:T(8,128)} %get-tuple-element.26), calls=%async_computation.3 | async-start | bytes 262144 | tf_op jit(solution)/shard_map/all_to_all | solution.py:531
  79.5 2.2 %turn.1 = bf16[16,256,128]{2,1,0:T(8,128)(2,1)} custom-call(bf16[128,2048]{1,0:T(8,128)(2,1)} %q_ref.1), custom_call_target="tpu_custom_call" | custom-call | tf_op jit(solution)/shard_map/turn/pallas_call | solution.py:477
  81.8 0.0 copy-done
  81.8 3.8 %all-to-all-done.3 = f32[4,32,256]{2,1,0:T(8,128)S(1)} async-done(((f32[4,32,256]{2,1,0:T(8,128)}), f32[4,32,256]{2,1,0:T(8,128)S(1)}, u32[]{:S(2)}, u32[]{:S(2)}) %all-to-all-start.3) | async-done | bytes 131104 | tf_op jit(solution)/shard_map/all_to_all | solution.py:531
  85.6 3.7 %all-to-all-start = ((bf16[16,256,128]{2,1,0:T(8,128)(2,1)}), bf16[16,256,128]{2,1,0:T(8,128)(2,1)S(1)}, u32[]{:S(2)}, u32[]{:S(2)}) async-start(bf16[16,256,128]{2,1,0:T(8,128)(2,1)} %turn.1), calls=%async_computation | async-start | bytes 2097152 | tf_op jit(solution)/shard_map/all_to_all | solution.py:484
  89.2 0.0 copy-done.3
  89.3 0.1 mix.1
  89.4 1.9 %collective-permute-start.4 = (f32[128,256]{1,0:T(8,128)S(1)}, f32[128,256]{1,0:T(8,128)S(1)}, u32[]{:S(2)}, u32[]{:S(2)}) collective-permute-start(f32[128,256]{1,0:T(8,128)S(1)} %get-tuple-element.28), channel_id=1, source_target_pairs={{0,16},{16,0},{32,48},{48,32},{64,80},{80,64},{96,112},{112,96},{1... | collective-permute-start | bytes 393224 | tf_op jit(solution)/shard_map/ppermute | solution.py:543
  91.3 5.5 %entries.1 = (bf16[8,256,512]{2,1,0:T(8,128)(2,1)}, f32[8,8,256]{2,1,0:T(8,128)}) custom-call(bf16[16,520,128]{2,1,0:T(8,128)(2,1)} %copy-done), custom_call_target="tpu_custom_call" | custom-call | tf_op jit(solution)/shard_map/entries/pallas_call | solution.py:488
  96.8 8.1 %all-to-all-done.asked_ref.asked_in = bf16[16,256,128]{2,1,0:T(8,128)(2,1)S(1)} async-done(((bf16[16,256,128]{2,1,0:T(8,128)(2,1)}), bf16[16,256,128]{2,1,0:T(8,128)(2,1)S(1)}, u32[]{:S(2)}, u32[]{:S(2)}) %all-to-all-start) | async-done | bytes 1048608 | tf_op jit(solution)/shard_map/all_to_all | solution.py:484
  104.9 5.6 %inside.1 = (f32[8,256,256]{2,1,0:T(8,128)S(1)}, f32[8,8,256]{2,1,0:T(8,128)S(1)}) custom-call(bf16[16,520,128]{2,1,0:T(8,128)(2,1)} %copy-done, bf16[16,256,128]{2,1,0:T(8,128)(2,1)S(1)} %all-to-all-done.asked_ref.asked_in, bf16[8,256,512]{2,1,0:T(8,128)(2,1)} %get-tuple-element.17.entry_in, f32[8,8,256]{2,1,0:T(8,128)} %get-tuple-element.18.aux_ref, ...), custom_call_target="tpu_custom_call" | custom-call | tf_op jit(solution)/shard_map/inside/pallas_call | solution.py:545
  110.6 0.0 copy-done.1
  110.6 0.0 collective-permute-done.4.came_ref
  110.6 2.8 %finish.1 = bf16[2048,256]{1,0:T(8,128)(2,1)} custom-call(bf16[16,256,128]{2,1,0:T(8,128)(2,1)} %copy-done.1, f32[8,256,256]{2,1,0:T(8,128)S(1)} %get-tuple-element.24.num_ref, f32[8,8,256]{2,1,0:T(8,128)S(1)} %get-tuple-element.25.row_ref, f32[128,256]{1,0:T(8,128)S(1)} %get-tuple-element.27.keep_ref, f32[128,256]{1,0:T(8,128)S(1)} %collective-permute-done.4.came_ref), custom_call_target="tpu_custom_call" | custom-call | tf_op jit(solution)/shard_map/finish/pallas_call | solution.py:562
  (2 shorter events, 0.0 us)
Async XLA Ops:
  37.9 43.9 %copy-start = (bf16[16,520,128]{2,1,0:T(8,128)(2,1)}, bf16[16,520,128]{2,1,0:T(8,128)(2,1)S(1)}, u32[]{:S(2)}) copy-start(bf16[16,520,128]{2,1,0:T(8,128)(2,1)S(1)} %all_to_all.20.r_in.r_ref) | copy-start | bytes 6389764
  38.9 3.3 %collective-permute-start = (f32[136,256]{1,0:T(8,128)S(1)}, f32[136,256]{1,0:T(8,128)S(1)}, u32[]{:S(2)}, u32[]{:S(2)}) collective-permute-start(f32[136,256]{1,0:T(8,128)S(1)} %get-tuple-element.20), channel_id=1, source_target_pairs={{0,16},{16,0},{32,48},{48,32},{64,80},{80,64},{96,112},{112,96},{1... | collective-permute-start | bytes 417800 | tf_op jit(solution)/shard_map/ppermute | solution.py:459
  55.0 19.4 %copy-start.2 = (f32[4,40,256]{2,1,0:T(8,128)}, f32[4,40,256]{2,1,0:T(8,128)S(1)}, u32[]{:S(2)}) copy-start(f32[4,40,256]{2,1,0:T(8,128)S(1)} %all_to_all.21.z_ref.refs_0_) | copy-start | bytes 491524
  55.1 11.5 %collective-permute-start.3 = (f32[40,256]{1,0:T(8,128)S(1)}, f32[40,256]{1,0:T(8,128)S(1)}, u32[]{:S(2)}, u32[]{:S(2)}) collective-permute-start(f32[40,256]{1,0:T(8,128)S(1)} %near.1), channel_id=1, source_target_pairs={{0,384},{16,400},{32,416},{48,432},{64,448},{80,464},{96,480},{112... | collective-permute-start | bytes 122888 | tf_op jit(solution)/shard_map/ppermute | solution.py:517
  55.7 11.4 %collective-permute-start.2 = (f32[40,256]{1,0:T(8,128)S(1)}, f32[40,256]{1,0:T(8,128)S(1)}, u32[]{:S(2)}, u32[]{:S(2)}) collective-permute-start(f32[40,256]{1,0:T(8,128)S(1)} %near.1), channel_id=1, source_target_pairs={{0,256},{16,272},{32,288},{48,304},{64,320},{80,336},{96,352},{112... | collective-permute-start | bytes 122888 | tf_op jit(solution)/shard_map/ppermute | solution.py:517
  64.6 9.8 %collective-permute-start.1 = (f32[40,256]{1,0:T(8,128)S(1)}, f32[40,256]{1,0:T(8,128)S(1)}, u32[]{:S(2)}, u32[]{:S(2)}) collective-permute-start(f32[40,256]{1,0:T(8,128)S(1)} %near.1), channel_id=1, source_target_pairs={{0,128},{16,144},{32,160},{48,176},{64,192},{80,208},{96,224},{112... | collective-permute-start | bytes 122888 | tf_op jit(solution)/shard_map/ppermute | solution.py:517
  76.1 13.2 %copy-start.3 = (f32[8,256]{1,0:T(8,128)S(1)}, f32[8,256]{1,0:T(8,128)}, u32[]{:S(2)}) copy-start(f32[8,256]{1,0:T(8,128)} %get-tuple-element.23.nin_ref) | copy-start | bytes 24580
  76.1 9.5 %all-to-all-start.3 = ((f32[4,32,256]{2,1,0:T(8,128)}), f32[4,32,256]{2,1,0:T(8,128)S(1)}, u32[]{:S(2)}, u32[]{:S(2)}) async-start(f32[4,32,256]{2,1,0:T(8,128)} %get-tuple-element.26), calls=%async_computation.3 | async-start | bytes 262144 | tf_op jit(solution)/shard_map/all_to_all | solution.py:531
  85.6 19.3 %all-to-all-start = ((bf16[16,256,128]{2,1,0:T(8,128)(2,1)}), bf16[16,256,128]{2,1,0:T(8,128)(2,1)S(1)}, u32[]{:S(2)}, u32[]{:S(2)}) async-start(bf16[16,256,128]{2,1,0:T(8,128)(2,1)} %turn.1), calls=%async_computation | async-start | bytes 2097152 | tf_op jit(solution)/shard_map/all_to_all | solution.py:484
  89.4 21.2 %collective-permute-start.4 = (f32[128,256]{1,0:T(8,128)S(1)}, f32[128,256]{1,0:T(8,128)S(1)}, u32[]{:S(2)}, u32[]{:S(2)}) collective-permute-start(f32[128,256]{1,0:T(8,128)S(1)} %get-tuple-element.28), channel_id=1, source_target_pairs={{0,16},{16,0},{32,48},{48,32},{64,80},{80,64},{96,112},{112,96},{1... | collective-permute-start | bytes 393224 | tf_op jit(solution)/shard_map/ppermute | solution.py:543
  104.9 5.7 %copy-start.1 = (bf16[16,256,128]{2,1,0:T(8,128)(2,1)}, bf16[16,256,128]{2,1,0:T(8,128)(2,1)S(1)}, u32[]{:S(2)}) copy-start(bf16[16,256,128]{2,1,0:T(8,128)(2,1)S(1)} %all-to-all-done.asked_ref.asked_in) | copy-start | bytes 3145732
